TPU v7x, 32 devices: a whole 2x2x4 slice. The times are simulated.
32 devices in a mesh: dir: 2 (over y), dp: 16 (over z, x, core).
Axes of the slice: x: 2, y: 2, z: 4, core: 2. Of those that a mesh axis runs over, the one named last changes fastest.
Arguments:
- tokens: bfloat16 [16, 1024, 768], P('dp', 'dir'), may hold values from -6 to 6
- norm_gain: float32 [768], replicated, may hold values from 0.5 to 1.5
- w_zx: bfloat16 [768, 3072], P('dp'), may hold values from -0.21875 to 0.21875
- w_bc: bfloat16 [768, 128], P('dp'), may hold values from -0.21875 to 0.21875
- w_dt: bfloat16 [768, 48], P('dp'), may hold values from -0.21875 to 0.21875
- conv_w: float32 [4, 1664], replicated, may hold values from -3 to 3
- conv_b: float32 [1664], replicated, may hold values from -1.75 to 1.75
- dt_bias: float32 [48], replicated, may hold values from -4.5 to -2
- a_log: float32 [48], replicated, may hold values from -2.5 to 1.5
- d_skip: float32 [24], replicated, may hold values from 0.5 to 1.5
- out_gain: float32 [1536], replicated, may hold values from 0.5 to 1.5
- w_out: bfloat16 [1536, 768], P('dp'), may hold values from -0.15625 to 0.15625
- doc_lengths: int32 [16, 4], P('dp'), may hold values from 1 to 512, 1024 in all within a row
- out_grad: bfloat16 [16, 1024, 768], P('dp', 'dir'), may hold values from -6 to 6
Outputs:
- block_out: bfloat16 [16, 1024, 768], P('dp', 'dir')
- grad_tokens: bfloat16 [16, 1024, 768], P('dp', 'dir')
- grad_norm_gain: float32 [768], replicated
- grad_w_zx: float32 [768, 3072], replicated
- grad_w_bc: float32 [768, 128], replicated
- grad_w_dt: float32 [768, 48], replicated
- grad_conv_w: float32 [4, 1664], replicated
- grad_conv_b: float32 [1664], replicated
- grad_dt_bias: float32 [48], replicated
- grad_a_log: float32 [48], replicated
- grad_d_skip: float32 [24], replicated
- grad_out_gain: float32 [1536], replicated
- grad_w_out: float32 [1536, 768], replicated
Inputs may be any that keep to these rules, and one draw needn't show every extreme that they name: `doc_lengths`: in each row the 4 lengths sum to 1024, and the longest is exactly 512.
All inputs are finite; a program needn't handle non-finite values.
Results may differ from a plain program's by a relative error of at most 0.014.
Values may be sent and summed in bfloat16 or wider, within the bound.
No kernel may reach another device: no remote copies, remote signals or barrier semaphores. Data moves between devices by JAX's collectives and lax.ppermute only.
A program may use at most 192 MiB of HBM per device.

v0:
```python
from functools import partial

import jax
import jax.numpy as jnp
from jax import lax
from jax.sharding import PartitionSpec as P

D = 768
HEADS = 24
HEADDIM = 64
STATE = 64
INNER = 1536
BLOCK = 128
CONV = 4
LEN = 1024


highest = lax.Precision.HIGHEST
epsilon = 1e-05


def shifted_2(block, axis, distance):
    devices = range(lax.axis_size(axis))
    route = [(i - distance, i) for i in devices if i - distance in devices]
    return lax.ppermute(block, axis, route)


def partner(shard, axis, stride):
    return lax.ppermute(shard, axis, [(i, i ^ 1 << stride) for i in range(lax.axis_size(axis))])


def segment_ids(lengths_row, length):
    doc_ends = jnp.cumsum(lengths_row)
    places = jnp.arange(length, dtype=jnp.int32)
    return jnp.sum((places[:, None] >= doc_ends[None, :]).astype(jnp.int32), axis=1)


def conv_silu(pre_conv, seg_row, conv_w, conv_b):
    tap_count = conv_w.shape[0]
    row_len = pre_conv.shape[0]
    padded = jnp.pad(pre_conv, ((tap_count - 1, 0), (0, 0)))
    seg_pad = jnp.concatenate([jnp.full((tap_count - 1,), -1, jnp.int32), seg_row], axis=0)
    summed = conv_b[None, :] + conv_w[tap_count - 1][None, :] * pre_conv
    for offset in range(1, tap_count):
        start = tap_count - 1 - offset
        shifted = padded[start : start + row_len]
        same_doc = (seg_pad[start : start + row_len] == seg_row)[:, None]
        summed = summed + jnp.where(
            same_doc, conv_w[tap_count - 1 - offset][None, :] * shifted, 0.0
        )
    return jax.nn.silu(summed)


def block_step(a_neg, carried, inputs):
    states, prev_seg = carried
    x_block, b_block, c_block, dt_block, seg_block = inputs
    block_len = x_block.shape[0]
    log_rates = dt_block * a_neg[None, :]
    cumul = jnp.cumsum(log_rates, axis=0)
    cum_heads = cumul.T
    places = jnp.arange(block_len, dtype=jnp.int32)
    keep_mask = (places[:, None] > places[None, :]) & (seg_block[:, None] == seg_block[None, :])
    scores = jnp.dot(c_block, b_block.T, precision=highest)
    weighted = jnp.where(
        keep_mask[None],
        jnp.exp(jnp.minimum(cum_heads[:, :, None] - cum_heads[:, None, :], 0.0)) * scores[None],
        0.0,
    )
    inputs_dt = x_block * dt_block[:, :, None]
    y_inner = jnp.einsum("hts,shp->thp", weighted, inputs_dt, precision=highest)
    carried_in = jnp.where((seg_block == prev_seg)[:, None], jnp.exp(cumul), 0.0)
    y_carry = jnp.einsum("tn,hpn->thp", c_block, states, precision=highest) * carried_in[:, :, None]
    last_seg = seg_block[block_len - 1]
    tail_weights = jnp.where(
        (seg_block == last_seg)[:, None], jnp.exp(cumul[block_len - 1][None, :] - cumul), 0.0
    )
    carry_keep = jnp.where(last_seg == prev_seg, jnp.exp(cumul[block_len - 1]), 0.0)
    new_states = states * carry_keep[:, None, None] + jnp.einsum(
        "shp,sn->hpn", inputs_dt * tail_weights[:, :, None], b_block, precision=highest
    )
    return ((new_states, last_seg), y_inner + y_carry)


def scan_dir(x_row, b_row, c_row, dt_row, a_neg, seg_row):
    length = x_row.shape[0]
    block_count = length // BLOCK
    head_count = dt_row.shape[1]
    head_width = x_row.shape[1] // head_count
    state_width = b_row.shape[1]
    sliced = (
        x_row.reshape(block_count, BLOCK, head_count, head_width),
        b_row.reshape(block_count, BLOCK, state_width),
        c_row.reshape(block_count, BLOCK, state_width),
        dt_row.reshape(block_count, BLOCK, head_count),
        seg_row.reshape(block_count, BLOCK),
    )
    initial = (
        jnp.zeros((head_count, head_width, state_width), x_row.dtype),
        jnp.array(-1, jnp.int32),
    )
    advance = jax.checkpoint(partial(block_step, a_neg))
    final_carry, results = lax.scan(advance, initial, sliced)
    return (results.reshape(length, head_count * head_width), final_carry[0])


def rms_scale(values, gain):
    return (
        values
        * lax.rsqrt(jnp.mean(values * values, axis=1, keepdims=True) + epsilon)
        * gain[None, :]
    )


def gate_norm(mixed_vals, gate_vals, gain):
    gated = mixed_vals * jax.nn.silu(gate_vals)
    return (
        gated * lax.rsqrt(jnp.mean(gated * gated, axis=1, keepdims=True) + epsilon) * gain[None, :]
    )


def body(
    tokens,
    norm_gain,
    w_zx,
    w_bc,
    w_dt,
    conv_w,
    conv_b,
    dt_bias,
    a_log,
    d_skip,
    out_gain,
    w_out,
    doc_lengths,
    out_grad,
):
    direction = lax.axis_index("dir")
    forward_side = direction == 0
    full_zx, full_bc, full_dt, full_out = (
        lax.all_gather(w_zx, "dp", axis=0, tiled=True),
        lax.all_gather(w_bc, "dp", axis=0, tiled=True),
        lax.all_gather(w_dt, "dp", axis=0, tiled=True),
        lax.all_gather(w_out, "dp", axis=0, tiled=True),
    )
    row_count = tokens.shape[0]
    half_len = tokens.shape[1]
    token_count = row_count * half_len
    x_flat = tokens.reshape(token_count, D).astype(jnp.float32)
    normed_f, rms_pull = jax.vjp(rms_scale, x_flat, norm_gain)
    normed = normed_f.astype(jnp.bfloat16)
    zx_proj = jnp.dot(normed, full_zx, preferred_element_type=jnp.float32)
    bc_proj = jnp.dot(normed, full_bc, preferred_element_type=jnp.float32)
    dt_proj = jnp.dot(normed, full_dt, preferred_element_type=jnp.float32).astype(jnp.bfloat16)
    gate_z = zx_proj[:, :INNER]
    pre_conv = jnp.concatenate([zx_proj[:, INNER:], bc_proj], axis=1).astype(jnp.bfloat16)
    seg_rows = jax.vmap(partial(segment_ids, length=LEN))(doc_lengths)
    pre_rows = pre_conv.reshape(row_count, half_len, INNER + 2 * STATE)
    dt_rows = dt_proj.reshape(row_count, half_len, 2 * HEADS)
    rim_len = CONV - 1
    rim_in = shifted_2(pre_rows[:, half_len - rim_len :, :], "dir", 1)
    pre_ext = jnp.concatenate([rim_in, pre_rows], axis=1).astype(jnp.float32)
    seg_padded = jnp.concatenate([jnp.full((row_count, rim_len), -1, jnp.int32), seg_rows], axis=1)
    seg_ext = lax.dynamic_slice_in_dim(seg_padded, direction * half_len, half_len + rim_len, 1)
    seam_fwd = seg_rows[:, half_len - 1]
    seam_rev = seg_rows[:, half_len]

    def local_mixer(pre_vals, dt_vals, conv_w_in, conv_b_in, bias_in, alog_in, skip_in):
        a_fwd = -jnp.exp(alog_in[:HEADS])
        a_rev = -jnp.exp(alog_in[HEADS:])
        skip_cols = jnp.repeat(skip_in, HEADDIM)

        def one_half(row_args):
            pre_row, dt_row, seg_row, fwd_seam, rev_seam = row_args
            conv_out = conv_silu(pre_row, seg_row, conv_w_in, conv_b_in)[rim_len:]
            seg_here = seg_row[rim_len:]
            dt_fwd = jax.nn.softplus(dt_row[:, :HEADS] + bias_in[None, :HEADS])
            dt_rev = jax.nn.softplus(dt_row[:, HEADS:] + bias_in[None, HEADS:])
            x_in = conv_out[:, :INNER]
            b_in = conv_out[:, INNER : INNER + STATE]
            c_in = conv_out[:, INNER + STATE :]
            y_fwd, state_fwd = scan_dir(x_in, b_in, c_in, dt_fwd, a_fwd, seg_here)
            y_flip, state_rev = scan_dir(
                jnp.flip(x_in, axis=0),
                jnp.flip(b_in, axis=0),
                jnp.flip(c_in, axis=0),
                jnp.flip(dt_rev, axis=0),
                a_rev,
                jnp.flip(seg_here, axis=0),
            )
            y_local = y_fwd + jnp.flip(y_flip, axis=0) + x_in * skip_cols[None, :]
            sending = jnp.where(forward_side, state_fwd, state_rev)
            cum_fwd = jnp.cumsum(dt_fwd * a_fwd[None, :], axis=0)
            cum_rev = jnp.flip(
                jnp.cumsum(jnp.flip(dt_rev * a_rev[None, :], axis=0), axis=0), axis=0
            )
            carry_rev = jnp.where((seg_here == rev_seam)[:, None], jnp.exp(cum_rev), 0.0)
            carry_fwd = jnp.where((seg_here == fwd_seam)[:, None], jnp.exp(cum_fwd), 0.0)
            carry_weight = jnp.where(forward_side, carry_rev, carry_fwd)
            return (y_local, sending, c_in, carry_weight)

        return lax.map(one_half, (pre_vals, dt_vals, seg_ext, seam_fwd, seam_rev))

    local_parts, local_pull = jax.vjp(
        local_mixer, pre_ext, dt_rows.astype(jnp.float32), conv_w, conv_b, dt_bias, a_log, d_skip
    )
    y_local, sending, c_kept, carry_kept = local_parts
    received = partner(sending.astype(jnp.bfloat16), "dir", 0).astype(sending.dtype)

    def seam_term(state_in, c_vals, weights):
        term = (
            jnp.einsum("rtn,rhpn->rthp", c_vals, state_in, precision=highest)
            * weights[:, :, :, None]
        )
        return term.reshape(row_count, half_len, INNER)

    correction, seam_pull = jax.vjp(seam_term, received, c_kept, carry_kept)
    mixed = y_local + correction
    mixed_flat = mixed.reshape(token_count, INNER)
    normed_out_f, gate_pull = jax.vjp(gate_norm, mixed_flat, gate_z, out_gain)
    normed_out = normed_out_f.astype(jnp.bfloat16)
    summed_out = x_flat + jnp.dot(normed_out, full_out, preferred_element_type=jnp.float32)
    block_out = summed_out.astype(jnp.bfloat16).reshape(row_count, half_len, D)
    grad_flat = out_grad.reshape(token_count, D)
    grad_w_out = jnp.einsum("tk,td->kd", normed_out, grad_flat, preferred_element_type=jnp.float32)
    grad_normed_out = jnp.einsum(
        "td,kd->tk", grad_flat, full_out, preferred_element_type=jnp.float32
    )
    grad_mixed, grad_gate, grad_out_gain = gate_pull(grad_normed_out)
    grad_mixed_low = grad_mixed.astype(jnp.bfloat16).reshape(row_count, half_len, INNER)
    grad_mixed_vals = grad_mixed_low.astype(jnp.float32)
    grad_received, grad_c_seam, grad_carry = seam_pull(grad_mixed_vals)
    grad_sending = partner(grad_received.astype(jnp.bfloat16), "dir", 0).astype(grad_received.dtype)
    grad_ext, grad_dt_half, grad_conv_w, grad_conv_b, grad_dt_bias, grad_a_log, grad_d_skip = (
        local_pull((grad_mixed_vals, grad_sending, grad_c_seam, grad_carry))
    )
    rim_back = shifted_2(grad_ext[:, :rim_len, :], "dir", -1)
    grad_pre_half = grad_ext[:, rim_len:, :] + jnp.pad(
        rim_back, ((0, 0), (half_len - rim_len, 0), (0, 0))
    )
    grad_pre_flat = grad_pre_half.reshape(token_count, INNER + 2 * STATE)
    grad_zx = jnp.concatenate([grad_gate, grad_pre_flat[:, :INNER]], axis=1).astype(jnp.bfloat16)
    grad_bc = grad_pre_flat[:, INNER:].astype(jnp.bfloat16)
    grad_dt_low = grad_dt_half.reshape(token_count, 2 * HEADS).astype(jnp.bfloat16)
    grad_w_zx = jnp.einsum("tk,tj->kj", normed, grad_zx, preferred_element_type=jnp.float32)
    grad_w_bc = jnp.einsum("tk,tj->kj", normed, grad_bc, preferred_element_type=jnp.float32)
    grad_w_dt = jnp.einsum("tk,tj->kj", normed, grad_dt_low, preferred_element_type=jnp.float32)
    grad_normed = (
        jnp.einsum("tj,kj->tk", grad_zx, full_zx, preferred_element_type=jnp.float32)
        + jnp.einsum("tj,kj->tk", grad_bc, full_bc, preferred_element_type=jnp.float32)
        + jnp.einsum("tj,kj->tk", grad_dt_low, full_dt, preferred_element_type=jnp.float32)
    )
    grad_x_norm, grad_norm_gain = rms_pull(grad_normed)
    grad_tokens = (
        (grad_flat.astype(jnp.float32) + grad_x_norm)
        .astype(jnp.bfloat16)
        .reshape(row_count, half_len, D)
    )
    (
        sum_norm_gain,
        sum_w_zx,
        sum_w_bc,
        sum_w_dt,
        sum_conv_w,
        sum_conv_b,
        sum_dt_bias,
        sum_a_log,
        sum_d_skip,
        sum_out_gain,
        sum_w_out,
    ) = lax.psum(
        (
            grad_norm_gain,
            grad_w_zx,
            grad_w_bc,
            grad_w_dt,
            grad_conv_w,
            grad_conv_b,
            grad_dt_bias,
            grad_a_log,
            grad_d_skip,
            grad_out_gain,
            grad_w_out,
        ),
        ("dir", "dp"),
    )
    return (
        block_out,
        grad_tokens,
        sum_norm_gain,
        sum_w_zx,
        sum_w_bc,
        sum_w_dt,
        sum_conv_w,
        sum_conv_b,
        sum_dt_bias,
        sum_a_log,
        sum_d_skip,
        sum_out_gain,
        sum_w_out,
    )


def solution(mesh):
    placed = (
        P("dp", "dir", None),
        P(),
        P("dp", None),
        P("dp", None),
        P("dp", None),
        P(),
        P(),
        P(),
        P(),
        P(),
        P(),
        P("dp", None),
        P("dp", None),
        P("dp", "dir", None),
    )
    return jax.shard_map(
        body,
        mesh=mesh,
        in_specs=placed,
        out_specs=(
            P("dp", "dir", None),
            P("dp", "dir", None),
            P(),
            P(),
            P(),
            P(),
            P(),
            P(),
            P(),
            P(),
            P(),
            P(),
            P(),
        ),
        check_vma=False,
    )
```

profile of v0, /device:TPU:0, one launch (start us, length us, event | category | flops | bytes accessed | tf_op | source)
XLA Modules:
  0.0 1082.4 jit_solution(1993637158967317221)
XLA Ops:
  10.2 24.4 %all_gather.14 = bf16[768,128]{1,0:T(8,128)(2,1)S(1)} all-gather(bf16[48,128]{1,0:T(8,128)(2,1)} %param.28), channel_id=1, replica_groups=mesh['dir'=2,'dp'=16] {'dp'}, dimensions={0}, use_global_device_ids=true | all-gather | bytes 208896 | tf_op jit(solution)/shard_map/all_gather | solution.py:141
  37.3 18.9 %all_gather.12 = bf16[768,48]{1,0:T(8,128)(2,1)S(1)} all-gather(bf16[48,48]{1,0:T(8,128)(2,1)} %param.29), channel_id=1, replica_groups=mesh['dir'=2,'dp'=16] {'dp'}, dimensions={0}, use_global_device_ids=true | all-gather | bytes 78336 | tf_op jit(solution)/shard_map/all_gather | solution.py:142
  67.4 4.6 fusion.288
  84.9 4.9 fusion.204
  93.8 24.7 %rev.107 = f32[512,1536]{1,0:T(8,128)} reverse(f32[512,1536]{1,0:T(8,128)} %slice.328), dimensions={0} | reverse | bytes 6291456 | tf_op jit(solution)/shard_map/jvp()/while/body/eval_jaxpr/jit(_flip)/rev | solution.py:183
  118.5 5.5 reshape.1386
  124.5 5.5 reshape.1387
  129.9 6.1 copy.490
  140.6 59.0 %while.230 = (s32[]{:T(128)}, f32[24,64,64]{2,1,0:T(8,128)S(1)}, s32[]{:T(128)}, f32[4,128,24,64]{1,3,2,0:T(8,128)}, f32[4,24,64,64]{3,2,1,0:T(8,128)}, /*index=...) while((s32[]{:T(128)}, f32[24,64,64]{2,1,0:T(8,128)S(1)}, ...), condition=%wide.region_8.10_spmd.clone, body=%wide.region_6.9_spmd.clone.sunk | while | flops 620061952 | bytes 7651091 | solution.py:102
  202.6 6.2 copy.484
  213.5 63.2 %while.229 = (s32[]{:T(128)}, f32[24,64,64]{2,1,0:T(8,128)S(1)}, s32[]{:T(128)}, f32[4,128,24,64]{1,3,2,0:T(8,128)}, f32[4,24,64,64]{3,2,1,0:T(8,128)}, /*index=...) while((s32[]{:T(128)}, f32[24,64,64]{2,1,0:T(8,128)S(1)}, ...), condition=%wide.region_5.7_spmd.clone, body=%wide.region_3.6_spmd.clone.sunk | while | flops 620061952 | bytes 7257875 | solution.py:102
  280.4 5.9 copy.544
  286.3 4.7 reshape.1381
  291.0 15.7 %rev.110 = f32[512,1536]{1,0:T(8,128)} reverse(f32[512,1536]{1,0:T(8,128)S(1)} %reshape.1381), dimensions={0} | reverse | bytes 6291456 | tf_op jit(solution)/shard_map/jvp()/while/body/eval_jaxpr/jit(_flip)/rev | solution.py:190
  306.7 5.9 copy.543
  312.6 6.3 reshape.1380
  318.9 5.2 broadcast_multiply_fusion.4
  327.7 7.1 multiply_reduce_fusion.16
  340.2 5.0 multiply_reduce_fusion.12
  345.7 5.7 multiply_reduce_fusion.13
  361.0 5.5 fusion.230
  371.7 5.0 reduce-window.64
  380.5 15.9 %reverse.3 = f32[512,1536]{1,0:T(8,128)} reverse(bf16[512,1536]{1,0:T(8,128)(2,1)S(1)} %get-tuple-element.2333), dimensions={0} | reverse | bytes 4718592 | tf_op jit(solution)/shard_map/reverse
  396.4 6.2 copy.519
  404.1 5.0 reduce-window.66
  413.3 6.1 copy.511
  424.7 144.4 %while.232 = (s32[]{:T(128)}, f32[24]{0:T(128)}, f32[24,64,64]{2,1,0:T(8,128)S(1)}, f32[4,128,24,64]{1,3,2,0:T(8,128)}, f32[4,128,64]{1,2,0:T(8,128)}, /*index=5...) while((s32[]{:T(128)}, f32[24]{0:T(128)}, ...), condition=%wide.region_40.42_spmd.clone, body=%wide.region_28.41_spmd.clone.sunk | while | flops 1408011520 | bytes 22274224 | solution.py:102
  438.4 4.8 multiply_reduce_fusion.28
  444.2 4.7 fusion.494
  474.4 4.8 multiply_reduce_fusion.28
  480.2 4.7 fusion.494
  510.3 4.8 multiply_reduce_fusion.28
  516.2 4.7 fusion.494
  546.3 4.8 multiply_reduce_fusion.28
  552.1 4.7 fusion.494
  574.8 142.2 %while.231 = (s32[]{:T(128)}, f32[24]{0:T(128)}, f32[24,64,64]{2,1,0:T(8,128)S(1)}, f32[4,128,24,64]{1,3,2,0:T(8,128)}, f32[4,128,64]{1,2,0:T(8,128)}, /*index=5...) while((s32[]{:T(128)}, f32[24]{0:T(128)}, ...), condition=%wide.region_27.29_spmd.clone, body=%wide.region_15.28_spmd.clone.sunk | while | flops 1408011520 | bytes 19111204 | solution.py:102
  588.5 4.5 multiply_reduce_fusion.25
  624.0 4.5 multiply_reduce_fusion.25
  725.9 5.8 copy.553
  731.7 6.3 reshape.1385
  742.0 6.2 reshape.1384
  748.2 24.7 %rev.115 = f32[512,1536]{1,0:T(8,128)} reverse(f32[512,1536]{1,0:T(8,128)} %reshape.1384), dimensions={0} | reverse | bytes 6291456 | tf_op jit(solution)/shard_map/transpose(jvp())/while/body/eval_jaxpr/jit(_flip)/rev | solution.py:183
  783.2 5.5 multiply_reduce_fusion.11
  800.1 5.6 fusion.210
  814.2 5.6 fusion.221
  819.8 42.1 %all-reduce.25 = (f32[768]{0:T(1024)}, f32[4,1664]{1,0:T(4,128)}, f32[1664]{0:T(1024)}, f32[48]{0:T(128)}, f32[48]{0:T(128)}, /*index=5*/f32[24]{0:T(128)}, f32[1536]{0:T(1024)}) all-reduce(f32[768]{0:T(1024)S(1)} %get-tuple-element.2195, f32[4,1664]{1,0:T(4,128)S(1)} %pad_add_fusion.3, ...), channel_id=1, replica_groups=mesh['dir'=2,'dp'=16] {'dir','dp'}, use_global_device_ids=true, to_apply=%region_48.50 | all-reduce | flops 10744 | bytes 85952 | tf_op jit(solution)/shard_map/psum | solution.py:270
  863.3 199.8 %all-reduce.29.cloned.1.call-done = (f32[768,3072]{1,0:T(8,128)}, f32[768,128]{1,0:T(8,128)}, f32[768,48]{0,1:T(8,128)}, f32[1536,768]{1,0:T(8,128)}) async-done(((f32[768,3072]{1,0:T(8,128)}, f32[768,128]{1,0:T(8,128)}, f32[768,48]{0,1:T(8,128)}, f32[1536,768]{1,0:T(8,128)}), (f32[768,3072]{1,0:T(8,128)}, f32[768,128]{1,0:T(8,128)}, f32[768,48]{0,1:T(8,128)}, ...) | async-done | bytes 14696464 | tf_op jit(solution)/shard_map/psum | solution.py:270
  1063.1 8.8 copy.749
  (959 shorter events, 479.6 us)
Async XLA Ops:
  7.2 50.6 %copy-start.20 = (bf16[1,512,768]{2,1,0:T(8,128)(2,1)S(1)}, bf16[1,512,768]{2,1,0:T(8,128)(2,1)}, u32[]{:S(2)}) copy-start(bf16[1,512,768]{2,1,0:T(8,128)(2,1)} %param.25) | copy-start | bytes 2359300
  7.2 50.6 %copy-start.65 = (f32[768]{0:T(1024)S(1)}, f32[768]{0:T(1024)}, u32[]{:S(2)}) copy-start(f32[768]{0:T(1024)} %param.26) | copy-start | bytes 9220
  7.2 51.2 %copy-start.120 = (f32[48]{0:T(128)S(1)}, f32[48]{0:T(128)}, u32[]{:S(2)}) copy-start(f32[48]{0:T(128)} %param.32) | copy-start | bytes 580
  7.2 51.2 %copy-start.112 = (f32[48]{0:T(128)S(1)}, f32[48]{0:T(128)}, u32[]{:S(2)}) copy-start(f32[48]{0:T(128)} %param.33) | copy-start | bytes 580
  7.2 60.2 %all-gather.3.cloned.1.call-start = ((), (), s32[]{:S(2)}) async-start(), calls=%async_computation | async-start | bytes 5013504 | tf_op jit(solution)/shard_map/all_gather | solution.py:140
  8.0 332.2 %all-gather.5.cloned.1.call-start = ((), (), s32[]{:S(2)}) async-start(), calls=%async_computation.1 | async-start | bytes 2506752 | tf_op jit(solution)/shard_map/all_gather | solution.py:143
  8.7 1054.4 %all-reduce.29.cloned.1.call-start = ((), (), s32[]{:S(2)}) async-start(), calls=%async_computation.2 | async-start | bytes 29392896 | tf_op jit(solution)/shard_map/psum | solution.py:270
  10.1 48.9 %copy-start.97 = (f32[512]{0:T(512)}, f32[512]{0:T(512)S(1)}, u32[]{:S(2)}) copy-start(f32[512]{0:T(512)S(1)} %fusion.222) | copy-start | bytes 6148
  10.1 61.9 %copy-start.70 = (f32[512]{0:T(512)}, f32[512]{0:T(512)S(1)}, u32[]{:S(2)}) copy-start(f32[512]{0:T(512)S(1)} %fusion.273) | copy-start | bytes 6148
  34.6 37.5 %copy-start.47 = (bf16[768,128]{1,0:T(8,128)(2,1)}, bf16[768,128]{1,0:T(8,128)(2,1)S(1)}, u32[]{:S(2)}) copy-start(bf16[768,128]{1,0:T(8,128)(2,1)S(1)} %all_gather.14) | copy-start | bytes 589828
  36.2 48.7 %copy-start.105 = (pred[515]{0:T(1024)(128)(4,1)}, pred[515]{0:T(1024)(128)(4,1)S(1)}, u32[]{:S(2)}) copy-start(pred[515]{0:T(1024)(128)(4,1)S(1)} %get-tuple-element.2392) | copy-start | bytes 1549
  36.2 48.7 %copy-start.107 = (pred[515]{0:T(1024)(128)(4,1)}, pred[515]{0:T(1024)(128)(4,1)S(1)}, u32[]{:S(2)}) copy-start(pred[515]{0:T(1024)(128)(4,1)S(1)} %get-tuple-element.2393) | copy-start | bytes 1549
  36.2 48.7 %copy-start.109 = (pred[515]{0:T(1024)(128)(4,1)}, pred[515]{0:T(1024)(128)(4,1)S(1)}, u32[]{:S(2)}) copy-start(pred[515]{0:T(1024)(128)(4,1)S(1)} %get-tuple-element.2394) | copy-start | bytes 1549
  37.2 47.7 %copy-start.80 = (f32[1664]{0:T(1024)}, f32[1664]{0:T(1024)S(1)}, u32[]{:S(2)}) copy-start(f32[1664]{0:T(1024)S(1)} %get-tuple-element.2197) | copy-start | bytes 19972
  37.2 47.7 %copy-start.82 = (f32[1664]{0:T(1024)}, f32[1664]{0:T(1024)S(1)}, u32[]{:S(2)}) copy-start(f32[1664]{0:T(1024)S(1)} %get-tuple-element.2198) | copy-start | bytes 19972
  37.2 47.7 %copy-start.84 = (f32[1664]{0:T(1024)}, f32[1664]{0:T(1024)S(1)}, u32[]{:S(2)}) copy-start(f32[1664]{0:T(1024)S(1)} %get-tuple-element.2199) | copy-start | bytes 19972
  37.2 47.7 %copy-start.86 = (f32[1664]{0:T(1024)}, f32[1664]{0:T(1024)S(1)}, u32[]{:S(2)}) copy-start(f32[1664]{0:T(1024)S(1)} %get-tuple-element.2200) | copy-start | bytes 19972
  56.2 15.8 %copy-start.49 = (bf16[768,48]{1,0:T(8,128)(2,1)}, bf16[768,48]{1,0:T(8,128)(2,1)S(1)}, u32[]{:S(2)}) copy-start(bf16[768,48]{1,0:T(8,128)(2,1)S(1)} %all_gather.12) | copy-start | bytes 221188
  57.8 25.9 %copy-start.42 = (bf16[512,128]{1,0:T(8,128)(2,1)}, bf16[512,128]{1,0:T(8,128)(2,1)S(1)}, u32[]{:S(2)}) copy-start(bf16[512,128]{1,0:T(8,128)(2,1)S(1)} %convolution_convert_fusion.1) | copy-start | bytes 393220
  59.0 13.1 %copy-start.118 = (f32[24]{0:T(128)}, f32[24]{0:T(128)S(1)}, u32[]{:S(2)}) copy-start(f32[24]{0:T(128)S(1)} %get-tuple-element.2410) | copy-start | bytes 292
  59.8 19.6 %copy-start.56 = (f32[512,24]{0,1:T(8,128)}, f32[512,24]{0,1:T(8,128)S(1)}, u32[]{:S(2)}) copy-start(f32[512,24]{0,1:T(8,128)S(1)} %get-tuple-element.2343) | copy-start | bytes 147460
  59.8 20.1 %copy-start.52 = (f32[512,24]{0,1:T(8,128)}, f32[512,24]{0,1:T(8,128)S(1)}, u32[]{:S(2)}) copy-start(f32[512,24]{0,1:T(8,128)S(1)} %get-tuple-element.2387) | copy-start | bytes 147460
  75.0 8.7 collective-permute-start
  81.6 246.0 %copy-start.78 = (f32[1536]{0:T(1024)}, f32[1536]{0:T(1024)S(1)}, u32[]{:S(2)}) copy-start(f32[1536]{0:T(1024)S(1)} %mul.1288) | copy-start | bytes 18436
  91.7 32.3 %copy-start.37 = (f32[512,64]{1,0:T(8,128)}, f32[512,64]{1,0:T(8,128)S(1)}, u32[]{:S(2)}) copy-start(f32[512,64]{1,0:T(8,128)S(1)} %get-tuple-element.2379) | copy-start | bytes 393220
  91.7 32.5 %copy-start.36 = (f32[512,64]{1,0:T(8,128)}, f32[512,64]{1,0:T(8,128)S(1)}, u32[]{:S(2)}) copy-start(f32[512,64]{1,0:T(8,128)S(1)} %get-tuple-element.2378) | copy-start | bytes 393220
  199.6 9.2 copy-start.28
  199.6 9.1 copy-start.33
  199.6 9.1 copy-start.34
  213.5 64.1 %copy-start.54 = (f32[512,24]{0,1:T(8,128)S(1)}, f32[512,24]{0,1:T(8,128)}, u32[]{:S(2)}) copy-start(f32[512,24]{0,1:T(8,128)} %rev.112) | copy-start | bytes 147460
  277.6 41.4 %collective-permute-start.1 = (bf16[1,24,64,64]{3,2,1,0:T(8,128)(2,1)}, bf16[1,24,64,64]{3,2,1,0:T(8,128)(2,1)}, u32[]{:S(2)}, u32[]{:S(2)}) collective-permute-start(bf16[1,24,64,64]{3,2,1,0:T(8,128)(2,1)} %fusion.246), channel_id=1, source_target_pairs={{0,16},{16,0},{1,17},{17,1},{2,18},{18,2},{3,19},{19,3},{4,20},{20... | collective-permute-start | bytes 589832 | tf_op jit(solution)/shard_map/ppermute | solution.py:29
  327.7 8.8 copy-start.30
  327.7 8.8 copy-start.76
  334.8 10.4 copy-start.94
  351.4 29.1 %copy-start.1 = (bf16[512,1536]{1,0:T(8,128)(2,1)}, bf16[512,1536]{1,0:T(8,128)(2,1)S(1)}, u32[]{:S(2)}) copy-start(bf16[512,1536]{1,0:T(8,128)(2,1)S(1)} %get-tuple-element.2333) | copy-start | bytes 4718596
  366.5 52.9 %collective-permute-start.2 = (bf16[1,24,64,64]{3,2,1,0:T(8,128)(2,1)}, bf16[1,24,64,64]{3,2,1,0:T(8,128)(2,1)}, u32[]{:S(2)}, u32[]{:S(2)}) collective-permute-start(bf16[1,24,64,64]{3,2,1,0:T(8,128)(2,1)} %fusion.230), channel_id=1, source_target_pairs={{0,16},{16,0},{1,17},{17,1},{2,18},{18,2},{3,19},{19,3},{4,20},{20... | collective-permute-start | bytes 589832 | tf_op jit(solution)/shard_map/ppermute | solution.py:29
  396.4 13.4 %copy-start.17 = (f32[512,1536]{1,0:T(8,128)S(1)}, f32[512,1536]{1,0:T(8,128)}, u32[]{:S(2)}) copy-start(f32[512,1536]{1,0:T(8,128)} %reverse.3) | copy-start | bytes 9437188
  748.2 24.7 %copy-start.45 = (f32[4,128,64]{2,1,0:T(8,128)S(1)}, f32[4,128,64]{2,1,0:T(8,128)}, u32[]{:S(2)}) copy-start(f32[4,128,64]{2,1,0:T(8,128)} %copy.522) | copy-start | bytes 393220
  748.2 24.7 %copy-start.46 = (f32[512,64]{1,0:T(8,128)S(1)}, f32[512,64]{1,0:T(8,128)}, u32[]{:S(2)}) copy-start(f32[512,64]{1,0:T(8,128)} %rev.114) | copy-start | bytes 393220
  748.2 24.7 %copy-start.2 = (bf16[512,1536]{1,0:T(8,128)(2,1)S(1)}, bf16[512,1536]{1,0:T(8,128)(2,1)}, u32[]{:S(2)}) copy-start(bf16[512,1536]{1,0:T(8,128)(2,1)} %copy-done.1) | copy-start | bytes 4718596
  748.2 24.7 %copy-start.79 = (f32[1536]{0:T(1024)S(1)}, f32[1536]{0:T(1024)}, u32[]{:S(2)}) copy-start(f32[1536]{0:T(1024)} %copy-done.78) | copy-start | bytes 18436
  791.5 5.7 collective-permute-start.3
  814.2 47.7 %copy-start.98 = (f32[512]{0:T(512)S(1)}, f32[512]{0:T(512)}, u32[]{:S(2)}) copy-start(f32[512]{0:T(512)} %copy-done.97) | copy-start | bytes 6148
  814.2 47.7 %copy-start.32 = (bf16[1,512,768]{2,1,0:T(8,128)(2,1)S(1)}, bf16[1,512,768]{2,1,0:T(8,128)(2,1)}, u32[]{:S(2)}) copy-start(bf16[1,512,768]{2,1,0:T(8,128)(2,1)} %param.38) | copy-start | bytes 2359300
  1063.1 10.2 slice-start
  1063.1 8.8 copy-start.60
  1063.1 9.5 copy-start.69
  1063.1 10.2 slice-start.1
  (134 other events, 619.7 us)
Sparse Core Ops, SparseCore 0:
  10.3 57.0 all-gather.2
  69.7 41.3 all-gather.4
  805.8 257.2 all-reduce.28
where the time goes:
time: 1100 us; the launch traced here: 1080 us
  local copies, waits for them, and re-layouts  336 us (31%)
  matrix products  265 us (24%)
  waiting for transfers between devices  207 us (19%)
  other arithmetic  142 us (13%)
  blocking collectives  85.5 us (8%)
  loops' own time  24 us (2%)
  between operations  15.6 us (1%)
    psum x1, waiting for transfers between devices, body(): lax.psum((grad_norm_gain, grad_w_zx, grad_w_bc, grad_w_dt, grad_conv_w, g...  200 us
    dot_general x24, matrix products, block_step(): y_inner = jnp.einsum('hts,shp->thp', weighted, inputs_dt, precision=highest)  108 us
    unnamed x228, local copies, waits for them, and re-layouts  52.9 us
    rev x2, local copies, waits for them, and re-layouts, one_half(): jnp.flip(x_in, axis=0)  49.4 us
    dot_general x32, matrix products, block_step(): jnp.einsum('tn,hpn->thp', c_block, states, precision=highest)  48.6 us
    dot_general x24, matrix products, block_step(): jnp.einsum('shp,sn->hpn', inputs_dt * tail_weights[:, :, None], b_block,...  48.2 us
    psum x1, blocking collectives, body(): lax.psum((grad_norm_gain, grad_w_zx, grad_w_bc, grad_w_dt, grad_conv_w, g...  42.1 us
    squeeze x48, local copies, waits for them, and re-layouts, scan_dir(): final_carry, results = lax.scan(advance, initial, sliced)  41.2 us
  transfers between devices with their start and end apart: 7, of which 3 were waited for; matrix products, arithmetic and copies ran while one was open for 30% of the time, Pallas kernels for 0%

commit v1 on v0

v1 whole, which is shorter than its diff:
```python
import functools

import jax
import jax.numpy as jnp
from jax import lax
from jax.experimental import pallas as pl
from jax.experimental.pallas import tpu as pltpu
from jax.sharding import PartitionSpec as P

D = 768
HEADS = 24
HEADDIM = 64
STATE = 64
INNER = 1536
CONV = 4
NDOC = 4
PAIRS = HEADS // 2
HALO = 16
CH = 256
NCH = 7
SMALL_AT = (CONV + 2) * NCH - 1
SMALL = 64
EPS = 1e-05
LOG2E = 1.4426950408889634
BF = jnp.bfloat16
F32 = jnp.float32
HI = lax.Precision.HIGHEST


def nn(a, b):
    return lax.dot_general(a, b, (((1,), (0,)), ((), ())), preferred_element_type=F32)


def nt(a, b):
    return lax.dot_general(a, b, (((1,), (1,)), ((), ())), preferred_element_type=F32)


def iota(shape, axis):
    return lax.broadcasted_iota(jnp.int32, shape, axis)


def sigm(v):
    return 1.0 / (1.0 + jnp.exp(-v))


def lane_pair(col_a, col_b, rows):
    return jnp.where(iota((rows, 128), 1) < 64, col_a, col_b)


def params(mib=60):
    return pltpu.CompilerParams(
        dimension_semantics=("arbitrary",), vmem_limit_bytes=mib * 1024 * 1024
    )


def full(shape):
    return pl.BlockSpec(shape, lambda i: tuple(0 for _ in shape))


SMEM_SPEC = pl.BlockSpec(memory_space=pltpu.SMEM)


def doc_ids(flag, places):
    total = jnp.zeros(places.shape, jnp.int32)
    end = 0
    for k in range(NDOC):
        end = end + flag[1 + k]
        total = total + jnp.where(places >= end, 1, 0)
    return jnp.where(places < 0, -1, total)


def doc_at(flag, place):
    total = 0
    end = 0
    for k in range(NDOC):
        end = end + flag[1 + k]
        total = total + jnp.where(place >= end, 1, 0)
    return total


def doc_col(flag, T, lead=0):
    return doc_ids(flag, iota((T + lead, 1), 0) + (flag[0] * T - lead))


def doc_row(flag, T):
    return doc_ids(flag, iota((1, T), 1) + flag[0] * T)


def project_kernel(T, flag, tok, halo, gain, w, cw, cb, bias, alog,
                   norm_o, nh_o, pre_o, z_o, act_o, rows_o, wrc_o, b_o, bt_o, c_o, ct_o, st_o, ncat, pf, segc):
    step = pl.program_id(0)

    @pl.when(step == 0)
    def _():
        def norm(v):
            v = v.astype(F32)
            ms = jnp.mean(v * v, axis=1, keepdims=True)
            return (v * lax.rsqrt(ms + EPS) * gain[...]).astype(BF)

        nh = norm(halo[...])
        own = norm(tok[...])
        nh_o[...] = nh
        norm_o[...] = own
        ncat[0:HALO, :] = nh
        ncat[HALO:, :] = own
        segc[...] = doc_col(flag, T, HALO)

    proj = nn(ncat[...], w[...]).astype(BF)
    pre_o[...] = proj
    pf[...] = proj.astype(F32)
    segs = segc[...]
    here = segs[HALO:, :]
    z = cb[...] + cw[CONV - 1 : CONV, :] * pf[HALO:, :]
    for k in range(1, CONV):
        same = segs[HALO - k : HALO + T - k, :] == here
        z = z + jnp.where(same, cw[CONV - 1 - k : CONV - k, :] * pf[HALO - k : HALO + T - k, :], 0.0)
    z_o[...] = z.astype(BF)
    act = z * sigm(z)
    act_o[...] = act.astype(BF)

    @pl.when(step == 0)
    def _():
        bc = act[:, :128]
        b_o[...] = bc[:, :64].astype(BF)
        c_o[...] = bc[:, 64:].astype(BF)
        bct = bc.T
        bt_o[...] = bct[:64, :].astype(BF)
        ct_o[...] = bct[64:, :].astype(BF)
        v = pf[HALO:, 128:] + bias[...]
        dt = jnp.maximum(v, 0.0) + jnp.log1p(jnp.exp(-jnp.abs(v)))
        rate = dt * (-LOG2E * jnp.exp(alog[...]))
        rate_t = rate.T
        dt_t = dt.T
        upto = (iota((T, T), 0) <= iota((T, T), 1)).astype(F32)
        inc = lax.dot_general(rate_t, upto, (((1,), (0,)), ((), ())), precision=HI, preferred_element_type=F32)
        isf = iota((128, T), 0) < HEADS
        cum = jnp.where(isf, inc, inc - rate_t)
        ldt = jnp.log2(jnp.maximum(dt_t, 1e-37))
        key = jnp.where(isf, cum - ldt, cum + ldt)
        segv = doc_row(flag, T)
        left, right = doc_at(flag, T - 1), doc_at(flag, T)
        send_f = jnp.where(segv == left, jnp.exp2(cum[:, T - 1 :] - key), 0.0)
        send_b = jnp.where(segv == right, jnp.exp2(key), 0.0)
        recv_f = jnp.where(segv == left, jnp.exp2(cum), 0.0)
        recv_b = jnp.where(segv == right, jnp.exp2(inc[:, T - 1 :] - cum), 0.0)
        first = flag[0] == 0
        send = jnp.where(first, send_f[0:HEADS], send_b[HEADS : 2 * HEADS])
        recv = jnp.where(first, recv_b[HEADS : 2 * HEADS], recv_f[0:HEADS])
        for p in range(PAIRS):
            f, r = 2 * p, HEADS + 2 * p
            rows_o[p, 0:2, :] = cum[f : f + 2]
            rows_o[p, 2:4, :] = cum[r : r + 2]
            rows_o[p, 4:6, :] = key[f : f + 2]
            rows_o[p, 6:8, :] = key[r : r + 2]
            rows_o[p, 8:10, :] = send[f : f + 2]
            rows_o[p, 10:12, :] = recv[f : f + 2]
            rows_o[p, 12:16, :] = jnp.zeros((4, T), F32)
        recv_pad = jnp.concatenate([recv, jnp.zeros((128 - HEADS, T), F32)], axis=0)
        wrc_o[...] = recv_pad.T.astype(BF)

    @pl.when(step > 0)
    def _():
        for j in range(CH // 128):
            cols = rows_o[2 * (step - 1) + j, 8:16, :].T
            wide = lane_pair(cols[:, 0:1], cols[:, 1:2], T)
            xw = (act[:, 128 * j : 128 * (j + 1)] * wide).astype(BF)
            st_o[:, 128 * j : 128 * (j + 1)] = nn(bt_o[...], xw).astype(BF)


def project(flag, tok, halo, gain, w1, conv_w, conv_b, bias, alog):
    T = tok.shape[0]
    E = T + HALO
    chunk = lambda i: lax.rem(i + NCH - 1, NCH)
    xchunk = lambda i: jnp.maximum(i - 1, 0)
    col = lambda rows: pl.BlockSpec((rows, CH), lambda i: (0, chunk(i)))
    shapes = [
        ((T, D), BF), ((HALO, D), BF), ((E, NCH * CH), BF), ((T, NCH * CH), BF), ((T, NCH * CH), BF),
        ((PAIRS, 16, T), F32), ((T, 128), BF), ((T, 64), BF), ((64, T), BF), ((T, 64), BF), ((64, T), BF),
        ((64, INNER), BF),
    ]
    out_specs = [
        full((T, D)), full((HALO, D)), col(E), col(T), col(T), full((PAIRS, 16, T)), full((T, 128)), full((T, 64)),
        full((64, T)), full((T, 64)), full((64, T)), pl.BlockSpec((64, CH), lambda i: (0, xchunk(i))),
    ]
    return pl.pallas_call(
        functools.partial(project_kernel, T),
        grid=(NCH,),
        in_specs=[SMEM_SPEC, full((T, D)), full((HALO, D)), full((1, D)), col(D), col(CONV), col(1),
                  full((1, 128)), full((1, 128))],
        out_specs=out_specs,
        out_shape=[jax.ShapeDtypeStruct(s, d) for s, d in shapes],
        scratch_shapes=[pltpu.VMEM((E, D), BF), pltpu.VMEM((E, CH), F32), pltpu.VMEM((E, 1), jnp.int32)],
        compiler_params=params(),
        name="project",
    )(flag, tok, halo, gain, w1, conv_w, conv_b, bias, alog)


def same_doc(flag, T):
    return (doc_col(flag, T) == doc_row(flag, T)) & (iota((T, T), 0) != iota((T, T), 1))


def mix_kernel(T, flag, b, c, rows, x, skip, y_o, sc):
    Q = 128

    @pl.when(pl.program_id(0) == 0)
    def _():
        s = nt(c[...], b[...])
        sc[...] = jnp.where(same_doc(flag, T), s, 0.0)

    r = rows[0]
    cols = r[0:8].T
    x2 = x[...]
    later = iota((Q, Q), 0) > iota((Q, Q), 1)
    lane = iota((Q, 128), 1) < 64
    for i in range(T // Q):
        lo, hi = i * Q, (i + 1) * Q
        outs = []
        for h in range(2):
            cf = cols[lo:hi, h : h + 1]
            cr = cols[lo:hi, 2 + h : 3 + h]
            kf = r[4 + h : 5 + h]
            kr = r[6 + h : 7 + h]
            parts = []
            if i > 0:
                parts.append(cf - kf[:, :lo])
            parts.append(jnp.where(later, cf - kf[:, lo:hi], kr[:, lo:hi] - cr))
            if hi < T:
                parts.append(kr[:, hi:] - cr)
            e = jnp.concatenate(parts, axis=1)
            m = (sc[lo:hi, :] * jnp.exp2(e)).astype(BF)
            outs.append(nn(m, x2))
        y_o[lo:hi, :] = jnp.where(lane, outs[0], outs[1]) + skip[...] * x2[lo:hi, :].astype(F32)


def mix(flag, b, c, rows, act, skip):
    T = b.shape[0]
    blk = pl.BlockSpec((T, 128), lambda i: (0, i))
    return pl.pallas_call(
        functools.partial(mix_kernel, T),
        grid=(PAIRS,),
        in_specs=[SMEM_SPEC, full((T, 64)), full((T, 64)),
                  pl.BlockSpec((1, 16, T), lambda i: (i, 0, 0)), blk, pl.BlockSpec((1, 128), lambda i: (0, i))],
        out_specs=blk,
        out_shape=jax.ShapeDtypeStruct((T, INNER), F32),
        scratch_shapes=[pltpu.VMEM((T, T), F32)],
        compiler_params=params(),
        name="mix",
    )(flag, b, c, rows, act, skip)


def gate_kernel(shard, flag, y, wrc, c, ct, st, normed, rest, tok, og, gain,
                no_o, bo_o, gg_o, gm_o, gn_o, dcs_o, dlr_o, dst_o, ggain_o, acc):
    step = pl.program_id(0)
    rb = y.shape[0]
    spread = (lax.div(iota((128, INNER), 1), 64) == iota((128, INNER), 0)).astype(BF)
    wide = nn(wrc[...], spread)
    seam = nn(c[...], st[...]) * wide
    mixed = y[...] + seam
    half = INNER // 2
    wl = rest[:, :shard, :].reshape(D, half)
    wr = rest[:, shard : 2 * shard, :].reshape(D, half)
    wo = rest[:, 2 * shard :, :].reshape(INNER, D)
    own = normed[...]
    gz = jnp.concatenate([nn(own, wl), nn(own, wr)], axis=1)
    sig = sigm(gz)
    sil = gz * sig
    gated = mixed * sil
    rho = lax.rsqrt(jnp.mean(gated * gated, axis=1, keepdims=True) + EPS)
    no = (gated * rho * gain[...]).astype(BF)
    no_o[...] = no
    bo_o[...] = (tok[...].astype(F32) + nn(no, wo)).astype(BF)
    gno = nt(og[...], wo)
    e = gno * gain[...]
    part = jnp.sum(gno * gated * rho, axis=0, keepdims=True)
    mean_eg = jnp.mean(e * gated, axis=1, keepdims=True)
    ggated = rho * e - gated * (rho * rho * rho * mean_eg)
    gg = (ggated * mixed * sig * (1.0 + gz * (1.0 - sig))).astype(BF)
    gg_o[...] = gg
    gm = (ggated * sil).astype(BF)
    gm_o[...] = gm
    gn_o[...] = nt(gg[:, :half], wl) + nt(gg[:, half:], wr)
    gm32 = gm.astype(F32)
    gw = (gm32 * wide).astype(BF)
    dcs_o[...] = nt(gw, st[...])
    shift = jnp.where(flag[0] == 0, HEADS, 0)
    gather = (lax.div(iota((INNER, 128), 0), 64) + shift == iota((INNER, 128), 1)).astype(BF)
    dlr_o[...] = nn((gm32 * seam).astype(BF), gather)
    dst = nn(ct[...], gw)

    @pl.when(step == 0)
    def _():
        acc[...] = dst
        ggain_o[...] = part

    @pl.when(step > 0)
    def _():
        acc[...] += dst
        ggain_o[...] += part

    dst_o[...] = acc[...].astype(BF)


def gate(flag, y, wrc, c, ct, st, normed, rest, tok, og, gain, rb=128):
    T = y.shape[0]
    row = lambda n: pl.BlockSpec((rb, n), lambda i: (i, 0))
    shapes = [((T, INNER), BF), ((T, D), BF), ((T, INNER), BF), ((T, INNER), BF), ((T, D), F32), ((T, 64), F32),
              ((T, 128), F32), ((64, INNER), BF), ((1, INNER), F32)]
    return pl.pallas_call(
        functools.partial(gate_kernel, rest.shape[1] // 4),
        grid=(T // rb,),
        in_specs=[SMEM_SPEC, row(INNER), row(128), row(64), pl.BlockSpec((64, rb), lambda i: (0, i)), full((64, INNER)),
                  row(D), full(rest.shape), row(D), row(D), full((1, INNER))],
        out_specs=[row(INNER), row(D), row(INNER), row(INNER), row(D), row(64), row(128), full((64, INNER)), full((1, INNER))],
        out_shape=[jax.ShapeDtypeStruct(s, d) for s, d in shapes],
        scratch_shapes=[pltpu.VMEM((64, INNER), F32)],
        compiler_params=params(),
        name="gate",
    )(flag, y, wrc, c, ct, st, normed, rest, tok, og, gain)


def unmix_kernel(T, flag, b, c, rows, x, g, dx_o, rsum_o, csum_o, dbc_o, sc, dsc):
    step = pl.program_id(0)
    Q = 128

    @pl.when(step == 0)
    def _():
        sc[...] = jnp.where(same_doc(flag, T), nt(b[...], c[...]), 0.0)
        dsc[...] = jnp.zeros((T, T), F32)
        csum_o[...] = jnp.zeros((T, 128), F32)
        rsum_o[...] = jnp.zeros((128, T), F32)

    r = rows[0]
    cols = r[0:8].T
    x2 = x[...]
    g2 = g[...]
    earlier = iota((Q, Q), 0) < iota((Q, Q), 1)
    lane = iota((Q, 128), 1)
    half = lane < 64
    base = 2 * step
    totals = [[None, None], [None, None]]
    for j in range(T // Q):
        lo, hi = j * Q, (j + 1) * Q
        outs = []
        xs = x2[lo:hi, :]
        stat = jnp.zeros((Q, 128), F32)
        for h in range(2):
            kf = cols[lo:hi, 4 + h : 5 + h]
            kr = cols[lo:hi, 6 + h : 7 + h]
            cf = r[h : h + 1]
            cr = r[2 + h : 3 + h]
            keep = half if h == 0 else ~half
            gt = nt(jnp.where(keep, xs, jnp.zeros_like(xs)), g2)
            parts = []
            if j > 0:
                parts.append(kr - cr[:, :lo])
            parts.append(jnp.where(earlier, cf[:, lo:hi] - kf, kr - cr[:, lo:hi]))
            if hi < T:
                parts.append(cf[:, hi:] - kf)
            d = jnp.exp2(jnp.concatenate(parts, axis=1))
            m = sc[lo:hi, :] * d
            outs.append(nn(m.astype(BF), g2))
            dsc[lo:hi, :] += gt * d
            w = gt * m
            wd = w[:, lo:hi]
            wdf = jnp.where(earlier, wd, 0.0)
            wf = [wdf] + ([w[:, hi:]] if hi < T else [])
            wr = ([w[:, :lo]] if j > 0 else []) + [wd - wdf]
            wf = jnp.concatenate([jnp.zeros((Q, lo), F32)] * (j > 0) + wf, axis=1)
            wr = jnp.concatenate(wr + [jnp.zeros((Q, T - hi), F32)] * (hi < T), axis=1)
            cfs = jnp.sum(wf, axis=1, keepdims=True)
            crs = jnp.sum(wr, axis=1, keepdims=True)
            stat = stat + jnp.where(lane == base + h, cfs, 0.0) + jnp.where(lane == HEADS + base + h, crs, 0.0)
            for q, part in ((0, wf), (1, wr)):
                s = jnp.sum(part, axis=0, keepdims=True)
                totals[q][h] = s if totals[q][h] is None else totals[q][h] + s
        dx_o[lo:hi, :] = jnp.where(half, outs[0], outs[1])
        csum_o[lo:hi, :] += stat
    for q in range(2):
        for h in range(2):
            rsum_o[pl.ds(HEADS * q + base + h, 1), :] = totals[q][h]

    @pl.when(step == PAIRS - 1)
    def _():
        ds = jnp.where(same_doc(flag, T), dsc[...], 0.0)
        dbc_o[:, 0:64] = nn(ds.astype(BF), c[...])
        dbc_o[:, 64:128] = nn(ds.T.astype(BF), b[...])


def unmix(flag, b, c, rows, act, g):
    T = b.shape[0]
    blk = pl.BlockSpec((T, 128), lambda i: (0, i))
    shapes = [((T, INNER), F32), ((128, T), F32), ((T, 128), F32), ((T, 128), F32)]
    return pl.pallas_call(
        functools.partial(unmix_kernel, T),
        grid=(PAIRS,),
        in_specs=[SMEM_SPEC, full((T, 64)), full((T, 64)),
                  pl.BlockSpec((1, 16, T), lambda i: (i, 0, 0)), blk, blk],
        out_specs=[blk, full((128, T)), full((T, 128)), full((T, 128))],
        out_shape=[jax.ShapeDtypeStruct(s, d) for s, d in shapes],
        scratch_shapes=[pltpu.VMEM((T, T), F32), pltpu.VMEM((T, T), F32)],
        compiler_params=params(),
        name="unmix",
    )(flag, b, c, rows, act, g)


def unproject_kernel(T, flag, dx, g, act, z, pre, w, cw, rows, dst, b, normed, nh, skip, bias, alog,
                     rsum, csum, dbc, dcs, dlr, gn_in, tok, halo, ggain,
                     dw_o, gn_o, gnh_o, small_o,
                     nt_s, ht_s, pre_s, shift_s, hd_s, dbs, dls, small, segc):
    step = pl.program_id(0)
    E = T + HALO

    @pl.when(step == 0)
    def _():
        segc[...] = doc_col(flag, T, HALO)
        small[...] = jnp.zeros((SMALL, CH), F32)
        nt_s[...] = normed[...].astype(F32).T.astype(BF)
        pad = jnp.concatenate([nh[...].astype(F32), jnp.zeros((128 - HALO, D), F32)], axis=0)
        ht_s[...] = pad.T.astype(BF)
        hd_s[...] = jnp.zeros((128, CH), BF)
        shift_s[...] = jnp.zeros((E + 8, CH), F32)
        gn_o[...] = gn_in[...]
        gnh_o[...] = jnp.zeros((HALO, D), F32)
        dbs[...] = jnp.zeros((T, 64), F32)
        dls[...] = jnp.zeros((T, 128), F32)

    def through_conv(dact):
        zz = z[...].astype(F32)
        sg = sigm(zz)
        dz = dact * sg * (1.0 + zz * (1.0 - sg))
        small[pl.ds(CONV * NCH + step, 1), :] = jnp.sum(dz, axis=0, keepdims=True)
        pre_s[...] = pre[...].astype(F32)
        here = segc[HALO:, :]
        total = jnp.zeros((E, CH), F32)
        for k in range(CONV):
            tap = slice(CONV - 1 - k, CONV - k)
            dk = dz if k == 0 else jnp.where(segc[HALO - k : E - k, :] == here, dz, 0.0)
            small[pl.ds(CONV * step + CONV - 1 - k, 1), :] = jnp.sum(dk * pre_s[HALO - k : E - k, :], axis=0, keepdims=True)
            shift_s[HALO:E, :] = dk
            total = total + cw[tap, :] * shift_s[k : E + k, :]
        return total

    def emit(local, halo):
        local = local.astype(BF)
        hd_s[0:HALO, :] = halo.astype(BF)
        dw_o[0] = (nn(nt_s[...], local) + nn(ht_s[...], hd_s[...])).astype(BF)
        gn_o[...] += nt(local, w[...])
        gnh_o[...] += nt(hd_s[0:HALO, :], w[...])

    @pl.when(step < NCH - 1)
    def _():
        wides = []
        for j in range(CH // 128):
            cols = rows[2 * step + j, 8:16, :].T
            wides.append(lane_pair(cols[:, 0:1], cols[:, 1:2], T))
        wide = jnp.concatenate(wides, axis=1)
        x32 = act[...].astype(F32)
        g32 = g[...].astype(F32)
        wq = wide * nn(b[...], dst[...])
        dbs[...] += nt((x32 * wide).astype(BF), dst[...])
        base = 4 * step + jnp.where(flag[0] == 0, 0, HEADS)
        sel = (lax.div(iota((CH, 128), 0), 64) + base == iota((CH, 128), 1)).astype(BF)
        dls[...] += nn((x32 * wq).astype(BF), sel)
        small[pl.ds((CONV + 1) * NCH + step, 1), :] = jnp.sum(g32 * x32, axis=0, keepdims=True)
        total = through_conv(dx[...] + wq + skip[...] * g32)
        emit(total[HALO:], total[:HALO])

    @pl.when(step == NCH - 1)
    def _():
        dact = dbc[...] + jnp.concatenate([dbs[...], dcs[...]], axis=1)
        total = through_conv(jnp.concatenate([dact, jnp.zeros((T, 128), F32)], axis=1))
        v = pre_s[HALO:, 128:] + bias[...]
        dt = jnp.maximum(v, 0.0) + jnp.log1p(jnp.exp(-jnp.abs(v)))
        sg = sigm(v)
        a = -jnp.exp(alog[...])
        ratio = jnp.where(v < -15.0, 1.0, sg / jnp.maximum(dt, 1e-30))
        isf = iota((T, 128), 1) < HEADS
        rs = rsum[...].T
        cs = csum[...]
        first = flag[0] == 0
        seam = dls[...] + dlr[...]
        dp = jnp.where(isf, rs - cs, cs - rs) + jnp.where(first, -1.0, 1.0) * seam
        tot = jnp.where(first, 1.0, 0.0) * jnp.sum(seam, axis=0, keepdims=True)
        after = (iota((T, T), 0) <= iota((T, T), 1)).astype(F32)
        inc = lax.dot_general(after, dp, (((1,), (0,)), ((), ())), precision=HI, preferred_element_type=F32)
        dl = jnp.where(isf, inc, inc - dp) + tot
        dv = dl * a * sg + (cs + dls[...]) * ratio
        emit(jnp.concatenate([total[HALO:, :128], dv], axis=1), total[:HALO])

        def unit(v):
            v = v.astype(F32)
            return v * lax.rsqrt(jnp.mean(v * v, axis=1, keepdims=True) + EPS)

        at = SMALL_AT
        small[at : at + 1, 0:128] = jnp.sum(dv, axis=0, keepdims=True)
        small[at : at + 1, 128:] = jnp.sum(dl * dt * a, axis=0, keepdims=True)
        for q in range(INNER // CH):
            small[at + 1 + q : at + 2 + q, :] = ggain[:, CH * q : CH * (q + 1)]
        part = jnp.sum(gn_o[...] * unit(tok[...]), axis=0, keepdims=True)
        part = part + jnp.sum(gnh_o[...] * unit(halo[...]), axis=0, keepdims=True)
        for q in range(D // CH):
            small[at + 7 + q : at + 8 + q, :] = part[:, CH * q : CH * (q + 1)]
        small_o[...] = small[...].astype(BF)


def unproject(flag, dx, g, act, z, pre, w1, conv_w, rows, dst, b, normed, nh, skip, bias, alog,
              rsum, csum, dbc, dcs, dlr, gn, tok, halo, ggain):
    T = dx.shape[0]
    E = T + HALO
    col = lambda rows: pl.BlockSpec((rows, CH), lambda i: (0, i))
    xcol = lambda rows: pl.BlockSpec((rows, CH), lambda i: (0, jnp.minimum(i, NCH - 2)))
    shapes = [((NCH, D, CH), BF), ((T, D), F32), ((HALO, D), F32), ((SMALL, CH), BF)]
    return pl.pallas_call(
        functools.partial(unproject_kernel, T),
        grid=(NCH,),
        in_specs=[SMEM_SPEC, xcol(T), xcol(T), xcol(T), col(T), col(E), col(D), col(CONV), full((PAIRS, 16, T)),
                  xcol(64), full((T, 64)), full((T, D)), full((HALO, D)), xcol(1), full((1, 128)), full((1, 128)),
                  full((128, T)), full((T, 128)), full((T, 128)), full((T, 64)), full((T, 128)), full((T, D)),
                  full((T, D)), full((HALO, D)), full((1, INNER))],
        out_specs=[pl.BlockSpec((1, D, CH), lambda i: (i, 0, 0)), full((T, D)), full((HALO, D)),
                   full((SMALL, CH))],
        out_shape=[jax.ShapeDtypeStruct(s, d) for s, d in shapes],
        scratch_shapes=[pltpu.VMEM((D, T), BF), pltpu.VMEM((D, 128), BF), pltpu.VMEM((E, CH), F32),
                        pltpu.VMEM((E + 8, CH), F32), pltpu.VMEM((128, CH), BF), pltpu.VMEM((T, 64), F32),
                        pltpu.VMEM((T, 128), F32), pltpu.VMEM((SMALL, CH), F32), pltpu.VMEM((E, 1), jnp.int32)],
        compiler_params=params(),
        name="unproject",
    )(flag, dx, g, act, z, pre, w1, conv_w, rows, dst, b, normed, nh, skip, bias, alog, rsum, csum, dbc, dcs, dlr, gn, tok, halo, ggain)


def flip(v, axis, bit):
    size = lax.axis_size(axis)
    return lax.ppermute(v, axis, [(i, i ^ (1 << bit)) for i in range(size)])


def bit_of(axis, bit):
    return lax.rem(lax.div(lax.axis_index(axis), 1 << bit), 2)


def width(axis):
    return lax.axis_size(axis).bit_length() - 1


def gather_rows(shard, ready, rest):
    out = shard
    done = 0
    for bit in reversed(range(width("dp"))):
        other = flip(out, "dp", bit)
        low = bit_of("dp", bit) == 0
        out = jnp.stack([jnp.where(low, out, other), jnp.where(low, other, out)], axis=done)
        done += 1
        if done == 1:
            out, ready = lax.optimization_barrier((out, ready))
        if done == 2:
            out, rest = lax.optimization_barrier((out, rest))
    return out.reshape((-1,) + shard.shape[1:]), ready, rest


def halves(v, mine):
    n = v.shape[0] // 2
    return lax.dynamic_slice_in_dim(v, mine * n, n), lax.dynamic_slice_in_dim(v, (1 - mine) * n, n)


def add(p, q):
    return (p.astype(F32) + q.astype(F32)).astype(BF)


def reduce_all(main, small):
    order = [("dir", 0)] + [("dp", bit) for bit in range(1, width("dp"))]
    order = [o for o in order if o[1] < width(o[0])]
    paired = width("dp") > 0
    if paired:
        mine = bit_of("dp", 0)
        (keep, send), (keep_s, send_s) = halves(main, mine), halves(small, mine)
        main, small = add(keep, flip(send, "dp", 0)), add(keep_s, flip(send_s, "dp", 0))
    rows = main.shape[0]
    buf = jnp.concatenate([main, small], axis=0)
    for axis, bit in order:
        keep, send = halves(buf, bit_of(axis, bit))
        buf = add(keep, flip(send, axis, bit))
    for axis, bit in reversed(order):
        got = flip(buf, axis, bit)
        low = bit_of(axis, bit) == 0
        buf = jnp.concatenate([jnp.where(low, buf, got), jnp.where(low, got, buf)], axis=0)
    if not paired:
        return buf[:rows], buf[rows:]
    got = flip(buf, "dp", 0)
    low = bit_of("dp", 0) == 0
    lo, hi = jnp.where(low, buf, got), jnp.where(low, got, buf)
    return jnp.concatenate([lo[:rows], hi[:rows]], axis=0), jnp.concatenate([lo[rows:], hi[rows:]], axis=0)


def assemble_kernel(wg, x, last, wo, small, zx_o, bc_o, dt_o, wo_o, cw_o):
    step = pl.program_id(0)
    wo_o[...] = wo[...].astype(F32)

    @pl.when(step < INNER // CH)
    def _():
        zx_o[...] = wg[...].astype(F32)

    @pl.when(step >= INNER // CH)
    def _():
        zx_o[...] = x[0].astype(F32)

    @pl.when(step == 0)
    def _():
        tail = last[0].astype(F32)
        bc_o[...] = tail[:, :128]
        dt_o[...] = tail[:, 128 : 128 + 2 * HEADS]
        sm = small[...].astype(F32)
        for q in range(NCH - 1):
            cw_o[:, CH * q : CH * (q + 1)] = sm[CONV * q : CONV * (q + 1), :]
        cw_o[:, INNER:] = sm[CONV * (NCH - 1) : CONV * NCH, :128]


def assemble(wg, main, wo, small):
    n = INNER // CH
    taps = INNER + 2 * STATE
    rb = INNER // (2 * n)
    shapes = [(D, 2 * INNER), (D, 2 * STATE), (D, 2 * HEADS), (INNER, D), (CONV, taps)]
    return pl.pallas_call(
        assemble_kernel,
        grid=(2 * n,),
        in_specs=[pl.BlockSpec((D, CH), lambda i: (0, jnp.minimum(i, n - 1))),
                  pl.BlockSpec((1, D, CH), lambda i: (jnp.maximum(i - n, 0), 0, 0)),
                  pl.BlockSpec((1, D, CH), lambda i: (NCH - 1, 0, 0)),
                  pl.BlockSpec((rb, D), lambda i: (i, 0)), full(small.shape)],
        out_specs=[pl.BlockSpec((D, CH), lambda i: (0, i)), full(shapes[1]), full(shapes[2]),
                   pl.BlockSpec((rb, D), lambda i: (i, 0)), full(shapes[4])],
        out_shape=[jax.ShapeDtypeStruct(s, F32) for s in shapes],
        compiler_params=params(),
        name="assemble",
    )(wg, main, main, wo, small)


def body(tokens, norm_gain, w_zx, w_bc, w_dt, conv_w, conv_b, dt_bias, a_log, d_skip, out_gain, w_out, doc_lengths, out_grad):
    T = tokens.shape[1]
    devices = lax.axis_size("dir") * lax.axis_size("dp")
    side = lax.axis_index("dir")
    swap = lambda v: flip(v, "dir", 0)
    tok = tokens.reshape(T, D)
    og = out_grad.reshape(T, D)
    shard = w_zx.shape[0]
    half = INNER // 2
    mine = jnp.concatenate([w_zx[:, INNER:], w_bc, w_dt, jnp.zeros((shard, 128 - 2 * HEADS), BF)], axis=1)
    rest = jnp.concatenate([w_zx[:, :half], w_zx[:, half:INNER], w_out], axis=0)
    halo = lax.ppermute(tok[T - HALO :], "dir", [(0, 1)])
    flag = jnp.concatenate([side[None].astype(jnp.int32), doc_lengths[0]])
    wide = NCH * CH
    cw = jnp.pad(conv_w, ((0, 0), (0, wide - conv_w.shape[1])))
    cb = jnp.pad(conv_b, (0, wide - conv_b.shape[0]))[None]
    lanes = lambda v: jnp.pad(v, (0, 128 - v.shape[0]))[None]
    skip = jnp.repeat(d_skip, HEADDIM)[None]
    ready = (halo, flag, cw, cb, lanes(dt_bias), lanes(a_log), skip, norm_gain[None], out_gain[None])
    w1, ready, rest = gather_rows(mine, ready, rest)
    halo, flag, cw, cb, bias, alog, skip, gain_in, gain_out = ready
    rest = lax.all_gather(rest, "dp", axis=0, tiled=False)
    if shard % 16:
        rest = jnp.concatenate([rest[:, :shard].reshape(D, D), rest[:, shard : 2 * shard].reshape(D, D),
                                rest[:, 2 * shard :].reshape(INNER, D)], axis=0)[None]
    normed, nh, pre, z, act, rows, wrc, b, bt, c, ct, st = project(flag, tok, halo, gain_in, w1, cw, cb, bias, alog)
    st_in = swap(st)
    y = mix(flag, b, c, rows, act, skip)
    no, bo, gg, gm, gn, dcs, dlr, dst, ggain = gate(flag, y, wrc, c, ct, st_in, normed, rest, tok, og, gain_out)
    tn = lambda p, q: lax.dot_general(p, q, (((0,), (0,)), ((), ())), preferred_element_type=F32).astype(BF)
    dwo, dwg = tn(no, og), tn(normed, gg)
    dwo, dwg, gm = lax.optimization_barrier((dwo, dwg, gm))
    dwo, dwg = lax.psum((dwo, dwg), ("dir", "dp"))
    def finish(v):
        (flag, b, c, rows, act, gm, z, pre, w1, cw, dst, normed, nh, skip, bias, alog, dcs, dlr, gn, tok, halo, ggain, og, gain_in) = v
        dst_in = swap(dst)
        dx, rsum, csum, dbc = unmix(flag, b, c, rows, act, gm)
        dw1, gn, gnh, small = unproject(flag, dx, gm, act, z, pre, w1, cw, rows, dst_in, b, normed, nh, skip, bias, alog,
                                        rsum, csum, dbc, dcs, dlr, gn, tok, halo, ggain)
        back = lax.ppermute(gnh, "dir", [(1, 0)])
        main = dw1.reshape(NCH * D, CH)
        total = -(-(main.shape[0] + SMALL) // (16 * devices)) * 16 * devices
        small = jnp.pad(small, ((0, total - main.shape[0] - SMALL), (0, 0)))
        main, small = reduce_all(main, small)
        gn = gn + jnp.pad(back, ((T - HALO, 0), (0, 0)))
        x32 = tok.astype(F32)
        rho = lax.rsqrt(jnp.mean(x32 * x32, axis=1, keepdims=True) + EPS)
        e_in = gn * gain_in
        gx = rho * e_in - x32 * (rho * rho * rho * jnp.mean(e_in * x32, axis=1, keepdims=True))
        grad_tokens = (og.astype(F32) + gx).astype(BF)
        return main, small, grad_tokens

    def nothing(v):
        return tuple(jnp.zeros(o.shape, o.dtype) for o in jax.eval_shape(finish, v))

    args = (flag, b, c, rows, act, gm, z, pre, w1, cw, dst, normed, nh, skip, bias, alog, dcs, dlr, gn, tok, halo, ggain, og, gain_in)
    main, small, grad_tokens = lax.cond(flag[1] >= 0, finish, nothing, args)
    gw_zx, gw_bc, gw_dt, gw_out, g_cw = assemble(dwg, main.reshape(NCH, D, CH), dwo, small)
    small = small.astype(F32)
    g_cb = small[CONV * NCH : (CONV + 1) * NCH].reshape(wide)[: INNER + 2 * STATE]
    g_skip = jnp.sum(small[(CONV + 1) * NCH : SMALL_AT].reshape(HEADS, HEADDIM), axis=1)
    g_bias = small[SMALL_AT, : 2 * HEADS]
    g_alog = small[SMALL_AT, 128 : 128 + 2 * HEADS]
    g_out = small[SMALL_AT + 1 : SMALL_AT + 7].reshape(INNER)
    g_in = small[SMALL_AT + 7 : SMALL_AT + 10].reshape(D)
    return (bo.reshape(tokens.shape), grad_tokens.reshape(tokens.shape), g_in, gw_zx, gw_bc, gw_dt, g_cw, g_cb, g_bias,
            g_alog, g_skip, g_out, gw_out)


def solution(mesh):
    rows, weight, whole = P("dp", "dir", None), P("dp", None), P()
    placed = (rows, whole, weight, weight, weight, whole, whole, whole, whole, whole, whole, weight, weight, rows)
    return jax.shard_map(body, mesh=mesh, in_specs=placed, out_specs=(rows, rows) + (whole,) * 11, check_vma=False)
```

time: 1100 us -> 317 us (0.29); the launches traced: 1080 us -> 315 us
  local copies, waits for them, and re-layouts: 336 us -> 33.7 us
  matrix products: 265 us -> 7.24 us
  other arithmetic: 142 us -> 20.7 us
  Pallas kernels: 0 us -> 100 us
  waiting for transfers between devices: 207 us -> 116 us
  blocking collectives: 85.5 us -> 0 us
  loops' own time: 24 us -> 0.58 us
  starting transfers between devices: 7 us -> 21.3 us
    dot_general x127 -> x2, matrix products: 265 us -> 7.24 us  [body(): lax.dot_general(p, q, (((0,), (0,)), ((), ())), preferred_element_type=F32)]
    psum x1, waiting for transfers between devices: 200 us -> 0.01 us  [body(): dwo, dwg = lax.psum((dwo, dwg), ('dir', 'dp'))]
    ppermute x4 -> x19, waiting for transfers between devices: 2.35 us -> 113 us  [the longest x17 109 us: flip(): return lax.ppermute(v, axis, [(i, i ^ 1 << bit) for i in range(size)])]
    pallas_call x0 -> x6, Pallas kernels: none -> 100 us  [the longest x1 23.8 us: unmix(): pl.pallas_call(functools.partial(unmix_kernel, T), grid=(PAIRS,), in_spec...]
    rev x14 -> x0, local copies, waits for them, and re-layouts: 72.8 us -> none  [the longest x2 49.4 us: one_half(): jnp.flip(x_in, axis=0)]
    reshape x28 -> x4, local copies, waits for them, and re-layouts: 70.1 us -> 5.23 us  [the longest x1 1.36 us: body(): small[(CONV + 1) * NCH:SMALL_AT].reshape(HEADS, HEADDIM)]
    unnamed x228 -> x31, local copies, waits for them, and re-layouts: 52.9 us -> 3.34 us
    all_gather x2 -> x0, blocking collectives: 43.3 us -> none  [the longest x1 24.4 us: body(): lax.all_gather(w_bc, 'dp', axis=0, tiled=True)]
  transfers between devices with their start and end apart: 7 -> 21, of which waited for: 3 -> 14; matrix products, arithmetic and copies ran while one was open for 30% -> 16% of each run, Pallas kernels for 0% -> 23%
where the time goes in v1:
time: 317 us; the launch traced here: 315 us
  waiting for transfers between devices  116 us (37%)
  Pallas kernels  100 us (32%)
  local copies, waits for them, and re-layouts  33.7 us (11%)
  starting transfers between devices  21.3 us (7%)
  other arithmetic  20.7 us (7%)
  between operations  15 us (5%)
  matrix products  7.24 us (2%)
    ppermute x17, waiting for transfers between devices, flip(): return lax.ppermute(v, axis, [(i, i ^ 1 << bit) for i in range(size)])  109 us
    pallas_call x1, Pallas kernels, unmix(): pl.pallas_call(functools.partial(unmix_kernel, T), grid=(PAIRS,), in_spec...  23.8 us
    pallas_call x1, Pallas kernels, unproject(): pl.pallas_call(functools.partial(unproject_kernel, T), grid=(NCH,), in_sp...  21 us
    pallas_call x1, Pallas kernels, gate(): pl.pallas_call(functools.partial(gate_kernel, rest.shape[1] // 4), grid=(...  18.3 us
    ppermute x17, starting transfers between devices, flip(): return lax.ppermute(v, axis, [(i, i ^ 1 << bit) for i in range(size)])  16.4 us
    pallas_call x1, Pallas kernels, project(): pl.pallas_call(functools.partial(project_kernel, T), grid=(NCH,), in_spec...  14 us
    pallas_call x1, Pallas kernels, mix(): pl.pallas_call(functools.partial(mix_kernel, T), grid=(PAIRS,), in_specs=...  12.4 us
    pallas_call x1, Pallas kernels, assemble(): pl.pallas_call(assemble_kernel, grid=(2 * n,), in_specs=[pl.BlockSpec((D,...  10.7 us
  transfers between devices with their start and end apart: 21, of which 14 were waited for; matrix products, arithmetic and copies ran while one was open for 16% of the time, Pallas kernels for 23%

profile of v1, /device:TPU:0, one launch (start us, length us, event | category | flops | bytes accessed | tf_op | source)
XLA Modules:
  0.0 314.8 jit_solution(5723637546917731673)
XLA Ops:
  9.0 4.1 %collective-permute-start.13 = (bf16[48,1792]{1,0:T(8,128)(2,1)S(1)}, bf16[48,1792]{1,0:T(8,128)(2,1)S(1)}, u32[]{:S(2)}, u32[]{:S(2)}) collective-permute-start(bf16[48,1792]{1,0:T(8,128)(2,1)S(1)} %concatenate.30), channel_id=1, source_target_pairs={{0,8},{1,9},{2,10},{3,11},{4,12},{5,13},{6,14},{7,15},{8,0},{9,1},... | collective-permute-start | bytes 516104 | tf_op jit(solution)/shard_map/ppermute | solution.py:533
  13.9 3.4 %collective-permute-start.14 = (bf16[16,768]{1,0:T(8,128)(2,1)S(1)}, bf16[16,768]{1,0:T(8,128)(2,1)S(1)}, u32[]{:S(2)}, u32[]{:S(2)}) collective-permute-start(bf16[16,768]{1,0:T(8,128)(2,1)S(1)} %slice_bitcast_fusion), channel_id=1, source_target_pairs={{0,16},{1,17},{2,18},{3,19},{4,20},{5,21},{6,22},{7,23},{8,24},{9,... | collective-permute-start | bytes 73736 | tf_op jit(solution)/shard_map/ppermute | solution.py:647
  17.3 1.4 pad.23.cw
  25.4 1.6 collective-permute-start.15
  27.8 6.9 %collective-permute-done.15 = bf16[2,48,1792]{2,1,0:T(8,128)(2,1)S(1)} collective-permute-done((bf16[2,48,1792]{2,1,0:T(8,128)(2,1)S(1)}, bf16[2,48,1792]{2,1,0:T(8,128)(2,1)S(1)}, u32[]{:S(2)}, u32[]{:S(2)}) %collective-permute-start.15) | collective-permute-done | bytes 344096 | tf_op jit(solution)/shard_map/ppermute | solution.py:533
  34.9 1.6 collective-permute-start.16
  36.4 17.4 %collective-permute-done.16 = bf16[2,2,48,1792]{3,2,0,1:T(8,128)(2,1)S(1)} collective-permute-done((bf16[2,2,48,1792]{3,2,0,1:T(8,128)(2,1)S(1)}, bf16[2,2,48,1792]{3,2,0,1:T(8,128)(2,1)S(1)}, u32[]{:S(2)}, u32[]{:S(2)}) %collective-permute-start.16) | collective-permute-done | bytes 688160 | tf_op jit(solution)/shard_map/ppermute | solution.py:533
  55.1 3.3 %collective-permute-done.17 = bf16[2,2,2,48,1792]{4,3,0,1,2:T(8,128)(2,1)S(1)} collective-permute-done((bf16[2,2,2,48,1792]{4,3,0,1,2:T(8,128)(2,1)}, bf16[2,2,2,48,1792]{4,3,0,1,2:T(8,128)(2,1)S(1)}, u32[]{:S(2)}, u32[]{:S(2)}) %collective-permute-start.17) | collective-permute-done | bytes 1376288 | tf_op jit(solution)/shard_map/ppermute | solution.py:533
  60.0 14.0 %project.1 = (bf16[512,768]{1,0:T(8,128)(2,1)}, bf16[16,768]{1,0:T(8,128)(2,1)}, bf16[528,1792]{1,0:T(8,128)(2,1)}, bf16[512,1792]{1,0:T(8,128)(2,1)}, bf16[512,...) custom-call(s32[5]{0:T(128)S(1)} %pad_add_fusion.flag, ...), custom_call_target="tpu_custom_call" | custom-call | tf_op jit(solution)/shard_map/project/pallas_call | solution.py:185
  74.1 12.4 %mix.1.y = f32[512,1536]{1,0:T(8,128)} custom-call(s32[5]{0:T(128)S(1)} %pad_add_fusion.flag, bf16[512,64]{1,0:T(8,128)(2,1)S(1)} %get-tuple-element.168.b, bf16[512,64]{1,0:T(8,128)(2,1)} %get-tuple-element.169.c, f32[12,16,512]{2,1,0:T(8,128)S(1)} %get-tuple-element.170.rows, bf16[512,1792]{1,0:T(8,128)(2,1)} %get-tuple-element.171.x, ...), custom_call_target="tpu_custom_call" | custom-call | tf_op jit(solution)/shard_map/mix/pallas_call | solution.py:238
  86.6 2.8 all-gather.3.cloned.1.call-done
  89.4 18.3 %gate.1 = (bf16[512,1536]{1,0:T(8,128)(2,1)}, bf16[512,768]{1,0:T(8,128)(2,1)}, bf16[512,1536]{1,0:T(8,128)(2,1)}, bf16[512,1536]{1,0:T(8,128)(2,1)}, f32[512,76...) custom-call(s32[5]{0:T(128)S(1)} %pad_add_fusion.flag, ...), custom_call_target="tpu_custom_call" | custom-call | tf_op jit(solution)/shard_map/gate/pallas_call | solution.py:308
  107.7 4.4 %convolution_convert_fusion.1 = bf16[1536,768]{1,0:T(8,128)(2,1)} fusion(bf16[512,1536]{1,0:T(8,128)(2,1)} %get-tuple-element.180, bf16[1,512,768]{2,1,0:T(8,128)(2,1)S(1)} %copy-done.8), kind=kOutput, calls=%fused_computation.48 | convolution fusion | flops 1209139200 | bytes 4718592 | tf_op jit(solution)/shard_map/dot_general | solution.py:665
  112.1 2.9 convolution_convert_fusion
  116.2 179.2 %conditional.1 = (bf16[256,256]{1,0:T(8,128)(2,1)}, bf16[7,768,256]{2,1,0:T(8,128)(2,1)S(1)}, bf16[256,256]{1,0:T(8,128)(2,1)}, f32[3,256]{1,0:T(4,128)}, f32[7,...) conditional(s32[]{:T(128)} %bitcast.23, () %tuple.27, ...), branch_computations={%region_0.1_spmd, %region_1.5_spmd} | conditional | flops 33779276 | bytes 103021296 | solution.py:692
  116.5 1.6 collective-permute-start
  118.1 23.8 %unmix.1 = (f32[512,1536]{1,0:T(8,128)}, f32[128,512]{1,0:T(8,128)}, f32[512,128]{1,0:T(8,128)}, f32[512,128]{1,0:T(8,128)}) custom-call(s32[5]{0:T(128)S(1)} %get-tuple-element.65.flag, bf16[512,64]{1,0:T(8,128)(2,1)} %get-tuple-element.66.b, bf16[512,64]{1,0:T(8,128)(2,1)} %copy-done.14, f32[12,16,512]{2,1,0:T(8,128)} %get-tuple-element.68.rows, ...), custom_call_target="tpu_custom_call" | custom-call | tf_op jit(solution)/shard_map/cond/branch_1_fun/unmix/pallas_call | solution.py:393
  142.0 21.0 %unproject.1 = (bf16[7,768,256]{2,1,0:T(8,128)(2,1)}, f32[512,768]{1,0:T(8,128)}, f32[16,768]{1,0:T(8,128)}, bf16[64,256]{1,0:T(8,128)(2,1)}) custom-call(s32[5]{0:T(128)S(1)} %get-tuple-element.65.flag, f32[512,1536]{1,0:T(8,128)} %get-tuple-element.71.dx, bf16[512,1536]{1,0:T(8,128)(2,1)} %get-tuple-element.70.g, ...), custom_call_target="tpu_custom_call" | custom-call | tf_op jit(solution)/shard_map/cond/branch_1_fun/unproject/pallas_call | solution.py:513
  163.0 1.5 constant_dynamic-slice_fusion.3
  166.4 1.7 collective-permute-done.2
  169.0 1.7 add_convert_fusion
  172.6 19.1 %collective-permute-done.3 = bf16[1408,256]{1,0:T(8,128)(2,1)} collective-permute-done((bf16[1408,256]{1,0:T(8,128)(2,1)S(1)}, bf16[1408,256]{1,0:T(8,128)(2,1)}, u32[]{:S(2)}, u32[]{:S(2)}) %collective-permute-start.3) | collective-permute-done | bytes 720928 | tf_op jit(solution)/shard_map/cond/branch_1_fun/ppermute | solution.py:533
  191.7 1.6 add_convert_fusion.1
  193.5 10.2 %collective-permute-done.4 = bf16[704,256]{1,0:T(8,128)(2,1)S(1)} collective-permute-done((bf16[704,256]{1,0:T(8,128)(2,1)S(1)}, bf16[704,256]{1,0:T(8,128)(2,1)S(1)}, u32[]{:S(2)}, u32[]{:S(2)}) %collective-permute-start.4) | collective-permute-done | bytes 360480 | tf_op jit(solution)/shard_map/cond/branch_1_fun/ppermute | solution.py:533
  204.9 4.4 %collective-permute-done.5 = bf16[352,256]{1,0:T(8,128)(2,1)S(1)} collective-permute-done((bf16[352,256]{1,0:T(8,128)(2,1)S(1)}, bf16[352,256]{1,0:T(8,128)(2,1)S(1)}, u32[]{:S(2)}, u32[]{:S(2)}) %collective-permute-start.5) | collective-permute-done | bytes 180256 | tf_op jit(solution)/shard_map/cond/branch_1_fun/ppermute | solution.py:533
  209.4 1.6 collective-permute-start.6
  211.0 7.7 %collective-permute-done.6 = bf16[176,256]{1,0:T(8,128)(2,1)S(1)} collective-permute-done((bf16[176,256]{1,0:T(8,128)(2,1)S(1)}, bf16[176,256]{1,0:T(8,128)(2,1)S(1)}, u32[]{:S(2)}, u32[]{:S(2)}) %collective-permute-start.6) | collective-permute-done | bytes 90144 | tf_op jit(solution)/shard_map/cond/branch_1_fun/ppermute | solution.py:533
  218.8 7.1 %collective-permute-done.7 = bf16[176,256]{1,0:T(8,128)(2,1)S(1)} collective-permute-done((bf16[176,256]{1,0:T(8,128)(2,1)S(1)}, bf16[176,256]{1,0:T(8,128)(2,1)S(1)}, u32[]{:S(2)}, u32[]{:S(2)}) %collective-permute-start.7) | collective-permute-done | bytes 90144 | tf_op jit(solution)/shard_map/cond/branch_1_fun/ppermute | solution.py:533
  226.4 5.2 %collective-permute-done.8 = bf16[352,256]{1,0:T(8,128)(2,1)S(1)} collective-permute-done((bf16[352,256]{1,0:T(8,128)(2,1)S(1)}, bf16[352,256]{1,0:T(8,128)(2,1)S(1)}, u32[]{:S(2)}, u32[]{:S(2)}) %collective-permute-start.8) | collective-permute-done | bytes 180256 | tf_op jit(solution)/shard_map/cond/branch_1_fun/ppermute | solution.py:533
  231.8 12.6 %collective-permute-done.9 = bf16[704,256]{1,0:T(8,128)(2,1)S(1)} collective-permute-done((bf16[704,256]{1,0:T(8,128)(2,1)S(1)}, bf16[704,256]{1,0:T(8,128)(2,1)S(1)}, u32[]{:S(2)}, u32[]{:S(2)}) %collective-permute-start.9) | collective-permute-done | bytes 360480 | tf_op jit(solution)/shard_map/cond/branch_1_fun/ppermute | solution.py:533
  244.6 2.0 collective-permute-start.10
  246.6 13.0 %collective-permute-done.10 = bf16[1408,256]{1,0:T(8,128)(2,1)} collective-permute-done((bf16[1408,256]{1,0:T(8,128)(2,1)S(1)}, bf16[1408,256]{1,0:T(8,128)(2,1)}, u32[]{:S(2)}, u32[]{:S(2)}) %collective-permute-start.10) | collective-permute-done | bytes 720928 | tf_op jit(solution)/shard_map/cond/branch_1_fun/ppermute | solution.py:533
  259.6 1.4 broadcast_select_fusion.3
  262.2 1.4 collective-permute-start.12
  263.6 4.7 %collective-permute-done.12 = f32[16,768]{1,0:T(8,128)S(1)} collective-permute-done((f32[16,768]{1,0:T(8,128)S(1)}, f32[16,768]{1,0:T(8,128)S(1)}, u32[]{:S(2)}, u32[]{:S(2)}) %collective-permute-start.12) | collective-permute-done | bytes 49184 | tf_op jit(solution)/shard_map/cond/branch_1_fun/ppermute | solution.py:675
  268.3 1.8 fusion
  270.1 1.3 fusion.5
  271.5 1.9 broadcast_select_fusion.1
  276.4 1.6 copy.49
  280.6 1.3 fusion.12
  281.9 1.4 fusion.11
  288.2 1.4 reshape.99
  289.6 1.3 reshape.100
  290.9 1.3 copy.62
  292.2 1.9 pad_maximum_fusion
  294.1 1.3 reduce_sum.28
  295.4 10.7 %assemble.1 = (f32[768,3072]{1,0:T(8,128)}, f32[768,128]{1,0:T(8,128)}, f32[768,48]{1,0:T(8,128)}, f32[1536,768]{1,0:T(8,128)}, f32[4,1664]{1,0:T(4,128)}) custom-call(bf16[768,1536]{1,0:T(8,128)(2,1)} %get-tuple-element.223.wg, bf16[7,768,256]{2,1,0:T(8,128)(2,1)S(1)} %get-tuple-element.195.x.last, bf16[7,768,256]{2,1,0:T(8,128)(2,1)S(1)} %get-tuple-element.195.x.last, ...), custom_call_target="tpu_custom_call" | custom-call | tf_op jit(solution)/shard_map/assemble/pallas_call | solution.py:621
  306.2 1.8 copy.28
  (133 shorter events, 32.7 us)
Async XLA Ops:
  7.2 19.8 %copy-start.16 = (bf16[48,3072]{1,0:T(8,128)(2,1)S(1)}, bf16[48,3072]{1,0:T(8,128)(2,1)}, u32[]{:S(2)}) copy-start(bf16[48,3072]{1,0:T(8,128)(2,1)} %param.18) | copy-start | bytes 884740
  7.2 19.8 %copy-start.20 = (bf16[96,768]{1,0:T(8,128)(2,1)S(1)}, bf16[96,768]{1,0:T(8,128)(2,1)}, u32[]{:S(2)}) copy-start(bf16[96,768]{1,0:T(8,128)(2,1)} %param.27) | copy-start | bytes 442372
  7.2 82.2 %all-gather.3.cloned.1.call-start = ((), (), s32[]{:S(2)}) async-start(), calls=%async_computation | async-start | bytes 5013504 | tf_op jit(solution)/shard_map/all_gather | solution.py:657
  9.0 15.7 %collective-permute-start.13 = (bf16[48,1792]{1,0:T(8,128)(2,1)S(1)}, bf16[48,1792]{1,0:T(8,128)(2,1)S(1)}, u32[]{:S(2)}, u32[]{:S(2)}) collective-permute-start(bf16[48,1792]{1,0:T(8,128)(2,1)S(1)} %concatenate.30), channel_id=1, source_target_pairs={{0,8},{1,9},{2,10},{3,11},{4,12},{5,13},{6,14},{7,15},{8,0},{9,1},... | collective-permute-start | bytes 516104 | tf_op jit(solution)/shard_map/ppermute | solution.py:533
  13.9 10.9 %collective-permute-start.14 = (bf16[16,768]{1,0:T(8,128)(2,1)S(1)}, bf16[16,768]{1,0:T(8,128)(2,1)S(1)}, u32[]{:S(2)}, u32[]{:S(2)}) collective-permute-start(bf16[16,768]{1,0:T(8,128)(2,1)S(1)} %slice_bitcast_fusion), channel_id=1, source_target_pairs={{0,16},{1,17},{2,18},{3,19},{4,20},{5,21},{6,22},{7,23},{8,24},{9,... | collective-permute-start | bytes 73736 | tf_op jit(solution)/shard_map/ppermute | solution.py:647
  25.4 9.2 %collective-permute-start.15 = (bf16[2,48,1792]{2,1,0:T(8,128)(2,1)S(1)}, bf16[2,48,1792]{2,1,0:T(8,128)(2,1)S(1)}, u32[]{:S(2)}, u32[]{:S(2)}) collective-permute-start(bf16[2,48,1792]{2,1,0:T(8,128)(2,1)S(1)} %pad_maximum_fusion.9), channel_id=1, source_target_pairs={{0,4},{1,5},{2,6},{3,7},{4,0},{5,1},{6,2},{7,3},{8,12},{9,13},{10,... | collective-permute-start | bytes 1032200 | tf_op jit(solution)/shard_map/ppermute | solution.py:533
  34.8 260.6 %all-reduce.9.cloned.1.call-start = ((), (), s32[]{:S(2)}) async-start(), calls=%async_computation.1 | async-start | bytes 9437184 | tf_op jit(solution)/shard_map/psum | solution.py:668
  34.9 18.9 %collective-permute-start.16 = (bf16[2,2,48,1792]{3,2,0,1:T(8,128)(2,1)S(1)}, bf16[2,2,48,1792]{3,2,0,1:T(8,128)(2,1)S(1)}, u32[]{:S(2)}, u32[]{:S(2)}) collective-permute-start(bf16[2,2,48,1792]{3,2,0,1:T(8,128)(2,1)S(1)} %pad_maximum_fusion.8), channel_id=1, source_target_pairs={{0,2},{1,3},{2,0},{3,1},{4,6},{5,7},{6,4},{7,5},{8,10},{9,11},{10,... | collective-permute-start | bytes 2064392 | tf_op jit(solution)/shard_map/ppermute | solution.py:533
  55.1 3.3 %collective-permute-start.17 = (bf16[2,2,2,48,1792]{4,3,0,1,2:T(8,128)(2,1)}, bf16[2,2,2,48,1792]{4,3,0,1,2:T(8,128)(2,1)S(1)}, u32[]{:S(2)}, u32[]{:S(2)}) collective-permute-start(bf16[2,2,2,48,1792]{4,3,0,1,2:T(8,128)(2,1)} %pad_maximum_fusion.7), channel_id=1, source_target_pairs={{0,1},{1,0},{2,3},{3,2},{4,5},{5,4},{6,7},{7,6},{8,9},{9,8},{10,11... | collective-permute-start | bytes 4128776 | tf_op jit(solution)/shard_map/ppermute | solution.py:533
  58.9 1.1 copy-start.2
  58.9 1.1 copy-start.17
  58.9 1.1 copy-start.23
  59.1 14.9 %copy-start = (bf16[2,2,2,2,48,1792]{5,4,3,2,1,0:T(8,128)(2,1)}, bf16[2,2,2,2,48,1792]{5,4,3,2,1,0:T(8,128)(2,1)S(1)}, u32[]{:S(2)}) copy-start(bf16[2,2,2,2,48,1792]{5,4,3,2,1,0:T(8,128)(2,1)S(1)} %copy.27) | copy-start | bytes 8257540
  74.0 12.5 %copy-start.4 = (f32[12,16,512]{2,1,0:T(8,128)}, f32[12,16,512]{2,1,0:T(8,128)S(1)}, u32[]{:S(2)}) copy-start(f32[12,16,512]{2,1,0:T(8,128)S(1)} %get-tuple-element.170.rows) | copy-start | bytes 1179652
  74.0 12.5 %copy-start.11 = (bf16[512,64]{1,0:T(8,128)(2,1)}, bf16[512,64]{1,0:T(8,128)(2,1)S(1)}, u32[]{:S(2)}) copy-start(bf16[512,64]{1,0:T(8,128)(2,1)S(1)} %get-tuple-element.168.b) | copy-start | bytes 196612
  74.0 12.5 %collective-permute-start.18 = (bf16[64,1536]{1,0:T(8,128)(2,1)}, bf16[64,1536]{1,0:T(8,128)(2,1)S(1)}, u32[]{:S(2)}, u32[]{:S(2)}) collective-permute-start(bf16[64,1536]{1,0:T(8,128)(2,1)} %get-tuple-element.175), channel_id=1, source_target_pairs={{0,16},{16,0},{1,17},{17,1},{2,18},{18,2},{3,19},{19,3},{4,20},{20... | collective-permute-start | bytes 589832 | tf_op jit(solution)/shard_map/ppermute | solution.py:533
  74.1 15.3 %copy-start.6 = (bf16[512,768]{1,0:T(8,128)(2,1)S(1)}, bf16[512,768]{1,0:T(8,128)(2,1)}, u32[]{:S(2)}) copy-start(bf16[512,768]{1,0:T(8,128)(2,1)} %get-tuple-element.176.normed) | copy-start | bytes 2359300
  74.1 15.3 %copy-start.8 = (bf16[1,512,768]{2,1,0:T(8,128)(2,1)S(1)}, bf16[1,512,768]{2,1,0:T(8,128)(2,1)}, u32[]{:S(2)}) copy-start(bf16[1,512,768]{2,1,0:T(8,128)(2,1)} %param.29) | copy-start | bytes 2359300
  74.1 15.3 %copy-start.13 = (bf16[512,64]{1,0:T(8,128)(2,1)S(1)}, bf16[512,64]{1,0:T(8,128)(2,1)}, u32[]{:S(2)}) copy-start(bf16[512,64]{1,0:T(8,128)(2,1)} %get-tuple-element.169.c) | copy-start | bytes 196612
  86.5 2.8 copy-start.19
  107.7 4.4 %copy-start.27 = (bf16[512,1536]{1,0:T(8,128)(2,1)S(1)}, bf16[512,1536]{1,0:T(8,128)(2,1)}, u32[]{:S(2)}) copy-start(bf16[512,1536]{1,0:T(8,128)(2,1)} %get-tuple-element.181) | copy-start | bytes 4718596
  116.4 1.6 copy-start.7
  116.4 1.6 copy-start.9
  116.5 1.6 copy-start.14
  116.5 25.5 %collective-permute-start = (bf16[64,1536]{1,0:T(8,128)(2,1)}, bf16[64,1536]{1,0:T(8,128)(2,1)}, u32[]{:S(2)}, u32[]{:S(2)}) collective-permute-start(bf16[64,1536]{1,0:T(8,128)(2,1)} %get-tuple-element.76), channel_id=1, source_target_pairs={{0,16},{16,0},{1,17},{17,1},{2,18},{18,2},{3,19},{19,3},{4,20},{20... | collective-permute-start | bytes 589832 | tf_op jit(solution)/shard_map/cond/branch_1_fun/ppermute | solution.py:533
  118.1 23.9 %copy-start.1 = (bf16[768,1792]{1,0:T(8,128)(2,1)S(1)}, bf16[768,1792]{1,0:T(8,128)(2,1)}, u32[]{:S(2)}) copy-start(bf16[768,1792]{1,0:T(8,128)(2,1)} %get-tuple-element.74.w) | copy-start | bytes 8257540 | tf_op jit(solution)/shard_map/cond
  118.1 23.9 %copy-start.5 = (f32[12,16,512]{2,1,0:T(8,128)S(1)}, f32[12,16,512]{2,1,0:T(8,128)}, u32[]{:S(2)}) copy-start(f32[12,16,512]{2,1,0:T(8,128)} %get-tuple-element.68.rows) | copy-start | bytes 1179652 | tf_op jit(solution)/shard_map/cond
  118.1 23.9 %copy-start.12 = (bf16[512,64]{1,0:T(8,128)(2,1)S(1)}, bf16[512,64]{1,0:T(8,128)(2,1)}, u32[]{:S(2)}) copy-start(bf16[512,64]{1,0:T(8,128)(2,1)} %get-tuple-element.66.b) | copy-start | bytes 196612 | tf_op jit(solution)/shard_map/cond
  118.1 23.9 %copy-start.18 = (f32[4,1792]{1,0:T(4,128)S(1)}, f32[4,1792]{1,0:T(4,128)}, u32[]{:S(2)}) copy-start(f32[4,1792]{1,0:T(4,128)} %get-tuple-element.75.cw) | copy-start | bytes 86020 | tf_op jit(solution)/shard_map/cond
  118.1 23.9 %copy-start.22 = (f32[1,1536]{1,0:T(1,128)S(1)}, f32[1,1536]{1,0:T(1,128)}, u32[]{:S(2)}) copy-start(f32[1,1536]{1,0:T(1,128)} %get-tuple-element.90.ggain) | copy-start | bytes 18436 | tf_op jit(solution)/shard_map/cond
  118.1 23.9 %copy-start.24 = (f32[1,128]{1,0:T(1,128)S(1)}, f32[1,128]{1,0:T(1,128)}, u32[]{:S(2)}) copy-start(f32[1,128]{1,0:T(1,128)} %get-tuple-element.81.alog) | copy-start | bytes 1540 | tf_op jit(solution)/shard_map/cond
  118.1 23.9 %copy-start.26 = (f32[1,128]{1,0:T(1,128)S(1)}, f32[1,128]{1,0:T(1,128)}, u32[]{:S(2)}) copy-start(f32[1,128]{1,0:T(1,128)} %get-tuple-element.80.bias) | copy-start | bytes 1540 | tf_op jit(solution)/shard_map/cond
  164.4 4.5 %collective-permute-start.1 = (bf16[2688,256]{1,0:T(8,128)(2,1)S(1)}, bf16[2688,256]{1,0:T(8,128)(2,1)S(1)}, u32[]{:S(2)}, u32[]{:S(2)}) collective-permute-start(bf16[2688,256]{1,0:T(8,128)(2,1)S(1)} %constant_dynamic-slice_fusion.3), channel_id=1, source_target_pairs={{0,1},{1,0},{2,3},{3,2},{4,5},{5,4},{6,7},{7,6},{8,9},{9,8},{10,11... | collective-permute-start | bytes 4128776 | tf_op jit(solution)/shard_map/cond/branch_1_fun/ppermute | solution.py:533
  165.2 2.9 collective-permute-start.2
  168.9 1.7 copy-start.15
  171.8 19.9 %collective-permute-start.3 = (bf16[1408,256]{1,0:T(8,128)(2,1)S(1)}, bf16[1408,256]{1,0:T(8,128)(2,1)}, u32[]{:S(2)}, u32[]{:S(2)}) collective-permute-start(bf16[1408,256]{1,0:T(8,128)(2,1)S(1)} %fusion.6), channel_id=1, source_target_pairs={{0,16},{16,0},{1,17},{17,1},{2,18},{18,2},{3,19},{19,3},{4,20},{20... | collective-permute-start | bytes 2162696 | tf_op jit(solution)/shard_map/cond/branch_1_fun/ppermute | solution.py:533
  193.3 10.3 %collective-permute-start.4 = (bf16[704,256]{1,0:T(8,128)(2,1)S(1)}, bf16[704,256]{1,0:T(8,128)(2,1)S(1)}, u32[]{:S(2)}, u32[]{:S(2)}) collective-permute-start(bf16[704,256]{1,0:T(8,128)(2,1)S(1)} %constant_dynamic-slice_fusion.2), channel_id=1, source_target_pairs={{0,2},{1,3},{2,0},{3,1},{4,6},{5,7},{6,4},{7,5},{8,10},{9,11},{10,... | collective-permute-start | bytes 1081352 | tf_op jit(solution)/shard_map/cond/branch_1_fun/ppermute | solution.py:533
  203.8 5.6 %collective-permute-start.5 = (bf16[352,256]{1,0:T(8,128)(2,1)S(1)}, bf16[352,256]{1,0:T(8,128)(2,1)S(1)}, u32[]{:S(2)}, u32[]{:S(2)}) collective-permute-start(bf16[352,256]{1,0:T(8,128)(2,1)S(1)} %constant_dynamic-slice_fusion.1), channel_id=1, source_target_pairs={{0,4},{1,5},{2,6},{3,7},{4,0},{5,1},{6,2},{7,3},{8,12},{9,13},{10,... | collective-permute-start | bytes 540680 | tf_op jit(solution)/shard_map/cond/branch_1_fun/ppermute | solution.py:533
  209.4 9.3 %collective-permute-start.6 = (bf16[176,256]{1,0:T(8,128)(2,1)S(1)}, bf16[176,256]{1,0:T(8,128)(2,1)S(1)}, u32[]{:S(2)}, u32[]{:S(2)}) collective-permute-start(bf16[176,256]{1,0:T(8,128)(2,1)S(1)} %constant_dynamic-slice_fusion), channel_id=1, source_target_pairs={{0,8},{1,9},{2,10},{3,11},{4,12},{5,13},{6,14},{7,15},{8,0},{9,1},... | collective-permute-start | bytes 270344 | tf_op jit(solution)/shard_map/cond/branch_1_fun/ppermute | solution.py:533
  218.8 7.2 %collective-permute-start.7 = (bf16[176,256]{1,0:T(8,128)(2,1)S(1)}, bf16[176,256]{1,0:T(8,128)(2,1)S(1)}, u32[]{:S(2)}, u32[]{:S(2)}) collective-permute-start(bf16[176,256]{1,0:T(8,128)(2,1)S(1)} %add_convert_fusion.4), channel_id=1, source_target_pairs={{0,8},{1,9},{2,10},{3,11},{4,12},{5,13},{6,14},{7,15},{8,0},{9,1},... | collective-permute-start | bytes 270344 | tf_op jit(solution)/shard_map/cond/branch_1_fun/ppermute | solution.py:533
  226.0 5.6 %collective-permute-start.8 = (bf16[352,256]{1,0:T(8,128)(2,1)S(1)}, bf16[352,256]{1,0:T(8,128)(2,1)S(1)}, u32[]{:S(2)}, u32[]{:S(2)}) collective-permute-start(bf16[352,256]{1,0:T(8,128)(2,1)S(1)} %pad_maximum_fusion.4), channel_id=1, source_target_pairs={{0,4},{1,5},{2,6},{3,7},{4,0},{5,1},{6,2},{7,3},{8,12},{9,13},{10,... | collective-permute-start | bytes 540680 | tf_op jit(solution)/shard_map/cond/branch_1_fun/ppermute | solution.py:533
  231.7 12.7 %collective-permute-start.9 = (bf16[704,256]{1,0:T(8,128)(2,1)S(1)}, bf16[704,256]{1,0:T(8,128)(2,1)S(1)}, u32[]{:S(2)}, u32[]{:S(2)}) collective-permute-start(bf16[704,256]{1,0:T(8,128)(2,1)S(1)} %pad_maximum_fusion.3), channel_id=1, source_target_pairs={{0,2},{1,3},{2,0},{3,1},{4,6},{5,7},{6,4},{7,5},{8,10},{9,11},{10,... | collective-permute-start | bytes 1081352 | tf_op jit(solution)/shard_map/cond/branch_1_fun/ppermute | solution.py:533
  244.6 15.0 %collective-permute-start.10 = (bf16[1408,256]{1,0:T(8,128)(2,1)S(1)}, bf16[1408,256]{1,0:T(8,128)(2,1)}, u32[]{:S(2)}, u32[]{:S(2)}) collective-permute-start(bf16[1408,256]{1,0:T(8,128)(2,1)S(1)} %pad_maximum_fusion.2), channel_id=1, source_target_pairs={{0,16},{16,0},{1,17},{17,1},{2,18},{18,2},{3,19},{19,3},{4,20},{20... | collective-permute-start | bytes 2162696 | tf_op jit(solution)/shard_map/cond/branch_1_fun/ppermute | solution.py:533
  261.0 1.2 copy-start.28
  262.2 7.9 %copy-start.10 = (bf16[512,768]{1,0:T(8,128)(2,1)S(1)}, bf16[512,768]{1,0:T(8,128)(2,1)}, u32[]{:S(2)}) copy-start(bf16[512,768]{1,0:T(8,128)(2,1)} %copy-done.9) | copy-start | bytes 2359300 | tf_op jit(solution)/shard_map/cond
  262.2 9.3 %collective-permute-start.11 = (bf16[2816,256]{1,0:T(8,128)(2,1)}, bf16[2816,256]{1,0:T(8,128)(2,1)}, u32[]{:S(2)}, u32[]{:S(2)}) collective-permute-start(bf16[2816,256]{1,0:T(8,128)(2,1)} %pad_maximum_fusion.1), channel_id=1, source_target_pairs={{0,1},{1,0},{2,3},{3,2},{4,5},{5,4},{6,7},{7,6},{8,9},{9,8},{10,11... | collective-permute-start | bytes 4325384 | tf_op jit(solution)/shard_map/cond/branch_1_fun/ppermute | solution.py:533
  262.2 6.1 %collective-permute-start.12 = (f32[16,768]{1,0:T(8,128)S(1)}, f32[16,768]{1,0:T(8,128)S(1)}, u32[]{:S(2)}, u32[]{:S(2)}) collective-permute-start(f32[16,768]{1,0:T(8,128)S(1)} %copy-done.28), channel_id=1, source_target_pairs={{16,0},{17,1},{18,2},{19,3},{20,4},{21,5},{22,6},{23,7},{24,8},{25... | collective-permute-start | bytes 147464 | tf_op jit(solution)/shard_map/cond/branch_1_fun/ppermute | solution.py:675
  263.6 6.5 %copy-start.3 = (f32[512,768]{1,0:T(8,128)S(1)}, f32[512,768]{1,0:T(8,128)}, u32[]{:S(2)}) copy-start(f32[512,768]{1,0:T(8,128)} %get-tuple-element.94) | copy-start | bytes 4718596 | tf_op jit(solution)/shard_map/cond
  (2 other events, 1.7 us)
Sparse Core Ops, SparseCore 0:
  34.9 54.3 all-gather.2
  115.1 146.6 all-reduce.8

commit v2 on v1

--- a/solution.py
+++ b/solution.py
@@ -18,7 +18,7 @@
 HALO = 16
 CH = 256
 NCH = 7
-SMALL_AT = (CONV + 2) * NCH - 1
+SMALL_AT = (CONV + 1) * NCH
 SMALL = 64
 EPS = 1e-05
 LOG2E = 1.4426950408889634
@@ -300,7 +300,7 @@
     dst_o[...] = acc[...].astype(BF)
 
 
-def gate(flag, y, wrc, c, ct, st, normed, rest, tok, og, gain, rb=128):
+def gate(flag, y, wrc, c, ct, st, normed, rest, tok, og, gain, rb=256):
     T = y.shape[0]
     row = lambda n: pl.BlockSpec((rb, n), lambda i: (i, 0))
     shapes = [((T, INNER), BF), ((T, D), BF), ((T, INNER), BF), ((T, INNER), BF), ((T, D), F32), ((T, 64), F32),
@@ -461,7 +461,10 @@
         base = 4 * step + jnp.where(flag[0] == 0, 0, HEADS)
         sel = (lax.div(iota((CH, 128), 0), 64) + base == iota((CH, 128), 1)).astype(BF)
         dls[...] += nn((x32 * wq).astype(BF), sel)
-        small[pl.ds((CONV + 1) * NCH + step, 1), :] = jnp.sum(g32 * x32, axis=0, keepdims=True)
+        heads = (lax.div(iota((CH, 128), 0), 64) + 4 * step == iota((CH, 128), 1)).astype(F32)
+        both = jnp.broadcast_to(jnp.sum(g32 * x32, axis=0, keepdims=True), (8, CH))
+        both = lax.dot_general(both, heads, (((1,), (0,)), ((), ())), precision=HI, preferred_element_type=F32)
+        small[SMALL_AT + 10 : SMALL_AT + 11, 0:128] += both[0:1, :]
         total = through_conv(dx[...] + wq + skip[...] * g32)
         emit(total[HALO:], total[:HALO])
 
@@ -528,122 +531,192 @@
     )(flag, dx, g, act, z, pre, w1, conv_w, rows, dst, b, normed, nh, skip, bias, alog, rsum, csum, dbc, dcs, dlr, gn, tok, halo, ggain)
 
 
-def flip(v, axis, bit):
-    size = lax.axis_size(axis)
-    return lax.ppermute(v, axis, [(i, i ^ (1 << bit)) for i in range(size)])
-
-
-def bit_of(axis, bit):
-    return lax.rem(lax.div(lax.axis_index(axis), 1 << bit), 2)
+BOTH = ("dir", "dp")
 
 
 def width(axis):
     return lax.axis_size(axis).bit_length() - 1
 
 
+def exchange(v, mask_even, mask_odd):
+    size = lax.axis_size("dir") * lax.axis_size("dp")
+    return lax.ppermute(v, BOTH, [(i, i ^ (mask_odd if i & 1 else mask_even)) for i in range(size)])
+
+
+def side_of(mask_even, mask_odd):
+    me = lax.axis_index(BOTH)
+    return jnp.where(me % 2 == 0, me & mask_even, me & mask_odd) != 0
+
+
+def swap(v):
+    mask = lax.axis_size("dp")
+    return exchange(v, mask, mask)
+
+
 def gather_rows(shard, ready, rest):
+    bits = width("dp")
+    down = list(range(bits - 1, 0, -1))
+    even, odd = down, down[-1:] + down[:-1]
     out = shard
-    done = 0
-    for bit in reversed(range(width("dp"))):
-        other = flip(out, "dp", bit)
-        low = bit_of("dp", bit) == 0
-        out = jnp.stack([jnp.where(low, out, other), jnp.where(low, other, out)], axis=done)
-        done += 1
+    for done, (e, o) in enumerate(zip(even, odd)):
+        out = grow(out, done, e, o)
+        if done == 0:
+            out, rest = lax.optimization_barrier((out, rest))
         if done == 1:
             out, ready = lax.optimization_barrier((out, ready))
-        if done == 2:
-            out, rest = lax.optimization_barrier((out, rest))
-    return out.reshape((-1,) + shard.shape[1:]), ready, rest
-
-
-def halves(v, mine):
-    n = v.shape[0] // 2
-    return lax.dynamic_slice_in_dim(v, mine * n, n), lax.dynamic_slice_in_dim(v, (1 - mine) * n, n)
+    return gather_finish(out, shard.shape), ready, rest
+
+
+def grow(out, done, e, o):
+    other = exchange(out, 1 << e, 1 << o)
+    high = side_of(1 << e, 1 << o)
+    return jnp.stack([jnp.where(high, other, out), jnp.where(high, out, other)], axis=done)
+
+
+def gather_finish(out, shape):
+    bits = width("dp")
+    if bits == 0:
+        return out
+    other = exchange(out, 1, 1)
+    high = side_of(1, 1)
+    first = jnp.where(high, other, out)
+    second = jnp.where(high, out, other)
+    lead = max(bits - 1, 0)
+    if lead > 1:
+        second = jnp.moveaxis(second, 0, lead - 1)
+    return jnp.stack([first, second], axis=lead).reshape((-1,) + shape[1:])
+
+
+def halves(v, high, axis=0):
+    n = v.shape[axis] // 2
+    at = jnp.where(high, n, 0)
+    return lax.dynamic_slice_in_dim(v, at, n, axis), lax.dynamic_slice_in_dim(v, n - at, n, axis)
 
 
 def add(p, q):
     return (p.astype(F32) + q.astype(F32)).astype(BF)
 
 
-def reduce_all(main, small):
-    order = [("dir", 0)] + [("dp", bit) for bit in range(1, width("dp"))]
-    order = [o for o in order if o[1] < width(o[0])]
-    paired = width("dp") > 0
-    if paired:
-        mine = bit_of("dp", 0)
-        (keep, send), (keep_s, send_s) = halves(main, mine), halves(small, mine)
-        main, small = add(keep, flip(send, "dp", 0)), add(keep_s, flip(send_s, "dp", 0))
-    rows = main.shape[0]
-    buf = jnp.concatenate([main, small], axis=0)
-    for axis, bit in order:
-        keep, send = halves(buf, bit_of(axis, bit))
-        buf = add(keep, flip(send, axis, bit))
-    for axis, bit in reversed(order):
-        got = flip(buf, axis, bit)
-        low = bit_of(axis, bit) == 0
-        buf = jnp.concatenate([jnp.where(low, buf, got), jnp.where(low, got, buf)], axis=0)
-    if not paired:
-        return buf[:rows], buf[rows:]
-    got = flip(buf, "dp", 0)
-    low = bit_of("dp", 0) == 0
-    lo, hi = jnp.where(low, buf, got), jnp.where(low, got, buf)
-    return jnp.concatenate([lo[:rows], hi[:rows]], axis=0), jnp.concatenate([lo[rows:], hi[rows:]], axis=0)
-
-
-def assemble_kernel(wg, x, last, wo, small, zx_o, bc_o, dt_o, wo_o, cw_o):
+def reduce_all(main, small, beside):
+    bits = width("dp")
+    masks = [1 << b for b in [bits] * width("dir") + list(range(1, bits))]
+    odd = list(masks)
+    for i in range(0, len(masks) - 1, 2):
+        odd[i], odd[i + 1] = masks[i + 1], masks[i]
+    order = list(zip(masks, odd))
+    core = side_of(1, 1)
+    if bits:
+        (keep, send), (keep_s, send_s) = halves(main, core, 1), halves(small, core)
+        main, small = add(keep, exchange(send, 1, 1)), add(keep_s, exchange(send_s, 1, 1))
+    buf = jnp.concatenate([main.reshape(-1, CH), small], axis=0)
+    for pair in order:
+        keep, send = halves(buf, side_of(*pair))
+        buf = add(keep, exchange(send, *pair))
+    for at, pair in enumerate(reversed(order)):
+        if at == len(order) - 1:
+            buf, beside = lax.optimization_barrier((buf, beside))
+        got = exchange(buf, *pair)
+        high = side_of(*pair)
+        buf = jnp.concatenate([jnp.where(high, got, buf), jnp.where(high, buf, got)], axis=0)
+    if not bits:
+        rows = NCH * D
+        both = buf[:rows].reshape(NCH, 2, D // 2, CH)
+        parts = [jnp.concatenate([both[:, q].reshape(rows // 2, CH), buf[rows:]], axis=0) for q in range(2)]
+        return parts[0], parts[1], jnp.zeros((1,), jnp.int32), beside
+    return buf, exchange(buf, 1, 1), core.astype(jnp.int32)[None], beside
+
+
+def late_kernel(core, own, other, own_s, other_s, zx_o, bc_o, dt_o, cw_o, cb_o, dtb_o, alog_o, skip_o, og_o, ng_o):
     step = pl.program_id(0)
-    wo_o[...] = wo[...].astype(F32)
-
-    @pl.when(step < INNER // CH)
-    def _():
-        zx_o[...] = wg[...].astype(F32)
-
-    @pl.when(step >= INNER // CH)
-    def _():
-        zx_o[...] = x[0].astype(F32)
+    half = D // 2
+    first = core[0] == 0
+    upper = jnp.where(first, own[...], other[...]).astype(F32)
+    lower = jnp.where(first, other[...], own[...]).astype(F32)
+
+    @pl.when(step < NCH - 1)
+    def _():
+        zx_o[0:half, :] = upper
+        zx_o[half:, :] = lower
+
+    @pl.when(step == NCH - 1)
+    def _():
+        bc_o[0:half, :] = upper[:, :128]
+        bc_o[half:, :] = lower[:, :128]
+        dt_o[:, 0:half] = upper[:, 128:].T[: 2 * HEADS, :]
+        dt_o[:, half:] = lower[:, 128:].T[: 2 * HEADS, :]
 
     @pl.when(step == 0)
     def _():
-        tail = last[0].astype(F32)
-        bc_o[...] = tail[:, :128]
-        dt_o[...] = tail[:, 128 : 128 + 2 * HEADS]
-        sm = small[...].astype(F32)
-        for q in range(NCH - 1):
-            cw_o[:, CH * q : CH * (q + 1)] = sm[CONV * q : CONV * (q + 1), :]
-        cw_o[:, INNER:] = sm[CONV * (NCH - 1) : CONV * NCH, :128]
-
-
-def assemble(wg, main, wo, small):
+        sm = jnp.where(core[0] == 0, own_s[...], other_s[...]).astype(F32)
+        for q in range(NCH):
+            n = CH if q < NCH - 1 else 2 * STATE
+            cw_o[:, CH * q : CH * q + n] = sm[CONV * q : CONV * (q + 1), :n]
+            cb_o[CH * q : CH * q + n] = sm[CONV * NCH + q, :n]
+        at = SMALL_AT
+        dtb_o[...] = sm[at, : 2 * HEADS]
+        alog_o[...] = sm[at, 128 : 128 + 2 * HEADS]
+        for q in range(INNER // CH):
+            og_o[CH * q : CH * (q + 1)] = sm[at + 1 + q, :]
+        for q in range(D // CH):
+            ng_o[CH * q : CH * (q + 1)] = sm[at + 7 + q, :]
+        skip_o[...] = sm[at + 10, :HEADS]
+
+
+def late(core, own, other):
     n = INNER // CH
     taps = INNER + 2 * STATE
-    rb = INNER // (2 * n)
-    shapes = [(D, 2 * INNER), (D, 2 * STATE), (D, 2 * HEADS), (INNER, D), (CONV, taps)]
+    shapes = [(D, 2 * INNER), (D, 2 * STATE), (2 * HEADS, D), (CONV, taps), (taps,), (2 * HEADS,), (2 * HEADS,), (HEADS,),
+              (INNER,), (D,)]
+    half = pl.BlockSpec((D // 2, CH), lambda i: (i, 0))
+    small = pl.BlockSpec((SMALL, CH), lambda i: (NCH * D // (2 * SMALL), 0))
     return pl.pallas_call(
-        assemble_kernel,
-        grid=(2 * n,),
-        in_specs=[pl.BlockSpec((D, CH), lambda i: (0, jnp.minimum(i, n - 1))),
-                  pl.BlockSpec((1, D, CH), lambda i: (jnp.maximum(i - n, 0), 0, 0)),
-                  pl.BlockSpec((1, D, CH), lambda i: (NCH - 1, 0, 0)),
-                  pl.BlockSpec((rb, D), lambda i: (i, 0)), full(small.shape)],
-        out_specs=[pl.BlockSpec((D, CH), lambda i: (0, i)), full(shapes[1]), full(shapes[2]),
-                   pl.BlockSpec((rb, D), lambda i: (i, 0)), full(shapes[4])],
-        out_shape=[jax.ShapeDtypeStruct(s, F32) for s in shapes],
+        late_kernel,
+        grid=(NCH,),
+        in_specs=[SMEM_SPEC, half, half, small, small],
+        out_specs=[pl.BlockSpec((D, CH), lambda i: (0, n + jnp.minimum(i, n - 1)))] + [full(v) for v in shapes[1:]],
+        out_shape=[jax.ShapeDtypeStruct(v, F32) for v in shapes],
         compiler_params=params(),
-        name="assemble",
-    )(wg, main, main, wo, small)
+        name="late",
+    )(core, own, other, own, other)
+
+
+def early_kernel(wg, wo, zx, zx_o, wo_o):
+    zx_o[...] = wg[...].astype(F32)
+    wo_o[...] = wo[...].astype(F32)
+
+
+def early(wg, wo, zx):
+    n = INNER // CH
+    row = pl.BlockSpec((CH, D), lambda i: (i, 0))
+    col = pl.BlockSpec((D, CH), lambda i: (0, i))
+    return pl.pallas_call(
+        early_kernel,
+        grid=(n,),
+        in_specs=[col, row, pl.BlockSpec(memory_space=pl.ANY)],
+        out_specs=[col, row],
+        out_shape=[jax.ShapeDtypeStruct((D, 2 * INNER), F32), jax.ShapeDtypeStruct((INNER, D), F32)],
+        input_output_aliases={2: 0},
+        compiler_params=params(),
+        name="early",
+    )(wg, wo, zx)
+
+
+def apart(flag, part, args):
+    def nothing(v):
+        return jax.tree.map(lambda o: jnp.zeros(o.shape, o.dtype), jax.eval_shape(part, v))
+
+    return lax.cond(flag[1] >= 1, part, nothing, args)
 
 
 def body(tokens, norm_gain, w_zx, w_bc, w_dt, conv_w, conv_b, dt_bias, a_log, d_skip, out_gain, w_out, doc_lengths, out_grad):
     T = tokens.shape[1]
     devices = lax.axis_size("dir") * lax.axis_size("dp")
     side = lax.axis_index("dir")
-    swap = lambda v: flip(v, "dir", 0)
     tok = tokens.reshape(T, D)
     og = out_grad.reshape(T, D)
     shard = w_zx.shape[0]
     half = INNER // 2
     mine = jnp.concatenate([w_zx[:, INNER:], w_bc, w_dt, jnp.zeros((shard, 128 - 2 * HEADS), BF)], axis=1)
-    rest = jnp.concatenate([w_zx[:, :half], w_zx[:, half:INNER], w_out], axis=0)
     halo = lax.ppermute(tok[T - HALO :], "dir", [(0, 1)])
     flag = jnp.concatenate([side[None].astype(jnp.int32), doc_lengths[0]])
     wide = NCH * CH
@@ -651,55 +724,52 @@
     cb = jnp.pad(conv_b, (0, wide - conv_b.shape[0]))[None]
     lanes = lambda v: jnp.pad(v, (0, 128 - v.shape[0]))[None]
     skip = jnp.repeat(d_skip, HEADDIM)[None]
+    rest = jnp.concatenate([w_zx[:, :half], w_zx[:, half:INNER], w_out], axis=0)
     ready = (halo, flag, cw, cb, lanes(dt_bias), lanes(a_log), skip, norm_gain[None], out_gain[None])
     w1, ready, rest = gather_rows(mine, ready, rest)
-    halo, flag, cw, cb, bias, alog, skip, gain_in, gain_out = ready
-    rest = lax.all_gather(rest, "dp", axis=0, tiled=False)
-    if shard % 16:
-        rest = jnp.concatenate([rest[:, :shard].reshape(D, D), rest[:, shard : 2 * shard].reshape(D, D),
-                                rest[:, 2 * shard :].reshape(INNER, D)], axis=0)[None]
-    normed, nh, pre, z, act, rows, wrc, b, bt, c, ct, st = project(flag, tok, halo, gain_in, w1, cw, cb, bias, alog)
-    st_in = swap(st)
-    y = mix(flag, b, c, rows, act, skip)
-    no, bo, gg, gm, gn, dcs, dlr, dst, ggain = gate(flag, y, wrc, c, ct, st_in, normed, rest, tok, og, gain_out)
-    tn = lambda p, q: lax.dot_general(p, q, (((0,), (0,)), ((), ())), preferred_element_type=F32).astype(BF)
-    dwo, dwg = tn(no, og), tn(normed, gg)
-    dwo, dwg, gm = lax.optimization_barrier((dwo, dwg, gm))
-    dwo, dwg = lax.psum((dwo, dwg), ("dir", "dp"))
+
     def finish(v):
-        (flag, b, c, rows, act, gm, z, pre, w1, cw, dst, normed, nh, skip, bias, alog, dcs, dlr, gn, tok, halo, ggain, og, gain_in) = v
+        (flag, b, c, table, act, gm, z, pre, w1, cw, dst, normed, nh, skip, bias, alog, dcs, dlr, gn, tok, halo, ggain, og,
+         gain_in) = v
         dst_in = swap(dst)
-        dx, rsum, csum, dbc = unmix(flag, b, c, rows, act, gm)
-        dw1, gn, gnh, small = unproject(flag, dx, gm, act, z, pre, w1, cw, rows, dst_in, b, normed, nh, skip, bias, alog,
+        dx, rsum, csum, dbc = unmix(flag, b, c, table, act, gm)
+        dw1, gn, gnh, small = unproject(flag, dx, gm, act, z, pre, w1, cw, table, dst_in, b, normed, nh, skip, bias, alog,
                                         rsum, csum, dbc, dcs, dlr, gn, tok, halo, ggain)
         back = lax.ppermute(gnh, "dir", [(1, 0)])
-        main = dw1.reshape(NCH * D, CH)
-        total = -(-(main.shape[0] + SMALL) // (16 * devices)) * 16 * devices
-        small = jnp.pad(small, ((0, total - main.shape[0] - SMALL), (0, 0)))
-        main, small = reduce_all(main, small)
+        rows = NCH * D
+        total = -(-(rows + SMALL) // (16 * devices)) * 16 * devices
+        small = jnp.pad(small, ((0, total - rows - SMALL), (0, 0)))
         gn = gn + jnp.pad(back, ((T - HALO, 0), (0, 0)))
         x32 = tok.astype(F32)
         rho = lax.rsqrt(jnp.mean(x32 * x32, axis=1, keepdims=True) + EPS)
         e_in = gn * gain_in
         gx = rho * e_in - x32 * (rho * rho * rho * jnp.mean(e_in * x32, axis=1, keepdims=True))
         grad_tokens = (og.astype(F32) + gx).astype(BF)
-        return main, small, grad_tokens
-
-    def nothing(v):
-        return tuple(jnp.zeros(o.shape, o.dtype) for o in jax.eval_shape(finish, v))
-
-    args = (flag, b, c, rows, act, gm, z, pre, w1, cw, dst, normed, nh, skip, bias, alog, dcs, dlr, gn, tok, halo, ggain, og, gain_in)
-    main, small, grad_tokens = lax.cond(flag[1] >= 0, finish, nothing, args)
-    gw_zx, gw_bc, gw_dt, gw_out, g_cw = assemble(dwg, main.reshape(NCH, D, CH), dwo, small)
-    small = small.astype(F32)
-    g_cb = small[CONV * NCH : (CONV + 1) * NCH].reshape(wide)[: INNER + 2 * STATE]
-    g_skip = jnp.sum(small[(CONV + 1) * NCH : SMALL_AT].reshape(HEADS, HEADDIM), axis=1)
-    g_bias = small[SMALL_AT, : 2 * HEADS]
-    g_alog = small[SMALL_AT, 128 : 128 + 2 * HEADS]
-    g_out = small[SMALL_AT + 1 : SMALL_AT + 7].reshape(INNER)
-    g_in = small[SMALL_AT + 7 : SMALL_AT + 10].reshape(D)
-    return (bo.reshape(tokens.shape), grad_tokens.reshape(tokens.shape), g_in, gw_zx, gw_bc, gw_dt, g_cw, g_cb, g_bias,
-            g_alog, g_skip, g_out, gw_out)
+        own, other, core, grad_tokens = reduce_all(dw1, small, grad_tokens)
+        return (grad_tokens,) + tuple(late(core, own, other))
+
+    def rest_of(v):
+        w1, rest, (halo, flag, cw, cb, bias, alog, skip, gain_in, gain_out), tok, og = v
+        rest = lax.all_gather(rest, "dp", axis=0, tiled=False)
+        if shard % 16:
+            rest = jnp.concatenate([rest[:, :shard].reshape(D, D), rest[:, shard : 2 * shard].reshape(D, D),
+                                    rest[:, 2 * shard :].reshape(INNER, D)], axis=0)[None]
+        normed, nh, pre, z, act, rows, wrc, b, bt, c, ct, st = project(flag, tok, halo, gain_in, w1, cw, cb, bias, alog)
+        st_in = swap(st)
+        y = mix(flag, b, c, rows, act, skip)
+        no, bo, gg, gm, gn, dcs, dlr, dst, ggain = gate(flag, y, wrc, c, ct, st_in, normed, rest, tok, og, gain_out)
+        tn = lambda p, q: lax.dot_general(p, q, (((0,), (0,)), ((), ())), preferred_element_type=F32).astype(BF)
+        dwo, dwg = tn(no, og), tn(normed, gg)
+        dwo, dwg, gm = lax.optimization_barrier((dwo, dwg, gm))
+        dwo, dwg = lax.psum((dwo, dwg), BOTH)
+        args = (flag, b, c, rows, act, gm, z, pre, w1, cw, dst, normed, nh, skip, bias, alog, dcs, dlr, gn, tok, halo, ggain,
+                og, gain_in)
+        grad_tokens, zx, g_bc, g_dt, g_cw, g_cb, g_dtb, g_alog, g_skip, g_og, g_ng = apart(flag, finish, args)
+        zx, g_wo = early(dwg, dwo, zx)
+        return bo, grad_tokens, g_ng, zx, g_bc, g_dt.T, g_cw, g_cb, g_dtb, g_alog, g_skip, g_og, g_wo
+
+    outs = rest_of((w1, rest, ready, tok, og))
+    return (outs[0].reshape(tokens.shape), outs[1].reshape(tokens.shape)) + tuple(outs[2:])
 
 
 def solution(mesh):

time: 317 us -> 268 us (0.85)
  waiting for transfers between devices: 116 us -> 89.9 us
  local copies, waits for them, and re-layouts: 33.7 us -> 10.7 us
  starting transfers between devices: 21.3 us -> 31.5 us
  other arithmetic: 20.7 us -> 11.6 us
    ppermute x17, waiting for transfers between devices: 109 us -> 89.9 us  [exchange(): lax.ppermute(v, BOTH, [(i, i ^ (mask_odd if i & 1 else mask_even)) for i...]
    ppermute x17, starting transfers between devices: 16.4 us -> 26.7 us  [exchange(): lax.ppermute(v, BOTH, [(i, i ^ (mask_odd if i & 1 else mask_even)) for i...]
    slice x9 -> x1, local copies, waits for them, and re-layouts: 8.21 us -> 0.58 us  [apart(): return lax.cond(flag[1] >= 1, part, nothing, args)]
    cond x32 -> x22, local copies, waits for them, and re-layouts: 5.29 us -> 0.05 us
    reshape x4 -> x0, local copies, waits for them, and re-layouts: 5.23 us -> none  [the longest x1 1.36 us: body(): small[(CONV + 1) * NCH:SMALL_AT].reshape(HEADS, HEADDIM)]
    ppermute x1, waiting for transfers between devices: 4.66 us -> 0.01 us  [finish(): back = lax.ppermute(gnh, 'dir', [(1, 0)])]
    pallas_call x1, Pallas kernels: 18.3 us -> 14.5 us  [gate(): pl.pallas_call(functools.partial(gate_kernel, rest.shape[1] // 4), grid=(...]
    pallas_call x1 -> x2, Pallas kernels: 10.7 us -> 13.8 us  [the longest x1 6.94 us: early(): pl.pallas_call(early_kernel, grid=(n,), in_specs=[col, row, pl.BlockSpec(...]
  transfers between devices with their start and end apart: 21 -> 21, of which waited for: 14 -> 14; matrix products, arithmetic and copies ran while one was open for 16% -> 7% of each run, Pallas kernels for 23% -> 30%
where the time goes in v2:
time: 268 us; the launch traced here: 267 us
  Pallas kernels  101 us (38%)
  waiting for transfers between devices  89.9 us (34%)
  starting transfers between devices  31.5 us (12%)
  between operations  15 us (6%)
  other arithmetic  11.6 us (4%)
  local copies, waits for them, and re-layouts  10.7 us (4%)
  matrix products  7.49 us (3%)
    ppermute x17, waiting for transfers between devices, exchange(): lax.ppermute(v, BOTH, [(i, i ^ (mask_odd if i & 1 else mask_even)) for i...  89.9 us
    ppermute x17, starting transfers between devices, exchange(): lax.ppermute(v, BOTH, [(i, i ^ (mask_odd if i & 1 else mask_even)) for i...  26.7 us
    pallas_call x1, Pallas kernels, unmix(): pl.pallas_call(functools.partial(unmix_kernel, T), grid=(PAIRS,), in_spec...  23.4 us
    pallas_call x1, Pallas kernels, unproject(): pl.pallas_call(functools.partial(unproject_kernel, T), grid=(NCH,), in_sp...  22.4 us
    pallas_call x1, Pallas kernels, gate(): pl.pallas_call(functools.partial(gate_kernel, rest.shape[1] // 4), grid=(...  14.5 us
    pallas_call x1, Pallas kernels, project(): pl.pallas_call(functools.partial(project_kernel, T), grid=(NCH,), in_spec...  14.1 us
    pallas_call x1, Pallas kernels, mix(): pl.pallas_call(functools.partial(mix_kernel, T), grid=(PAIRS,), in_specs=...  12.3 us
    dot_general x2, matrix products, rest_of(): lax.dot_general(p, q, (((0,), (0,)), ((), ())), preferred_element_type=F32)  7.49 us
  transfers between devices with their start and end apart: 21, of which 14 were waited for; matrix products, arithmetic and copies ran while one was open for 7% of the time, Pallas kernels for 30%

profile of v2, /device:TPU:0, one launch (start us, length us, event | category | flops | bytes accessed | tf_op | source)
XLA Modules:
  0.0 267.0 jit_solution(7738359463411896166)
XLA Ops:
  7.2 1.0 slice.18
  8.3 0.8 concatenate.24
  9.2 4.1 %collective-permute-start.13 = (bf16[48,1792]{1,0:T(8,128)(2,1)S(1)}, bf16[48,1792]{1,0:T(8,128)(2,1)S(1)}, u32[]{:S(2)}, u32[]{:S(2)}) collective-permute-start(bf16[48,1792]{1,0:T(8,128)(2,1)S(1)} %concatenate.24), channel_id=1, source_target_pairs={{0,8},{1,3},{2,10},{3,1},{4,12},{5,7},{6,14},{7,5},{8,0},{9,11},{1... | collective-permute-start | bytes 516104 | tf_op jit(solution)/shard_map/ppermute | solution.py:543
  13.2 0.9 fusion.10
  14.2 1.6 pad_maximum_fusion.8
  15.8 2.6 collective-permute-done.13
  18.6 4.8 %collective-permute-start.14 = (bf16[2,48,1792]{2,1,0:T(8,128)(2,1)S(1)}, bf16[2,48,1792]{2,1,0:T(8,128)(2,1)S(1)}, u32[]{:S(2)}, u32[]{:S(2)}) collective-permute-start(bf16[2,48,1792]{2,1,0:T(8,128)(2,1)S(1)} %pad_maximum_fusion.7), channel_id=1, source_target_pairs={{0,4},{1,9},{2,6},{3,11},{4,0},{5,13},{6,2},{7,15},{8,12},{9,1},{1... | collective-permute-start | bytes 1032200 | tf_op jit(solution)/shard_map/ppermute | solution.py:543
  23.4 3.4 %collective-permute-start.15 = (bf16[16,768]{1,0:T(8,128)(2,1)S(1)}, bf16[16,768]{1,0:T(8,128)(2,1)S(1)}, u32[]{:S(2)}, u32[]{:S(2)}) collective-permute-start(bf16[16,768]{1,0:T(8,128)(2,1)S(1)} %slice_bitcast_fusion), channel_id=1, source_target_pairs={{0,16},{1,17},{2,18},{3,19},{4,20},{5,21},{6,22},{7,23},{8,24},{9,... | collective-permute-start | bytes 73736 | tf_op jit(solution)/shard_map/ppermute | solution.py:720
  30.6 1.8 collective-permute-start.16
  32.4 12.3 %collective-permute-done.16 = bf16[2,2,48,1792]{3,2,0,1:T(8,128)(2,1)S(1)} collective-permute-done((bf16[2,2,48,1792]{3,2,0,1:T(8,128)(2,1)S(1)}, bf16[2,2,48,1792]{3,2,0,1:T(8,128)(2,1)S(1)}, u32[]{:S(2)}, u32[]{:S(2)}) %collective-permute-start.16) | collective-permute-done | bytes 688160 | tf_op jit(solution)/shard_map/ppermute | solution.py:543
  45.0 1.2 copy.28
  46.1 3.3 %collective-permute-done.17 = bf16[2,2,2,48,1792]{4,3,2,0,1:T(8,128)(2,1)S(1)} collective-permute-done((bf16[2,2,2,48,1792]{4,3,2,0,1:T(8,128)(2,1)}, bf16[2,2,2,48,1792]{4,3,2,0,1:T(8,128)(2,1)S(1)}, u32[]{:S(2)}, u32[]{:S(2)}) %collective-permute-start.17) | collective-permute-done | bytes 1376288 | tf_op jit(solution)/shard_map/ppermute | solution.py:543
  51.0 14.1 %project.1 = (bf16[512,768]{1,0:T(8,128)(2,1)}, bf16[16,768]{1,0:T(8,128)(2,1)}, bf16[528,1792]{1,0:T(8,128)(2,1)}, bf16[512,1792]{1,0:T(8,128)(2,1)}, bf16[512,...) custom-call(s32[5]{0:T(128)S(1)} %pad_add_fusion.flag, ...), custom_call_target="tpu_custom_call" | custom-call | tf_op jit(solution)/shard_map/project/pallas_call | solution.py:185
  65.2 1.9 collective-permute-start.18
  67.1 12.3 %mix.1.y = f32[512,1536]{1,0:T(8,128)} custom-call(s32[5]{0:T(128)S(1)} %pad_add_fusion.flag, bf16[512,64]{1,0:T(8,128)(2,1)S(1)} %get-tuple-element.163.b, bf16[512,64]{1,0:T(8,128)(2,1)} %get-tuple-element.164.c, f32[12,16,512]{2,1,0:T(8,128)S(1)} %get-tuple-element.165.rows, bf16[512,1792]{1,0:T(8,128)(2,1)} %get-tuple-element.166.x, ...), custom_call_target="tpu_custom_call" | custom-call | tf_op jit(solution)/shard_map/mix/pallas_call | solution.py:238
  79.4 14.5 %gate.1 = (bf16[512,1536]{1,0:T(8,128)(2,1)}, bf16[512,768]{1,0:T(8,128)(2,1)}, bf16[512,1536]{1,0:T(8,128)(2,1)}, bf16[512,1536]{1,0:T(8,128)(2,1)}, f32[512,76...) custom-call(s32[5]{0:T(128)S(1)} %pad_add_fusion.flag, ...), custom_call_target="tpu_custom_call" | custom-call | tf_op jit(solution)/shard_map/gate/pallas_call | solution.py:308
  93.9 4.6 %convolution_convert_fusion.1 = bf16[1536,768]{1,0:T(8,128)(2,1)} fusion(bf16[512,1536]{1,0:T(8,128)(2,1)} %get-tuple-element.175, bf16[1,512,768]{2,1,0:T(8,128)(2,1)} %param.29), kind=kOutput, calls=%fused_computation.43 | convolution fusion | flops 1209139200 | bytes 4718592 | tf_op jit(solution)/shard_map/dot_general | solution.py:761
  98.5 2.9 %convolution_convert_fusion = bf16[768,1536]{1,0:T(8,128)(2,1)} fusion(bf16[512,768]{1,0:T(8,128)(2,1)S(1)} %copy-done.5, bf16[512,1536]{1,0:T(8,128)(2,1)S(1)} %copy-done.26), kind=kOutput, calls=%fused_computation.42 | convolution fusion | flops 1209139200 | bytes 4718592 | tf_op jit(solution)/shard_map/dot_general | solution.py:761
  102.7 150.5 %conditional.1 = (f32[768,3072]{1,0:T(8,128)}, f32[768,128]{1,0:T(8,128)S(1)}, f32[48,768]{1,0:T(8,128)}, f32[4,1664]{1,0:T(4,128)}, f32[1664]{0:T(1024)}, /*ind...) conditional(s32[]{:T(128)} %bitcast.22, () %tuple.24, ...), branch_computations={%region_0.1_spmd, %region_1.4_spmd} | conditional | flops 22243392 | bytes 73549432 | solution.py:708
  102.7 1.5 collective-permute-start
  104.3 23.4 %unmix.1 = (f32[512,1536]{1,0:T(8,128)}, f32[128,512]{1,0:T(8,128)}, f32[512,128]{1,0:T(8,128)}, f32[512,128]{1,0:T(8,128)}) custom-call(s32[5]{0:T(128)S(1)} %get-tuple-element.49.flag, bf16[512,64]{1,0:T(8,128)(2,1)} %get-tuple-element.50.b, bf16[512,64]{1,0:T(8,128)(2,1)} %get-tuple-element.51.c, f32[12,16,512]{2,1,0:T(8,128)} %get-tuple-element.52.rows, ...), custom_call_target="tpu_custom_call" | custom-call | tf_op jit(solution)/shard_map/cond/branch_1_fun/unmix/pallas_call | solution.py:393
  127.7 22.4 %unproject.1 = (bf16[7,768,256]{2,1,0:T(8,128)(2,1)}, f32[512,768]{1,0:T(8,128)}, f32[16,768]{1,0:T(8,128)}, bf16[64,256]{1,0:T(8,128)(2,1)}) custom-call(s32[5]{0:T(128)S(1)} %get-tuple-element.49.flag, f32[512,1536]{1,0:T(8,128)} %get-tuple-element.55.dx, bf16[512,1536]{1,0:T(8,128)(2,1)} %get-tuple-element.54.g, ...), custom_call_target="tpu_custom_call" | custom-call | tf_op jit(solution)/shard_map/cond/branch_1_fun/unproject/pallas_call | solution.py:516
  150.1 1.4 constant_dynamic-slice_fusion.3
  151.6 0.7 pad_dynamic-slice_fusion.4
  152.3 1.2 collective-permute-start.2
  153.5 1.7 collective-permute-done.2
  155.2 0.9 add_convert_fusion.5
  156.1 1.7 add_convert_fusion
  157.8 1.1 fusion.5
  159.5 12.4 %collective-permute-done.3 = bf16[1408,256]{1,0:T(8,128)(2,1)} collective-permute-done((bf16[1408,256]{1,0:T(8,128)(2,1)S(1)}, bf16[1408,256]{1,0:T(8,128)(2,1)}, u32[]{:S(2)}, u32[]{:S(2)}) %collective-permute-start.3) | collective-permute-done | bytes 720928 | tf_op jit(solution)/shard_map/cond/branch_1_fun/ppermute | solution.py:543
  171.9 1.6 add_convert_fusion.1
  174.1 7.0 %collective-permute-done.4 = bf16[704,256]{1,0:T(8,128)(2,1)} collective-permute-done((bf16[704,256]{1,0:T(8,128)(2,1)S(1)}, bf16[704,256]{1,0:T(8,128)(2,1)}, u32[]{:S(2)}, u32[]{:S(2)}) %collective-permute-start.4) | collective-permute-done | bytes 360480 | tf_op jit(solution)/shard_map/cond/branch_1_fun/ppermute | solution.py:543
  181.1 1.1 add_convert_fusion.2
  182.2 1.5 collective-permute-start.5
  183.7 5.6 %collective-permute-done.5 = bf16[352,256]{1,0:T(8,128)(2,1)S(1)} collective-permute-done((bf16[352,256]{1,0:T(8,128)(2,1)S(1)}, bf16[352,256]{1,0:T(8,128)(2,1)S(1)}, u32[]{:S(2)}, u32[]{:S(2)}) %collective-permute-start.5) | collective-permute-done | bytes 180256 | tf_op jit(solution)/shard_map/cond/branch_1_fun/ppermute | solution.py:543
  189.4 2.9 %collective-permute-start.6 = (bf16[176,256]{1,0:T(8,128)(2,1)S(1)}, bf16[176,256]{1,0:T(8,128)(2,1)S(1)}, u32[]{:S(2)}, u32[]{:S(2)}) collective-permute-start(bf16[176,256]{1,0:T(8,128)(2,1)S(1)} %constant_dynamic-slice_fusion), channel_id=1, source_target_pairs={{0,8},{1,5},{2,10},{3,7},{4,12},{5,1},{6,14},{7,3},{8,0},{9,13},{1... | collective-permute-start | bytes 270344 | tf_op jit(solution)/shard_map/cond/branch_1_fun/ppermute | solution.py:543
  192.3 3.0 %collective-permute-done.6 = bf16[176,256]{1,0:T(8,128)(2,1)S(1)} collective-permute-done((bf16[176,256]{1,0:T(8,128)(2,1)S(1)}, bf16[176,256]{1,0:T(8,128)(2,1)S(1)}, u32[]{:S(2)}, u32[]{:S(2)}) %collective-permute-start.6) | collective-permute-done | bytes 90144 | tf_op jit(solution)/shard_map/cond/branch_1_fun/ppermute | solution.py:543
  195.3 3.5 %collective-permute-start.7 = (bf16[176,256]{1,0:T(8,128)(2,1)S(1)}, bf16[176,256]{1,0:T(8,128)(2,1)S(1)}, u32[]{:S(2)}, u32[]{:S(2)}) collective-permute-start(bf16[176,256]{1,0:T(8,128)(2,1)S(1)} %add_convert_fusion.4), channel_id=1, source_target_pairs={{0,8},{1,5},{2,10},{3,7},{4,12},{5,1},{6,14},{7,3},{8,0},{9,13},{1... | collective-permute-start | bytes 270344 | tf_op jit(solution)/shard_map/cond/branch_1_fun/ppermute | solution.py:543
  198.8 1.3 collective-permute-start.10
  200.1 5.6 %collective-permute-done.7 = bf16[176,256]{1,0:T(8,128)(2,1)S(1)} collective-permute-done((bf16[176,256]{1,0:T(8,128)(2,1)S(1)}, bf16[176,256]{1,0:T(8,128)(2,1)S(1)}, u32[]{:S(2)}, u32[]{:S(2)}) %collective-permute-start.7) | collective-permute-done | bytes 90144 | tf_op jit(solution)/shard_map/cond/branch_1_fun/ppermute | solution.py:543
  205.8 1.3 collective-permute-start.8
  207.4 5.7 %collective-permute-done.8 = bf16[352,256]{1,0:T(8,128)(2,1)S(1)} collective-permute-done((bf16[352,256]{1,0:T(8,128)(2,1)S(1)}, bf16[352,256]{1,0:T(8,128)(2,1)S(1)}, u32[]{:S(2)}, u32[]{:S(2)}) %collective-permute-start.8) | collective-permute-done | bytes 180256 | tf_op jit(solution)/shard_map/cond/branch_1_fun/ppermute | solution.py:543
  213.7 1.3 fusion.4
  215.1 11.1 %collective-permute-done.9 = bf16[704,256]{1,0:T(8,128)(2,1)S(1)} collective-permute-done((bf16[704,256]{1,0:T(8,128)(2,1)S(1)}, bf16[704,256]{1,0:T(8,128)(2,1)S(1)}, u32[]{:S(2)}, u32[]{:S(2)}) %collective-permute-start.9) | collective-permute-done | bytes 360480 | tf_op jit(solution)/shard_map/cond/branch_1_fun/ppermute | solution.py:543
  226.7 15.8 %collective-permute-done.11 = bf16[1408,256]{1,0:T(8,128)(2,1)S(1)} collective-permute-done((bf16[1408,256]{1,0:T(8,128)(2,1)S(1)}, bf16[1408,256]{1,0:T(8,128)(2,1)S(1)}, u32[]{:S(2)}, u32[]{:S(2)}) %collective-permute-start.11) | collective-permute-done | bytes 720928 | tf_op jit(solution)/shard_map/cond/branch_1_fun/ppermute | solution.py:543
  242.9 3.4 %collective-permute-done.12.other.other_s = bf16[2816,256]{1,0:T(8,128)(2,1)} collective-permute-done((bf16[2816,256]{1,0:T(8,128)(2,1)S(1)}, bf16[2816,256]{1,0:T(8,128)(2,1)}, u32[]{:S(2)}, u32[]{:S(2)}) %collective-permute-start.12) | collective-permute-done | bytes 1441824 | tf_op jit(solution)/shard_map/cond/branch_1_fun/ppermute | solution.py:543
  246.3 6.9 %late.1 = (f32[768,3072]{1,0:T(8,128)}, f32[768,128]{1,0:T(8,128)S(1)}, f32[48,768]{1,0:T(8,128)}, f32[4,1664]{1,0:T(4,128)}, f32[1664]{0:T(1024)}, /*index=5*/f...) custom-call(s32[1]{0:T(128)} %bitcast.core, bf16[2816,256]{1,0:T(8,128)(2,1)} %copy-done.1, ...), custom_call_target="tpu_custom_call" | custom-call | tf_op jit(solution)/shard_map/cond/branch_1_fun/late/pallas_call | solution.py:672
  253.2 6.9 %early.1 = (f32[768,3072]{1,0:T(8,128)}, f32[1536,768]{1,0:T(8,128)}) custom-call(bf16[768,1536]{1,0:T(8,128)(2,1)} %get-tuple-element.204.wg, bf16[1536,768]{1,0:T(8,128)(2,1)} %get-tuple-element.205.wo, f32[768,3072]{1,0:T(8,128)} %get-tuple-element.191.zx), custom_call_target="tpu_custom_call", output_to_operand_aliasing={{0}: (2, {})} | custom-call | tf_op jit(solution)/shard_map/early/pallas_call | solution.py:692
  (115 shorter events, 9.7 us)
Async XLA Ops:
  7.2 16.2 %copy-start = (bf16[1,512,768]{2,1,0:T(8,128)(2,1)S(1)}, bf16[1,512,768]{2,1,0:T(8,128)(2,1)}, u32[]{:S(2)}) copy-start(bf16[1,512,768]{2,1,0:T(8,128)(2,1)} %param.16) | copy-start | bytes 2359300
  7.2 72.2 %all-gather.3.cloned.1.call-start = ((), (), s32[]{:S(2)}) async-start(), calls=%async_computation | async-start | bytes 5013504 | tf_op jit(solution)/shard_map/all_gather | solution.py:753
  8.2 18.6 %copy-start.22 = (f32[768]{0:T(1024)S(1)}, f32[768]{0:T(1024)}, u32[]{:S(2)}) copy-start(f32[768]{0:T(1024)} %param.17) | copy-start | bytes 9220
  8.2 18.6 %copy-start.15 = (f32[1536]{0:T(1024)S(1)}, f32[1536]{0:T(1024)}, u32[]{:S(2)}) copy-start(f32[1536]{0:T(1024)} %param.26) | copy-start | bytes 18436
  8.2 19.2 %copy-start.16 = (f32[1664]{0:T(1024)S(1)}, f32[1664]{0:T(1024)}, u32[]{:S(2)}) copy-start(f32[1664]{0:T(1024)} %param.22) | copy-start | bytes 19972
  8.3 19.8 %copy-start.23 = (f32[24]{0:T(128)S(1)}, f32[24]{0:T(128)}, u32[]{:S(2)}) copy-start(f32[24]{0:T(128)} %param.25) | copy-start | bytes 292
  8.3 20.0 %copy-start.14 = (f32[4,1664]{1,0:T(4,128)S(1)}, f32[4,1664]{1,0:T(4,128)}, u32[]{:S(2)}) copy-start(f32[4,1664]{1,0:T(4,128)} %param.21) | copy-start | bytes 79876
  8.3 20.6 %copy-start.28 = (s32[1,4]{1,0:T(1,128)S(1)}, s32[1,4]{1,0:T(1,128)}, u32[]{:S(2)}) copy-start(s32[1,4]{1,0:T(1,128)} %param.28) | copy-start | bytes 52
  8.3 20.6 %copy-start.24 = (f32[48]{0:T(128)S(1)}, f32[48]{0:T(128)}, u32[]{:S(2)}) copy-start(f32[48]{0:T(128)} %param.24) | copy-start | bytes 580
  8.3 20.6 %copy-start.25 = (f32[48]{0:T(128)S(1)}, f32[48]{0:T(128)}, u32[]{:S(2)}) copy-start(f32[48]{0:T(128)} %param.23) | copy-start | bytes 580
  9.2 9.3 %collective-permute-start.13 = (bf16[48,1792]{1,0:T(8,128)(2,1)S(1)}, bf16[48,1792]{1,0:T(8,128)(2,1)S(1)}, u32[]{:S(2)}, u32[]{:S(2)}) collective-permute-start(bf16[48,1792]{1,0:T(8,128)(2,1)S(1)} %concatenate.24), channel_id=1, source_target_pairs={{0,8},{1,3},{2,10},{3,1},{4,12},{5,7},{6,14},{7,5},{8,0},{9,11},{1... | collective-permute-start | bytes 516104 | tf_op jit(solution)/shard_map/ppermute | solution.py:543
  18.6 234.6 %all-reduce.9.cloned.1.call-start = ((), (), s32[]{:S(2)}) async-start(), calls=%async_computation.1 | async-start | bytes 9437184 | tf_op jit(solution)/shard_map/psum | solution.py:764
  18.6 11.3 %collective-permute-start.14 = (bf16[2,48,1792]{2,1,0:T(8,128)(2,1)S(1)}, bf16[2,48,1792]{2,1,0:T(8,128)(2,1)S(1)}, u32[]{:S(2)}, u32[]{:S(2)}) collective-permute-start(bf16[2,48,1792]{2,1,0:T(8,128)(2,1)S(1)} %pad_maximum_fusion.7), channel_id=1, source_target_pairs={{0,4},{1,9},{2,6},{3,11},{4,0},{5,13},{6,2},{7,15},{8,12},{9,1},{1... | collective-permute-start | bytes 1032200 | tf_op jit(solution)/shard_map/ppermute | solution.py:543
  23.4 6.6 %collective-permute-start.15 = (bf16[16,768]{1,0:T(8,128)(2,1)S(1)}, bf16[16,768]{1,0:T(8,128)(2,1)S(1)}, u32[]{:S(2)}, u32[]{:S(2)}) collective-permute-start(bf16[16,768]{1,0:T(8,128)(2,1)S(1)} %slice_bitcast_fusion), channel_id=1, source_target_pairs={{0,16},{1,17},{2,18},{3,19},{4,20},{5,21},{6,22},{7,23},{8,24},{9,... | collective-permute-start | bytes 73736 | tf_op jit(solution)/shard_map/ppermute | solution.py:720
  30.6 14.1 %collective-permute-start.16 = (bf16[2,2,48,1792]{3,2,0,1:T(8,128)(2,1)S(1)}, bf16[2,2,48,1792]{3,2,0,1:T(8,128)(2,1)S(1)}, u32[]{:S(2)}, u32[]{:S(2)}) collective-permute-start(bf16[2,2,48,1792]{3,2,0,1:T(8,128)(2,1)S(1)} %pad_maximum_fusion.6), channel_id=1, source_target_pairs={{0,2},{1,5},{2,0},{3,7},{4,6},{5,1},{6,4},{7,3},{8,10},{9,13},{10,... | collective-permute-start | bytes 2064392 | tf_op jit(solution)/shard_map/ppermute | solution.py:543
  46.1 3.3 %collective-permute-start.17 = (bf16[2,2,2,48,1792]{4,3,2,0,1:T(8,128)(2,1)}, bf16[2,2,2,48,1792]{4,3,2,0,1:T(8,128)(2,1)S(1)}, u32[]{:S(2)}, u32[]{:S(2)}) collective-permute-start(bf16[2,2,2,48,1792]{4,3,2,0,1:T(8,128)(2,1)} %copy.28), channel_id=1, source_target_pairs={{0,1},{1,0},{2,3},{3,2},{4,5},{5,4},{6,7},{7,6},{8,9},{9,8},{10,11... | collective-permute-start | bytes 4128776 | tf_op jit(solution)/shard_map/ppermute | solution.py:543
  50.2 0.7 copy-start.11
  50.2 0.7 copy-start.18
  65.1 14.2 %copy-start.3 = (f32[12,16,512]{2,1,0:T(8,128)}, f32[12,16,512]{2,1,0:T(8,128)S(1)}, u32[]{:S(2)}) copy-start(f32[12,16,512]{2,1,0:T(8,128)S(1)} %get-tuple-element.165.rows) | copy-start | bytes 1179652
  65.1 14.2 %copy-start.7 = (bf16[512,64]{1,0:T(8,128)(2,1)}, bf16[512,64]{1,0:T(8,128)(2,1)S(1)}, u32[]{:S(2)}) copy-start(bf16[512,64]{1,0:T(8,128)(2,1)S(1)} %get-tuple-element.163.b) | copy-start | bytes 196612
  65.2 14.2 %collective-permute-start.18 = (bf16[64,1536]{1,0:T(8,128)(2,1)}, bf16[64,1536]{1,0:T(8,128)(2,1)}, u32[]{:S(2)}, u32[]{:S(2)}) collective-permute-start(bf16[64,1536]{1,0:T(8,128)(2,1)} %get-tuple-element.170), channel_id=1, source_target_pairs={{0,16},{1,17},{2,18},{3,19},{4,20},{5,21},{6,22},{7,23},{8,24},{9,... | collective-permute-start | bytes 589832 | tf_op jit(solution)/shard_map/ppermute | solution.py:543
  93.9 4.6 %copy-start.5 = (bf16[512,768]{1,0:T(8,128)(2,1)S(1)}, bf16[512,768]{1,0:T(8,128)(2,1)}, u32[]{:S(2)}) copy-start(bf16[512,768]{1,0:T(8,128)(2,1)} %get-tuple-element.171.normed) | copy-start | bytes 2359300
  93.9 4.6 %copy-start.26 = (bf16[512,1536]{1,0:T(8,128)(2,1)S(1)}, bf16[512,1536]{1,0:T(8,128)(2,1)}, u32[]{:S(2)}) copy-start(bf16[512,1536]{1,0:T(8,128)(2,1)} %get-tuple-element.176) | copy-start | bytes 4718596
  102.7 25.0 %collective-permute-start = (bf16[64,1536]{1,0:T(8,128)(2,1)}, bf16[64,1536]{1,0:T(8,128)(2,1)}, u32[]{:S(2)}, u32[]{:S(2)}) collective-permute-start(bf16[64,1536]{1,0:T(8,128)(2,1)} %get-tuple-element.60), channel_id=1, source_target_pairs={{0,16},{1,17},{2,18},{3,19},{4,20},{5,21},{6,22},{7,23},{8,24},{9,... | collective-permute-start | bytes 589832 | tf_op jit(solution)/shard_map/cond/branch_1_fun/ppermute | solution.py:543
  104.2 23.4 %copy-start.4 = (f32[12,16,512]{2,1,0:T(8,128)S(1)}, f32[12,16,512]{2,1,0:T(8,128)}, u32[]{:S(2)}) copy-start(f32[12,16,512]{2,1,0:T(8,128)} %get-tuple-element.52.rows) | copy-start | bytes 1179652 | tf_op jit(solution)/shard_map/cond
  104.2 23.4 %copy-start.8 = (bf16[512,64]{1,0:T(8,128)(2,1)S(1)}, bf16[512,64]{1,0:T(8,128)(2,1)}, u32[]{:S(2)}) copy-start(bf16[512,64]{1,0:T(8,128)(2,1)} %get-tuple-element.50.b) | copy-start | bytes 196612 | tf_op jit(solution)/shard_map/cond
  104.2 23.5 %copy-start.12 = (f32[4,1792]{1,0:T(4,128)S(1)}, f32[4,1792]{1,0:T(4,128)}, u32[]{:S(2)}) copy-start(f32[4,1792]{1,0:T(4,128)} %get-tuple-element.59.cw) | copy-start | bytes 86020 | tf_op jit(solution)/shard_map/cond
  104.2 23.5 %copy-start.17 = (f32[1,1536]{1,0:T(1,128)S(1)}, f32[1,1536]{1,0:T(1,128)}, u32[]{:S(2)}) copy-start(f32[1,1536]{1,0:T(1,128)} %get-tuple-element.74.ggain) | copy-start | bytes 18436 | tf_op jit(solution)/shard_map/cond
  104.2 23.5 %copy-start.19 = (f32[1,128]{1,0:T(1,128)S(1)}, f32[1,128]{1,0:T(1,128)}, u32[]{:S(2)}) copy-start(f32[1,128]{1,0:T(1,128)} %get-tuple-element.65.alog) | copy-start | bytes 1540 | tf_op jit(solution)/shard_map/cond
  104.2 23.5 %copy-start.21 = (f32[1,128]{1,0:T(1,128)S(1)}, f32[1,128]{1,0:T(1,128)}, u32[]{:S(2)}) copy-start(f32[1,128]{1,0:T(1,128)} %get-tuple-element.64.bias) | copy-start | bytes 1540 | tf_op jit(solution)/shard_map/cond
  151.5 4.5 %collective-permute-start.1 = (bf16[7,384,256]{2,1,0:T(8,128)(2,1)S(1)}, bf16[7,384,256]{2,1,0:T(8,128)(2,1)S(1)}, u32[]{:S(2)}, u32[]{:S(2)}) collective-permute-start(bf16[7,384,256]{2,1,0:T(8,128)(2,1)S(1)} %constant_dynamic-slice_fusion.3), channel_id=1, source_target_pairs={{0,1},{1,0},{2,3},{3,2},{4,5},{5,4},{6,7},{7,6},{8,9},{9,8},{10,11... | collective-permute-start | bytes 4128776 | tf_op jit(solution)/shard_map/cond/branch_1_fun/ppermute | solution.py:543
  152.3 2.9 %collective-permute-start.2 = (bf16[128,256]{1,0:T(8,128)(2,1)}, bf16[128,256]{1,0:T(8,128)(2,1)}, u32[]{:S(2)}, u32[]{:S(2)}) collective-permute-start(bf16[128,256]{1,0:T(8,128)(2,1)} %pad_dynamic-slice_fusion.4), channel_id=1, source_target_pairs={{0,1},{1,0},{2,3},{3,2},{4,5},{5,4},{6,7},{7,6},{8,9},{9,8},{10,11... | collective-permute-start | bytes 196616 | tf_op jit(solution)/shard_map/cond/branch_1_fun/ppermute | solution.py:543
  156.0 1.7 copy-start.9
  158.9 13.0 %collective-permute-start.3 = (bf16[1408,256]{1,0:T(8,128)(2,1)S(1)}, bf16[1408,256]{1,0:T(8,128)(2,1)}, u32[]{:S(2)}, u32[]{:S(2)}) collective-permute-start(bf16[1408,256]{1,0:T(8,128)(2,1)S(1)} %fusion.5), channel_id=1, source_target_pairs={{0,16},{1,3},{2,18},{3,1},{4,20},{5,7},{6,22},{7,5},{8,24},{9,11},... | collective-permute-start | bytes 2162696 | tf_op jit(solution)/shard_map/cond/branch_1_fun/ppermute | solution.py:543
  173.5 25.4 %copy-start.27 = (f32[16,768]{1,0:T(8,128)S(1)}, f32[16,768]{1,0:T(8,128)}, u32[]{:S(2)}) copy-start(f32[16,768]{1,0:T(8,128)} %get-tuple-element.79) | copy-start | bytes 147460 | tf_op jit(solution)/shard_map/cond
  173.5 7.6 %collective-permute-start.4 = (bf16[704,256]{1,0:T(8,128)(2,1)S(1)}, bf16[704,256]{1,0:T(8,128)(2,1)}, u32[]{:S(2)}, u32[]{:S(2)}) collective-permute-start(bf16[704,256]{1,0:T(8,128)(2,1)S(1)} %constant_dynamic-slice_fusion.2), channel_id=1, source_target_pairs={{0,2},{1,17},{2,0},{3,19},{4,6},{5,21},{6,4},{7,23},{8,10},{9,25},... | collective-permute-start | bytes 1081352 | tf_op jit(solution)/shard_map/cond/branch_1_fun/ppermute | solution.py:543
  174.1 33.0 %copy-start.2 = (f32[512,768]{1,0:T(8,128)S(1)}, f32[512,768]{1,0:T(8,128)}, u32[]{:S(2)}) copy-start(f32[512,768]{1,0:T(8,128)} %get-tuple-element.78) | copy-start | bytes 4718596 | tf_op jit(solution)/shard_map/cond
  182.2 7.1 %collective-permute-start.5 = (bf16[352,256]{1,0:T(8,128)(2,1)S(1)}, bf16[352,256]{1,0:T(8,128)(2,1)S(1)}, u32[]{:S(2)}, u32[]{:S(2)}) collective-permute-start(bf16[352,256]{1,0:T(8,128)(2,1)S(1)} %constant_dynamic-slice_fusion.1), channel_id=1, source_target_pairs={{0,4},{1,9},{2,6},{3,11},{4,0},{5,13},{6,2},{7,15},{8,12},{9,1},{1... | collective-permute-start | bytes 540680 | tf_op jit(solution)/shard_map/cond/branch_1_fun/ppermute | solution.py:543
  189.4 5.9 %collective-permute-start.6 = (bf16[176,256]{1,0:T(8,128)(2,1)S(1)}, bf16[176,256]{1,0:T(8,128)(2,1)S(1)}, u32[]{:S(2)}, u32[]{:S(2)}) collective-permute-start(bf16[176,256]{1,0:T(8,128)(2,1)S(1)} %constant_dynamic-slice_fusion), channel_id=1, source_target_pairs={{0,8},{1,5},{2,10},{3,7},{4,12},{5,1},{6,14},{7,3},{8,0},{9,13},{1... | collective-permute-start | bytes 270344 | tf_op jit(solution)/shard_map/cond/branch_1_fun/ppermute | solution.py:543
  195.3 10.4 %collective-permute-start.7 = (bf16[176,256]{1,0:T(8,128)(2,1)S(1)}, bf16[176,256]{1,0:T(8,128)(2,1)S(1)}, u32[]{:S(2)}, u32[]{:S(2)}) collective-permute-start(bf16[176,256]{1,0:T(8,128)(2,1)S(1)} %add_convert_fusion.4), channel_id=1, source_target_pairs={{0,8},{1,5},{2,10},{3,7},{4,12},{5,1},{6,14},{7,3},{8,0},{9,13},{1... | collective-permute-start | bytes 270344 | tf_op jit(solution)/shard_map/cond/branch_1_fun/ppermute | solution.py:543
  198.8 8.2 %collective-permute-start.10 = (f32[16,768]{1,0:T(8,128)S(1)}, f32[16,768]{1,0:T(8,128)S(1)}, u32[]{:S(2)}, u32[]{:S(2)}) collective-permute-start(f32[16,768]{1,0:T(8,128)S(1)} %copy-done.27), channel_id=1, source_target_pairs={{16,0},{17,1},{18,2},{19,3},{20,4},{21,5},{22,6},{23,7},{24,8},{25... | collective-permute-start | bytes 147464 | tf_op jit(solution)/shard_map/cond/branch_1_fun/ppermute | solution.py:738
  205.8 7.3 %collective-permute-start.8 = (bf16[352,256]{1,0:T(8,128)(2,1)S(1)}, bf16[352,256]{1,0:T(8,128)(2,1)S(1)}, u32[]{:S(2)}, u32[]{:S(2)}) collective-permute-start(bf16[352,256]{1,0:T(8,128)(2,1)S(1)} %pad_maximum_fusion.3), channel_id=1, source_target_pairs={{0,4},{1,9},{2,6},{3,11},{4,0},{5,13},{6,2},{7,15},{8,12},{9,1},{1... | collective-permute-start | bytes 540680 | tf_op jit(solution)/shard_map/cond/branch_1_fun/ppermute | solution.py:543
  207.0 6.7 %copy-start.6 = (bf16[512,768]{1,0:T(8,128)(2,1)S(1)}, bf16[512,768]{1,0:T(8,128)(2,1)}, u32[]{:S(2)}) copy-start(bf16[512,768]{1,0:T(8,128)(2,1)} %get-tuple-element.77) | copy-start | bytes 2359300 | tf_op jit(solution)/shard_map/cond
  213.2 12.9 %collective-permute-start.9 = (bf16[704,256]{1,0:T(8,128)(2,1)S(1)}, bf16[704,256]{1,0:T(8,128)(2,1)S(1)}, u32[]{:S(2)}, u32[]{:S(2)}) collective-permute-start(bf16[704,256]{1,0:T(8,128)(2,1)S(1)} %pad_maximum_fusion.2), channel_id=1, source_target_pairs={{0,2},{1,17},{2,0},{3,19},{4,6},{5,21},{6,4},{7,23},{8,10},{9,25},... | collective-permute-start | bytes 1081352 | tf_op jit(solution)/shard_map/cond/branch_1_fun/ppermute | solution.py:543
  226.4 16.1 %collective-permute-start.11 = (bf16[1408,256]{1,0:T(8,128)(2,1)S(1)}, bf16[1408,256]{1,0:T(8,128)(2,1)S(1)}, u32[]{:S(2)}, u32[]{:S(2)}) collective-permute-start(bf16[1408,256]{1,0:T(8,128)(2,1)S(1)} %pad_maximum_fusion.1), channel_id=1, source_target_pairs={{0,16},{1,3},{2,18},{3,1},{4,20},{5,7},{6,22},{7,5},{8,24},{9,11},... | collective-permute-start | bytes 2162696 | tf_op jit(solution)/shard_map/cond/branch_1_fun/ppermute | solution.py:543
  242.8 3.5 %copy-start.1 = (bf16[2816,256]{1,0:T(8,128)(2,1)}, bf16[2816,256]{1,0:T(8,128)(2,1)S(1)}, u32[]{:S(2)}) copy-start(bf16[2816,256]{1,0:T(8,128)(2,1)S(1)} %pad_maximum_fusion.own.own_s) | copy-start | bytes 4325380 | tf_op jit(solution)/shard_map/cond
  242.8 3.5 %collective-permute-start.12 = (bf16[2816,256]{1,0:T(8,128)(2,1)S(1)}, bf16[2816,256]{1,0:T(8,128)(2,1)}, u32[]{:S(2)}, u32[]{:S(2)}) collective-permute-start(bf16[2816,256]{1,0:T(8,128)(2,1)S(1)} %pad_maximum_fusion.own.own_s), channel_id=1, source_target_pairs={{0,1},{1,0},{2,3},{3,2},{4,5},{5,4},{6,7},{7,6},{8,9},{9,8},{10,11... | collective-permute-start | bytes 4325384 | tf_op jit(solution)/shard_map/cond/branch_1_fun/ppermute | solution.py:543
  253.2 7.0 %copy-start.10 = (f32[768,128]{1,0:T(8,128)}, f32[768,128]{1,0:T(8,128)S(1)}, u32[]{:S(2)}) copy-start(f32[768,128]{1,0:T(8,128)S(1)} %get-tuple-element.145) | copy-start | bytes 1179652
  (2 other events, 1.3 us)
Sparse Core Ops, SparseCore 0:
  18.7 60.6 all-gather.2
  101.6 149.7 all-reduce.8

commit v3 on v2

v3 whole, which is shorter than its diff:
```python
import functools

import jax
import jax.numpy as jnp
from jax import lax
from jax.experimental import pallas as pl
from jax.experimental.pallas import tpu as pltpu
from jax.sharding import PartitionSpec as P

D = 768
HEADS = 24
HEADDIM = 64
STATE = 64
INNER = 1536
CONV = 4
NDOC = 4
PAIRS = HEADS // 2
HALO = 16
CH = 256
NCH = 7
Q = 128
GROUP = CH // HEADDIM
SMALL_AT = (CONV + 1) * NCH
SMALL = 64
EXTRA = 16
EPS = 1e-05
LOG2E = 1.4426950408889634
BF = jnp.bfloat16
F32 = jnp.float32
HI = lax.Precision.HIGHEST


def nn(a, b):
    return lax.dot_general(a, b, (((1,), (0,)), ((), ())), preferred_element_type=F32)


def nt(a, b):
    return lax.dot_general(a, b, (((1,), (1,)), ((), ())), preferred_element_type=F32)


def iota(shape, axis):
    return lax.broadcasted_iota(jnp.int32, shape, axis)


def sigm(v):
    return 1.0 / (1.0 + jnp.exp(-v))


def lane_pair(col_a, col_b, rows):
    return jnp.where(iota((rows, 128), 1) < 64, col_a, col_b)


def params(mib=60):
    return pltpu.CompilerParams(
        dimension_semantics=("arbitrary",), vmem_limit_bytes=mib * 1024 * 1024
    )


def full(shape):
    return pl.BlockSpec(shape, lambda i: tuple(0 for _ in shape))


SMEM_SPEC = pl.BlockSpec(memory_space=pltpu.SMEM)


def doc_ids(flag, places):
    total = jnp.zeros(places.shape, jnp.int32)
    end = 0
    for k in range(NDOC):
        end = end + flag[1 + k]
        total = total + jnp.where(places >= end, 1, 0)
    return jnp.where(places < 0, -1, total)


def doc_at(flag, place):
    total = 0
    end = 0
    for k in range(NDOC):
        end = end + flag[1 + k]
        total = total + jnp.where(place >= end, 1, 0)
    return total


def doc_col(flag, T, lead=0):
    return doc_ids(flag, iota((T + lead, 1), 0) + (flag[0] * T - lead))


def doc_row(flag, T):
    return doc_ids(flag, iota((1, T), 1) + flag[0] * T)


def project_kernel(T, flag, tok, halo, gain, w, cw, cb, bias, alog,
                   norm_o, normt_o, nh_o, pre_o, z_o, act_o, rows_o, wrc_o, uv_o, keep_o, b_o, bt_o, c_o, ct_o, st_o, ncat, pf, segc):
    step = pl.program_id(0)

    @pl.when(step == 0)
    def _():
        def norm(v):
            v = v.astype(F32)
            ms = jnp.mean(v * v, axis=1, keepdims=True)
            return (v * lax.rsqrt(ms + EPS) * gain[...]).astype(BF)

        nh = norm(halo[...])
        own = norm(tok[...])
        nh_o[...] = nh
        norm_o[...] = own
        normt_o[...] = own.astype(F32).T.astype(BF)
        ncat[0:HALO, :] = nh
        ncat[HALO:, :] = own
        segc[...] = doc_col(flag, T, HALO)

    proj = nn(ncat[...], w[...]).astype(BF)
    pre_o[...] = proj
    pf[...] = proj.astype(F32)
    segs = segc[...]
    here = segs[HALO:, :]
    z = cb[...] + cw[CONV - 1 : CONV, :] * pf[HALO:, :]
    for k in range(1, CONV):
        same = segs[HALO - k : HALO + T - k, :] == here
        z = z + jnp.where(same, cw[CONV - 1 - k : CONV - k, :] * pf[HALO - k : HALO + T - k, :], 0.0)
    z_o[...] = z.astype(BF)
    act = z * sigm(z)
    act_o[...] = act.astype(BF)

    @pl.when(step == 0)
    def _():
        bc = act[:, :128]
        b_o[...] = bc[:, :64].astype(BF)
        c_o[...] = bc[:, 64:].astype(BF)
        bct = bc.T
        bt_o[...] = bct[:64, :].astype(BF)
        ct_o[...] = bct[64:, :].astype(BF)
        v = pf[HALO:, 128:] + bias[...]
        dt = jnp.maximum(v, 0.0) + jnp.log1p(jnp.exp(-jnp.abs(v)))
        rate = dt * (-LOG2E * jnp.exp(alog[...]))
        rate_t = rate.T
        dt_t = dt.T
        upto = (iota((T, T), 0) <= iota((T, T), 1)).astype(F32)
        inc = lax.dot_general(rate_t, upto, (((1,), (0,)), ((), ())), precision=HI, preferred_element_type=F32)
        isf = iota((128, T), 0) < HEADS
        cum = jnp.where(isf, inc, inc - rate_t)
        ldt = jnp.log2(jnp.maximum(dt_t, 1e-37))
        key = jnp.where(isf, cum - ldt, cum + ldt)
        segv = doc_row(flag, T)
        left, right = doc_at(flag, T - 1), doc_at(flag, T)
        send_f = jnp.where(segv == left, jnp.exp2(cum[:, T - 1 :] - key), 0.0)
        send_b = jnp.where(segv == right, jnp.exp2(key), 0.0)
        recv_f = jnp.where(segv == left, jnp.exp2(cum), 0.0)
        recv_b = jnp.where(segv == right, jnp.exp2(inc[:, T - 1 :] - cum), 0.0)
        first = flag[0] == 0
        send = jnp.where(first, send_f[0:HEADS], send_b[HEADS : 2 * HEADS])
        recv = jnp.where(first, recv_b[HEADS : 2 * HEADS], recv_f[0:HEADS])
        for p in range(PAIRS):
            f, r = 2 * p, HEADS + 2 * p
            rows_o[p, 0:2, :] = cum[f : f + 2]
            rows_o[p, 2:4, :] = cum[r : r + 2]
            rows_o[p, 4:6, :] = key[f : f + 2]
            rows_o[p, 6:8, :] = key[r : r + 2]
            rows_o[p, 8:10, :] = send[f : f + 2]
            rows_o[p, 10:12, :] = recv[f : f + 2]
            rows_o[p, 12:16, :] = jnp.zeros((4, T), F32)
        recv_pad = jnp.concatenate([recv, jnp.zeros((128 - HEADS, T), F32)], axis=0)
        wrc_o[...] = recv_pad.T.astype(BF)
        cum_f, cum_r = cum[0:HEADS], cum[HEADS : 2 * HEADS]
        key_f, key_r = key[0:HEADS], key[HEADS : 2 * HEADS]
        quads = [[], [], [], []]
        none = jnp.zeros((HEADS, Q), F32)
        lane = iota((HEADS, 128), 1)
        keep_f = jnp.zeros((HEADS, 128), F32)
        keep_r = jnp.zeros((HEADS, 128), F32)
        for k in range(T // Q):
            lo, hi = k * Q, (k + 1) * Q
            sg = segv[:, lo:hi]
            before = cum_f[:, lo - 1 : lo] if k > 0 else None
            after = cum_r[:, hi : hi + 1] if hi < T else None
            quads[0].append(none if k == 0 else jnp.where(sg == segv[:, lo - 1 : lo], jnp.exp2(cum_f[:, lo:hi] - before), 0.0))
            quads[1].append(jnp.where(sg == segv[:, hi - 1 : hi], jnp.exp2(cum_f[:, hi - 1 : hi] - key_f[:, lo:hi]), 0.0))
            quads[2].append(none if hi == T else jnp.where(sg == segv[:, hi : hi + 1], jnp.exp2(after - cum_r[:, lo:hi]), 0.0))
            quads[3].append(jnp.where(sg == segv[:, lo : lo + 1], jnp.exp2(key_r[:, lo:hi] - cum_r[:, lo : lo + 1]), 0.0))
            if k > 0:
                through = jnp.where(segv[:, lo - 1 : lo] == segv[:, hi - 1 : hi], jnp.exp2(cum_f[:, hi - 1 : hi] - before), 0.0)
                keep_f = jnp.where(lane == k, through, keep_f)
            if hi < T:
                through = jnp.where(segv[:, lo : lo + 1] == segv[:, hi : hi + 1], jnp.exp2(after - cum_r[:, lo : lo + 1]), 0.0)
                keep_r = jnp.where(lane == k, through, keep_r)
        quads = [jnp.concatenate(v, axis=1) for v in quads]
        uv_o[...] = jnp.concatenate(quads + [jnp.zeros((128 - 4 * HEADS, T), F32)], axis=0).T.astype(BF)
        keeps = jnp.concatenate([keep_f, keep_r, jnp.zeros((128 - 2 * HEADS, 128), F32)], axis=0).T
        keep_o[...] = keeps[0:8, :]

    @pl.when(step > 0)
    def _():
        for j in range(CH // 128):
            cols = rows_o[2 * (step - 1) + j, 8:16, :].T
            wide = lane_pair(cols[:, 0:1], cols[:, 1:2], T)
            xw = (act[:, 128 * j : 128 * (j + 1)] * wide).astype(BF)
            st_o[:, 128 * j : 128 * (j + 1)] = nn(bt_o[...], xw).astype(BF)


def project(flag, tok, halo, gain, w1, conv_w, conv_b, bias, alog):
    T = tok.shape[0]
    E = T + HALO
    chunk = lambda i: lax.rem(i + NCH - 1, NCH)
    xchunk = lambda i: jnp.maximum(i - 1, 0)
    col = lambda rows: pl.BlockSpec((rows, CH), lambda i: (0, chunk(i)))
    shapes = [
        ((T, D), BF), ((D, T), BF), ((HALO, D), BF), ((E, NCH * CH), BF), ((T, NCH * CH), BF), ((T, NCH * CH), BF),
        ((PAIRS, 16, T), F32), ((T, 128), BF), ((T, 128), BF), ((8, 128), F32), ((T, 64), BF), ((64, T), BF), ((T, 64), BF), ((64, T), BF),
        ((64, INNER), BF),
    ]
    out_specs = [
        full((T, D)), full((D, T)), full((HALO, D)), col(E), col(T), col(T), full((PAIRS, 16, T)), full((T, 128)), full((T, 128)), full((8, 128)), full((T, 64)),
        full((64, T)), full((T, 64)), full((64, T)), pl.BlockSpec((64, CH), lambda i: (0, xchunk(i))),
    ]
    return pl.pallas_call(
        functools.partial(project_kernel, T),
        grid=(NCH,),
        in_specs=[SMEM_SPEC, full((T, D)), full((HALO, D)), full((1, D)), col(D), col(CONV), col(1),
                  full((1, 128)), full((1, 128))],
        out_specs=out_specs,
        out_shape=[jax.ShapeDtypeStruct(s, d) for s, d in shapes],
        scratch_shapes=[pltpu.VMEM((E, D), BF), pltpu.VMEM((E, CH), F32), pltpu.VMEM((E, 1), jnp.int32)],
        compiler_params=params(),
        name="project",
    )(flag, tok, halo, gain, w1, conv_w, conv_b, bias, alog)


def shift_matrix(flag, T, lo):
    first = flag[0] * T + lo
    own = doc_ids(flag, iota((Q, 1), 0) + first)
    from_doc = doc_ids(flag, iota((1, Q + HALO), 1) + (first - HALO))
    gap = iota((Q, Q + HALO), 0) + HALO - iota((Q, Q + HALO), 1)
    return jnp.concatenate([((gap == k) & (own == from_doc)).astype(F32) for k in range(1, CONV)], axis=0).astype(BF)


def shift_back_matrix(flag, T, lo):
    first = flag[0] * T + lo
    own = doc_ids(flag, iota((1, Q), 1) + first)
    from_doc = doc_ids(flag, iota((Q + HALO, 1), 0) + (first - HALO))
    gap = iota((Q + HALO, Q), 1) + HALO - iota((Q + HALO, Q), 0)
    return jnp.concatenate([((gap == k) & (own == from_doc)).astype(F32) for k in range(1, CONV)], axis=0).astype(BF)


def same_doc(flag, T, lo):
    first = flag[0] * T + lo
    a = doc_ids(flag, iota((Q, 1), 0) + first)
    b = doc_ids(flag, iota((1, Q), 1) + first)
    return (a == b) & (iota((Q, Q), 0) != iota((Q, Q), 1))


def spread_of(step, slot, dtype=BF):
    base = slot * HEADS + GROUP * step
    return (lax.div(iota((128, CH), 1), HEADDIM) + base == iota((128, CH), 0)).astype(dtype)


def exact(a, b):
    return lax.dot_general(a, b, (((1,), (0,)), ((), ())), precision=HI, preferred_element_type=F32)


def states(T, bt, vf, vr, keep_f, keep_r):
    n = T // Q
    ahead, back = [None] * n, [None] * n
    for k in range(1, n):
        new = nn(bt[:, (k - 1) * Q : k * Q], vf[(k - 1) * Q : k * Q])
        ahead[k] = new if k == 1 else new + keep_f[k - 1 : k] * ahead[k - 1]
    for k in reversed(range(n - 1)):
        new = nn(bt[:, (k + 1) * Q : (k + 2) * Q], vr[(k + 1) * Q : (k + 2) * Q])
        back[k] = new if k == n - 2 else new + keep_r[k + 1 : k + 2] * back[k + 1]
    return ahead, back


def mix_kernel(T, flag, b, bt, c, uv, keep, rows, x, skip, y_o, sc):
    step = pl.program_id(0)
    n = T // Q

    @pl.when(step == 0)
    def _():
        for i in range(n):
            lo, hi = i * Q, (i + 1) * Q
            sc[i] = jnp.where(same_doc(flag, T, lo), nt(c[lo:hi, :], b[lo:hi, :]), 0.0)

    x4 = x[...]
    x32 = x4.astype(F32)
    table = uv[...]
    uf, vf, ur, vr = [nn(table, spread_of(step, slot)) for slot in range(4)]
    keep_f = exact(keep[...], spread_of(step, 0, F32))
    keep_r = exact(keep[...], spread_of(step, 1, F32))
    ahead, back = states(T, bt, (vf * x32).astype(BF), (vr * x32).astype(BF), keep_f, keep_r)
    later = iota((Q, Q), 0) > iota((Q, Q), 1)
    lane = iota((Q, 128), 1) < HEADDIM
    cols = [rows[p][0:8].T for p in range(GROUP // 2)]
    for i in range(n):
        lo, hi = i * Q, (i + 1) * Q
        pieces = []
        for p in range(GROUP // 2):
            xs = x4[lo:hi, 128 * p : 128 * (p + 1)]
            outs = []
            for h in range(2):
                cf = cols[p][lo:hi, h : h + 1]
                cr = cols[p][lo:hi, 2 + h : 3 + h]
                kf = rows[p, 4 + h : 5 + h, lo:hi]
                kr = rows[p, 6 + h : 7 + h, lo:hi]
                m = sc[i] * jnp.exp2(jnp.where(later, cf - kf, kr - cr))
                outs.append(nn(m.astype(BF), xs))
            pieces.append(jnp.where(lane, outs[0], outs[1]))
        y = jnp.concatenate(pieces, axis=1) + skip[...] * x32[lo:hi]
        if i > 0:
            y = y + uf[lo:hi] * nn(c[lo:hi, :], ahead[i].astype(BF))
        if i < n - 1:
            y = y + ur[lo:hi] * nn(c[lo:hi, :], back[i].astype(BF))
        y_o[lo:hi, :] = y


def mix(flag, b, bt, c, uv, keep, rows, act, skip):
    T = b.shape[0]
    blk = pl.BlockSpec((T, CH), lambda i: (0, i))
    return pl.pallas_call(
        functools.partial(mix_kernel, T),
        grid=(INNER // CH,),
        in_specs=[SMEM_SPEC, full((T, 64)), full((64, T)), full((T, 64)), full((T, 128)), full((8, 128)),
                  pl.BlockSpec((GROUP // 2, 16, T), lambda i: (i, 0, 0)), blk, pl.BlockSpec((1, CH), lambda i: (0, i))],
        out_specs=blk,
        out_shape=jax.ShapeDtypeStruct((T, INNER), F32),
        scratch_shapes=[pltpu.VMEM((T // Q, Q, Q), F32)],
        compiler_params=params(),
        name="mix",
    )(flag, b, bt, c, uv, keep, rows, act, skip)


def seam_width(wrc):
    spread = (lax.div(iota((128, INNER), 1), HEADDIM) == iota((128, INNER), 0)).astype(BF)
    return nn(wrc[...], spread)


def gate_kernel(shard, y, wrc, c, st, normed, normt, rest, og, ogt, gain, no_o, gg_o, gm_o, dwg_o, dwo_o, ggain_o, acc_g, acc_o):
    step = pl.program_id(0)
    mixed = y[...] + nn(c[...], st[...]) * seam_width(wrc)
    half = INNER // 2
    own = normed[...]
    gz = jnp.concatenate([nn(own, rest[:, :shard, :].reshape(D, half)), nn(own, rest[:, shard : 2 * shard, :].reshape(D, half))],
                         axis=1)
    sig = sigm(gz)
    sil = gz * sig
    gated = mixed * sil
    rho = lax.rsqrt(jnp.mean(gated * gated, axis=1, keepdims=True) + EPS)
    no = (gated * rho * gain[...]).astype(BF)
    no_o[...] = no
    gno = nt(og[...], rest[:, 2 * shard :, :].reshape(INNER, D))
    e = gno * gain[...]
    part = jnp.sum(gno * gated * rho, axis=0, keepdims=True)
    mean_eg = jnp.mean(e * gated, axis=1, keepdims=True)
    ggated = rho * e - gated * (rho * rho * rho * mean_eg)
    gg = (ggated * mixed * sig * (1.0 + gz * (1.0 - sig))).astype(BF)
    gg_o[...] = gg
    gm_o[...] = (ggated * sil).astype(BF)
    dwg = nn(normt[...], gg)
    dwo = nn(ogt[...], no)

    @pl.when(step == 0)
    def _():
        acc_g[...] = dwg
        acc_o[...] = dwo
        ggain_o[...] = part

    @pl.when(step > 0)
    def _():
        dwg_o[...] = (acc_g[...] + dwg).astype(BF)
        dwo_o[...] = (acc_o[...] + dwo).astype(BF)
        ggain_o[...] += part


def gate(y, wrc, c, st, normed, normt, rest, og, ogt, gain):
    T = y.shape[0]
    rb = T // 2
    row = lambda n: pl.BlockSpec((rb, n), lambda i: (i, 0))
    col = lambda n: pl.BlockSpec((n, rb), lambda i: (0, i))
    shapes = [((T, INNER), BF), ((T, INNER), BF), ((T, INNER), BF), ((D, INNER), BF), ((D, INNER), BF), ((1, INNER), F32)]
    return pl.pallas_call(
        functools.partial(gate_kernel, rest.shape[1] // 4),
        grid=(2,),
        in_specs=[row(INNER), row(128), row(64), full((64, INNER)), row(D), col(D), full(rest.shape), row(D), col(D),
                  full((1, INNER))],
        out_specs=[row(INNER), row(INNER), row(INNER), full((D, INNER)), full((D, INNER)), full((1, INNER))],
        out_shape=[jax.ShapeDtypeStruct(v, d) for v, d in shapes],
        scratch_shapes=[pltpu.VMEM((D, INNER), F32), pltpu.VMEM((D, INNER), F32)],
        compiler_params=params(),
        name="gate",
    )(y, wrc, c, st, normed, normt, rest, og, ogt, gain)


def side_kernel(flag, gm, wrc, c, ct, st, dcs_o, dlr_o, dst_o, acc):
    step = pl.program_id(0)
    gw = gm[...].astype(F32) * seam_width(wrc)
    seam = gw * nn(c[...], st[...])
    gw = gw.astype(BF)
    dcs_o[...] = nt(gw, st[...])
    shift = jnp.where(flag[0] == 0, HEADS, 0)
    gather = (lax.div(iota((INNER, 128), 0), HEADDIM) + shift == iota((INNER, 128), 1)).astype(BF)
    dlr_o[...] = nn(seam.astype(BF), gather)
    dst = nn(ct[...], gw)

    @pl.when(step == 0)
    def _():
        acc[...] = dst

    @pl.when(step > 0)
    def _():
        dst_o[...] = (acc[...] + dst).astype(BF)


def aside(flag, gm, wrc, c, ct, st):
    T = gm.shape[0]
    rb = T // 2
    row = lambda n: pl.BlockSpec((rb, n), lambda i: (i, 0))
    shapes = [((T, 64), F32), ((T, 128), F32), ((64, INNER), BF)]
    return pl.pallas_call(
        side_kernel,
        grid=(2,),
        in_specs=[SMEM_SPEC, row(INNER), row(128), row(64), pl.BlockSpec((64, rb), lambda i: (0, i)), full((64, INNER))],
        out_specs=[row(64), row(128), full((64, INNER))],
        out_shape=[jax.ShapeDtypeStruct(v, d) for v, d in shapes],
        scratch_shapes=[pltpu.VMEM((64, INNER), F32)],
        compiler_params=params(),
        name="side",
    )(flag, gm, wrc, c, ct, st)


def deferred_kernel(shard, dpl, dph, w1, gg, no, rest, tok, halo, bo_o, gn_o, gnh_o, part_o, acc):
    step = pl.program_id(0)
    half = INNER // 2

    def unit(v):
        v = v.astype(F32)
        return v * lax.rsqrt(jnp.mean(v * v, axis=1, keepdims=True) + EPS)

    bo_o[...] = (tok[...].astype(F32) + nn(no[...], rest[:, 2 * shard :, :].reshape(INNER, D))).astype(BF)
    gn = nt(dpl[...], w1[...])
    gn = gn + nt(gg[:, :half], rest[:, :shard, :].reshape(D, half))
    gn = gn + nt(gg[:, half:], rest[:, shard : 2 * shard, :].reshape(D, half))
    gn_o[...] = gn
    part = jnp.sum(gn * unit(tok[...]), axis=0, keepdims=True)

    @pl.when(step == 0)
    def _():
        gnh = nt(dph[...], w1[...])
        gnh_o[...] = gnh
        acc[0:1, :] = part + jnp.sum(gnh * unit(halo[...]), axis=0, keepdims=True)

    @pl.when(step > 0)
    def _():
        total = acc[0:1, :] + part
        rows = [total[:, CH * q : CH * (q + 1)] for q in range(D // CH)]
        part_o[...] = jnp.concatenate(rows + [jnp.zeros((EXTRA - D // CH, CH), F32)], axis=0).astype(BF)


def deferred(dpl, dph, w1, gg, no, rest, tok, halo):
    T = dpl.shape[0]
    rb = T // 2
    wide = NCH * CH
    row = lambda n: pl.BlockSpec((rb, n), lambda i: (i, 0))
    shapes = [((T, D), BF), ((T, D), F32), ((HALO, D), F32), ((EXTRA, CH), BF)]
    return pl.pallas_call(
        functools.partial(deferred_kernel, rest.shape[1] // 4),
        grid=(2,),
        in_specs=[row(wide), full((HALO, wide)), full((D, wide)), row(INNER), row(INNER), full(rest.shape), row(D),
                  full((HALO, D))],
        out_specs=[row(D), row(D), full((HALO, D)), full((EXTRA, CH))],
        out_shape=[jax.ShapeDtypeStruct(v, d) for v, d in shapes],
        scratch_shapes=[pltpu.VMEM((8, D), F32)],
        compiler_params=params(),
        name="deferred",
    )(dpl, dph, w1, gg, no, rest, tok, halo)


def unmix_kernel(T, flag, b, bt, c, ct, uv, keep, rows, x, g, dx_o, rsum_o, csum_o, roff_o, coff_o, dkeep_o, dbc_o,
                 sc, dsc, db, dc):
    step = pl.program_id(0)
    n = T // Q

    @pl.when(step == 0)
    def _():
        for i in range(n):
            lo, hi = i * Q, (i + 1) * Q
            sc[i] = jnp.where(same_doc(flag, T, lo), nt(b[lo:hi, :], c[lo:hi, :]), 0.0)
        dsc[...] = jnp.zeros((n, Q, Q), F32)
        db[...] = jnp.zeros((T, 64), F32)
        dc[...] = jnp.zeros((T, 64), F32)
        rsum_o[...] = jnp.zeros((128, T), F32)
        csum_o[...] = jnp.zeros((T, 128), F32)
        roff_o[...] = jnp.zeros((T, 128), F32)
        coff_o[...] = jnp.zeros((T, 128), F32)
        dkeep_o[...] = jnp.zeros((8, 128), F32)

    x4 = x[...]
    g4 = g[...]
    x32 = x4.astype(F32)
    g32 = g4.astype(F32)
    wide = nn(uv[...], jnp.concatenate([spread_of(step, slot) for slot in range(4)], axis=1))
    uf, vf, ur, vr = [wide[:, CH * q : CH * (q + 1)] for q in range(4)]
    keep_f = exact(keep[...], spread_of(step, 0, F32))
    keep_r = exact(keep[...], spread_of(step, 1, F32))
    vxf, vxr = (vf * x32).astype(BF), (vr * x32).astype(BF)
    ugf, ugr = (uf * g32).astype(BF), (ur * g32).astype(BF)
    ahead, back = states(T, bt, vxf, vxr, keep_f, keep_r)
    lane = iota((Q, 128), 1)
    half = lane < HEADDIM
    earlier = iota((Q, Q), 0) < iota((Q, Q), 1)
    base = GROUP * step
    slot = lax.div(iota((2 * CH, 128), 0), HEADDIM)
    gather = (jnp.where(slot < GROUP, slot, slot + HEADS - GROUP) + base == iota((2 * CH, 128), 1)).astype(BF)
    cols = [rows[p][0:8].T for p in range(GROUP // 2)]
    dahead, dback = [None] * (n + 1), [None] * (n + 1)
    for k in reversed(range(1, n)):
        own = nn(ct[:, k * Q : (k + 1) * Q], ugf[k * Q : (k + 1) * Q])
        dahead[k] = own if k == n - 1 else own + keep_f[k : k + 1] * dahead[k + 1]
    for k in range(n - 1):
        own = nn(ct[:, k * Q : (k + 1) * Q], ugr[k * Q : (k + 1) * Q])
        dback[k] = own if k == 0 else own + keep_r[k : k + 1] * dback[k - 1]
    through = [jnp.zeros((1, 2 * CH), F32)] * 8
    for k in range(1, n - 1):
        pf = jnp.sum(keep_f[k : k + 1] * ahead[k] * dahead[k + 1], axis=0, keepdims=True)
        pr = jnp.sum(keep_r[k : k + 1] * back[k] * dback[k - 1], axis=0, keepdims=True)
        through[k] = jnp.concatenate([pf, pr], axis=1)
    dkeep_o[...] += nn(jnp.concatenate(through, axis=0).astype(BF), gather)
    totals = [[] for _ in range(2 * GROUP)]
    r_off, c_off = [], []
    none = jnp.zeros((Q, CH), F32)
    for j in range(n):
        lo, hi = j * Q, (j + 1) * Q
        pieces = []
        stat = jnp.zeros((Q, 128), F32)
        for p in range(GROUP // 2):
            xs = x4[lo:hi, 128 * p : 128 * (p + 1)]
            gs = g4[lo:hi, 128 * p : 128 * (p + 1)]
            zero = jnp.zeros_like(xs)
            gts = nt(jnp.concatenate([jnp.where(half, xs, zero), jnp.where(half, zero, xs)], axis=0), gs)
            ms = []
            for h in range(2):
                cf = rows[p, h : h + 1, lo:hi]
                cr = rows[p, 2 + h : 3 + h, lo:hi]
                kf = cols[p][lo:hi, 4 + h : 5 + h]
                kr = cols[p][lo:hi, 6 + h : 7 + h]
                gt = gts[h * Q : (h + 1) * Q]
                d = jnp.exp2(jnp.where(earlier, cf - kf, kr - cr))
                m = sc[j] * d
                ms.append(m.astype(BF))
                dsc[j] += gt * d
                w = gt * m
                wf = jnp.where(earlier, w, 0.0)
                wr = w - wf
                at = base + 2 * p + h
                stat = stat + jnp.where(lane == at, jnp.sum(wf, axis=1, keepdims=True), 0.0)
                stat = stat + jnp.where(lane == at + HEADS, jnp.sum(wr, axis=1, keepdims=True), 0.0)
                totals[2 * p + h].append(jnp.sum(wf, axis=0, keepdims=True))
                totals[GROUP + 2 * p + h].append(jnp.sum(wr, axis=0, keepdims=True))
            out = nn(jnp.concatenate(ms, axis=0), gs)
            pieces.append(jnp.where(half, out[:Q], out[Q:]))
        dx = jnp.concatenate(pieces, axis=1)
        zero = jnp.zeros((STATE, CH), BF)
        into = jnp.concatenate([ahead[j].astype(BF) if j > 0 else zero, back[j].astype(BF) if j < n - 1 else zero], axis=1)
        outof = jnp.concatenate([dahead[j + 1].astype(BF) if j < n - 1 else zero, dback[j - 1].astype(BF) if j > 0 else zero],
                                axis=1)
        both_u = jnp.concatenate([ugf[lo:hi], ugr[lo:hi]], axis=1)
        both_v = jnp.concatenate([vxf[lo:hi], vxr[lo:hi]], axis=1)
        r_off.append((both_u.astype(F32) * nn(c[lo:hi, :], into)).astype(BF))
        dv = nn(b[lo:hi, :], outof)
        c_off.append((both_v.astype(F32) * dv).astype(BF))
        dx_o[lo:hi, :] = dx + vf[lo:hi] * dv[:, :CH] + vr[lo:hi] * dv[:, CH:]
        dc[lo:hi, :] += nt(both_u, into)
        db[lo:hi, :] += nt(both_v, outof)
        csum_o[lo:hi, :] += stat
    off = nn(jnp.concatenate(r_off + c_off, axis=0), gather)
    roff_o[...] += off[:T]
    coff_o[...] += off[T:]
    for q in range(2):
        for h in range(GROUP):
            rsum_o[pl.ds(HEADS * q + base + h, 1), :] = jnp.concatenate(totals[GROUP * q + h], axis=1)

    @pl.when(step == INNER // CH - 1)
    def _():
        for j in range(n):
            lo, hi = j * Q, (j + 1) * Q
            ds = jnp.where(same_doc(flag, T, lo), dsc[j], 0.0)
            dbc_o[lo:hi, 0:64] = db[lo:hi, :] + nn(ds.astype(BF), c[lo:hi, :])
            dbc_o[lo:hi, 64:128] = dc[lo:hi, :] + nn(ds.T.astype(BF), b[lo:hi, :])


def unmix(flag, b, bt, c, ct, uv, keep, rows, act, g):
    T = b.shape[0]
    n = T // Q
    blk = pl.BlockSpec((T, CH), lambda i: (0, i))
    shapes = [(T, INNER), (128, T), (T, 128), (T, 128), (T, 128), (8, 128), (T, 128)]
    return pl.pallas_call(
        functools.partial(unmix_kernel, T),
        grid=(INNER // CH,),
        in_specs=[SMEM_SPEC, full((T, 64)), full((64, T)), full((T, 64)), full((64, T)), full((T, 128)), full((8, 128)),
                  pl.BlockSpec((GROUP // 2, 16, T), lambda i: (i, 0, 0)), blk, blk],
        out_specs=[blk] + [full(v) for v in shapes[1:]],
        out_shape=[jax.ShapeDtypeStruct(v, F32) for v in shapes],
        scratch_shapes=[pltpu.VMEM((n, Q, Q), F32), pltpu.VMEM((n, Q, Q), F32), pltpu.VMEM((T, 64), F32),
                        pltpu.VMEM((T, 64), F32)],
        compiler_params=params(),
        name="unmix",
    )(flag, b, bt, c, ct, uv, keep, rows, act, g)


def unproject_kernel(T, flag, dx, g, act, z, pre, cw, rows, dst, b, nt_s, nh, skip, bias, alog,
                     rsum, csum, roff, coff, dkeep, dbc, dcs, dlr, ggain,
                     dw_o, dpl_o, dph_o, small_o,
                     ht_s, tot, hd_s, dbs, dls, small, shifts, shifts_back):
    step = pl.program_id(0)
    E = T + HALO

    @pl.when(step == 0)
    def _():
        for i in range(T // Q):
            shifts[i] = shift_matrix(flag, T, i * Q)
            shifts_back[i] = shift_back_matrix(flag, T, i * Q)
        small[...] = jnp.zeros((SMALL, CH), F32)
        pad = jnp.concatenate([nh[...].astype(F32), jnp.zeros((128 - HALO, D), F32)], axis=0)
        ht_s[...] = pad.T.astype(BF)
        hd_s[...] = jnp.zeros((128, CH), BF)
        dbs[...] = jnp.zeros((T, 64), F32)
        dls[...] = jnp.zeros((T, 128), F32)

    def through_conv(dact):
        tot[...] = jnp.zeros((E, CH), F32)
        g_b = jnp.zeros((1, CH), F32)
        g_w = [jnp.zeros((1, CH), F32) for _ in range(CONV)]
        wide = Q + HALO
        for i in range(T // Q):
            lo, hi = i * Q, (i + 1) * Q
            zz = z[lo:hi, :].astype(F32)
            sg = sigm(zz)
            dz = dact[lo:hi] * sg * (1.0 + zz * (1.0 - sg))
            moved = nn(shifts[i], pre[lo : hi + HALO, :])
            back = nn(shifts_back[i], dz.astype(BF))
            g_b = g_b + jnp.sum(dz, axis=0, keepdims=True)
            g_w[0] = g_w[0] + jnp.sum(dz * pre[lo + HALO : hi + HALO, :].astype(F32), axis=0, keepdims=True)
            part = jnp.zeros((wide, CH), F32)
            for k in range(1, CONV):
                g_w[k] = g_w[k] + jnp.sum(dz * moved[(k - 1) * Q : k * Q], axis=0, keepdims=True)
                part = part + cw[CONV - 1 - k : CONV - k, :] * back[(k - 1) * wide : k * wide]
            tot[lo : hi + HALO, :] += part
            tot[lo + HALO : hi + HALO, :] += cw[CONV - 1 : CONV, :] * dz
        small[pl.ds(CONV * NCH + step, 1), :] = g_b
        for k in range(CONV):
            small[pl.ds(CONV * step + CONV - 1 - k, 1), :] = g_w[k]
        return tot[...]

    def emit(local, halo):
        local = local.astype(BF)
        hd_s[0:HALO, :] = halo.astype(BF)
        dw_o[0] = (nn(nt_s[...], local) + nn(ht_s[...], hd_s[...])).astype(BF)
        dpl_o[...] = local
        dph_o[...] = hd_s[0:HALO, :]

    @pl.when(step < NCH - 1)
    def _():
        wides = []
        for j in range(CH // 128):
            cols = rows[2 * step + j, 8:16, :].T
            wides.append(lane_pair(cols[:, 0:1], cols[:, 1:2], T))
        wide = jnp.concatenate(wides, axis=1)
        x32 = act[...].astype(F32)
        g32 = g[...].astype(F32)
        wq = wide * nn(b[...], dst[...])
        dbs[...] += nt((x32 * wide).astype(BF), dst[...])
        base = 4 * step + jnp.where(flag[0] == 0, 0, HEADS)
        sel = (lax.div(iota((CH, 128), 0), 64) + base == iota((CH, 128), 1)).astype(BF)
        dls[...] += nn((x32 * wq).astype(BF), sel)
        heads = (lax.div(iota((CH, 128), 0), 64) + 4 * step == iota((CH, 128), 1)).astype(F32)
        both = jnp.broadcast_to(jnp.sum(g32 * x32, axis=0, keepdims=True), (8, CH))
        both = lax.dot_general(both, heads, (((1,), (0,)), ((), ())), precision=HI, preferred_element_type=F32)
        small[SMALL_AT + 10 : SMALL_AT + 11, 0:128] += both[0:1, :]
        total = through_conv(dx[...] + wq + skip[...] * g32)
        emit(total[HALO:], total[:HALO])

    @pl.when(step == NCH - 1)
    def _():
        dact = dbc[...] + jnp.concatenate([dbs[...], dcs[...]], axis=1)
        total = through_conv(jnp.concatenate([dact, jnp.zeros((T, 128), F32)], axis=1))
        v = pre[HALO:, 128:].astype(F32) + bias[...]
        dt = jnp.maximum(v, 0.0) + jnp.log1p(jnp.exp(-jnp.abs(v)))
        sg = sigm(v)
        a = -jnp.exp(alog[...])
        ratio = jnp.where(v < -15.0, 1.0, sg / jnp.maximum(dt, 1e-30))
        isf = iota((T, 128), 1) < HEADS
        rs = rsum[...].T
        cs = csum[...]
        first = flag[0] == 0
        seam = dls[...] + dlr[...]
        dp = jnp.where(isf, rs - cs, cs - rs) + jnp.where(first, -1.0, 1.0) * seam
        tot = jnp.where(first, 1.0, 0.0) * jnp.sum(seam, axis=0, keepdims=True)
        inc = exact((iota((T, T), 0) <= iota((T, T), 1)).astype(F32), dp)
        dl = jnp.where(isf, inc, inc - dp) + tot
        suffix = (iota((Q, Q), 0) <= iota((Q, Q), 1)).astype(F32)
        head = iota((Q, 128), 1) < HEADS
        offs = []
        for k in range(T // Q):
            ro, co = roff[k * Q : (k + 1) * Q, :], coff[k * Q : (k + 1) * Q, :]
            sums = exact(suffix, jnp.concatenate([ro, co], axis=1))
            sr, sco = sums[:, :128], sums[:, 128:]
            fwd = sr + (sco[0:1] - sco)
            rev = (sr[0:1] - sr + ro) + (sco - co)
            offs.append(jnp.where(head, fwd, rev) + dkeep[k : k + 1, :])
        dl = dl + jnp.concatenate(offs, axis=0)
        dv = dl * a * sg + (cs + coff[...] + dls[...]) * ratio
        emit(jnp.concatenate([total[HALO:, :128], dv], axis=1), total[:HALO])

        at = SMALL_AT
        small[at : at + 1, 0:128] = jnp.sum(dv, axis=0, keepdims=True)
        small[at : at + 1, 128:] = jnp.sum(dl * dt * a, axis=0, keepdims=True)
        for q in range(INNER // CH):
            small[at + 1 + q : at + 2 + q, :] = ggain[:, CH * q : CH * (q + 1)]
        small_o[...] = small[...].astype(BF)


def unproject(flag, dx, g, act, z, pre, conv_w, rows, dst, b, normt, nh, skip, bias, alog,
              rsum, csum, roff, coff, dkeep, dbc, dcs, dlr, ggain):
    T = dx.shape[0]
    E = T + HALO
    col = lambda rows: pl.BlockSpec((rows, CH), lambda i: (0, i))
    xcol = lambda rows: pl.BlockSpec((rows, CH), lambda i: (0, jnp.minimum(i, NCH - 2)))
    shapes = [((NCH, D, CH), BF), ((T, NCH * CH), BF), ((HALO, NCH * CH), BF), ((SMALL, CH), BF)]
    return pl.pallas_call(
        functools.partial(unproject_kernel, T),
        grid=(NCH,),
        in_specs=[SMEM_SPEC, xcol(T), xcol(T), xcol(T), col(T), col(E), col(CONV), full((PAIRS, 16, T)),
                  xcol(64), full((T, 64)), full((D, T)), full((HALO, D)), xcol(1), full((1, 128)), full((1, 128)),
                  full((128, T)), full((T, 128)), full((T, 128)), full((T, 128)), full((8, 128)), full((T, 128)),
                  full((T, 64)), full((T, 128)), full((1, INNER))],
        out_specs=[pl.BlockSpec((1, D, CH), lambda i: (i, 0, 0)), col(T), col(HALO), full((SMALL, CH))],
        out_shape=[jax.ShapeDtypeStruct(s, d) for s, d in shapes],
        scratch_shapes=[pltpu.VMEM((D, 128), BF), pltpu.VMEM((E, CH), F32),
                        pltpu.VMEM((128, CH), BF), pltpu.VMEM((T, 64), F32), pltpu.VMEM((T, 128), F32),
                        pltpu.VMEM((SMALL, CH), F32), pltpu.VMEM((T // Q, (CONV - 1) * Q, Q + HALO), BF),
                        pltpu.VMEM((T // Q, (CONV - 1) * (Q + HALO), Q), BF)],
        compiler_params=params(),
        name="unproject",
    )(flag, dx, g, act, z, pre, conv_w, rows, dst, b, normt, nh, skip, bias, alog, rsum, csum, roff, coff, dkeep, dbc, dcs, dlr,
      ggain)


BOTH = ("dir", "dp")


def width(axis):
    return lax.axis_size(axis).bit_length() - 1


def exchange(v, mask_even, mask_odd):
    size = lax.axis_size("dir") * lax.axis_size("dp")
    return lax.ppermute(v, BOTH, [(i, i ^ (mask_odd if i & 1 else mask_even)) for i in range(size)])


def side_of(mask_even, mask_odd):
    me = lax.axis_index(BOTH)
    return jnp.where(me % 2 == 0, me & mask_even, me & mask_odd) != 0


def swap(v):
    mask = lax.axis_size("dp")
    return exchange(v, mask, mask)


def gather_rows(shard, ready, rest):
    bits = width("dp")
    down = list(range(bits - 1, 0, -1))
    even, odd = down, down[-1:] + down[:-1]
    out = shard
    for done, (e, o) in enumerate(zip(even, odd)):
        out = grow(out, done, e, o)
        if done == 0:
            out, rest = lax.optimization_barrier((out, rest))
        if done == 1:
            out, ready = lax.optimization_barrier((out, ready))
    return gather_finish(out, shard.shape), ready, rest


def grow(out, done, e, o):
    other = exchange(out, 1 << e, 1 << o)
    high = side_of(1 << e, 1 << o)
    return jnp.stack([jnp.where(high, other, out), jnp.where(high, out, other)], axis=done)


def gather_finish(out, shape):
    bits = width("dp")
    if bits == 0:
        return out
    other = exchange(out, 1, 1)
    high = side_of(1, 1)
    first = jnp.where(high, other, out)
    second = jnp.where(high, out, other)
    lead = max(bits - 1, 0)
    if lead > 1:
        second = jnp.moveaxis(second, 0, lead - 1)
    return jnp.stack([first, second], axis=lead).reshape((-1,) + shape[1:])


def halves(v, high, axis=0):
    n = v.shape[axis] // 2
    at = jnp.where(high, n, 0)
    return lax.dynamic_slice_in_dim(v, at, n, axis), lax.dynamic_slice_in_dim(v, n - at, n, axis)


def add(p, q):
    return (p.astype(F32) + q.astype(F32)).astype(BF)


def reduce_all(main, small, later, inputs):
    bits = width("dp")
    masks = [1 << b for b in [bits] * width("dir") + list(range(1, bits))]
    odd = list(masks)
    for i in range(0, len(masks) - 1, 2):
        odd[i], odd[i + 1] = masks[i + 1], masks[i]
    order = list(zip(masks, odd))
    core = side_of(1, 1)
    if bits:
        (keep, send), (keep_s, send_s) = halves(main, core, 1), halves(small, core)
        main, small = add(keep, exchange(send, 1, 1)), add(keep_s, exchange(send_s, 1, 1))
    buf = jnp.concatenate([main.reshape(-1, CH), small], axis=0)
    if order:
        keep, send = halves(buf, side_of(*order[0]))
        send, inputs = lax.optimization_barrier((send, inputs))
        got = exchange(send, *order[0])
    extra, beside = later(*inputs)
    if order:
        for at, pair in enumerate(order[1:]):
            high = side_of(*pair)
            (keep, send), (got, got_send) = halves(keep, high), halves(got, high)
            send = add(send, got_send)
            if at == 0:
                send, extra = lax.optimization_barrier((send, extra))
            keep, got = add(keep, got), exchange(send, *pair)
        buf = add(keep, got)
    for at, pair in enumerate(reversed(order)):
        n = buf.shape[0]
        if at == len(order) - 1:
            buf, beside = lax.optimization_barrier((buf, beside))
        got = exchange(jnp.concatenate([buf, extra], axis=0), *pair)
        extra = add(extra, got[n:])
        high = side_of(*pair)
        buf = jnp.concatenate([jnp.where(high, got[:n], buf), jnp.where(high, buf, got[:n])], axis=0)
    if not bits:
        rows = NCH * D
        both = buf[:rows].reshape(NCH, 2, D // 2, CH)
        parts = [jnp.concatenate([both[:, q].reshape(rows // 2, CH), buf[rows : rows + (buf.shape[0] - rows) // 2], e], axis=0)
                 for q, e in ((0, extra), (1, jnp.zeros_like(extra)))]
        return parts[0], parts[1], jnp.zeros((1,), jnp.int32), beside
    buf = jnp.concatenate([buf, extra], axis=0)
    return buf, exchange(buf, 1, 1), core.astype(jnp.int32)[None], beside


def late_kernel(core, own, other, own_l, other_l, own_s, other_s, own_e, other_e, zx_o, bc_o, dt_o, cw_o, cb_o, dtb_o, alog_o,
                skip_o, og_o, ng_o):
    half = D // 2
    first = core[0] == 0
    upper = jnp.where(first, own[...], other[...]).astype(F32)
    lower = jnp.where(first, other[...], own[...]).astype(F32)
    for q in range(2):
        zx_o[0:half, CH * q : CH * (q + 1)] = upper[half * q : half * (q + 1)]
        zx_o[half:, CH * q : CH * (q + 1)] = lower[half * q : half * (q + 1)]

    @pl.when(pl.program_id(0) == 0)
    def _():
        tail = jnp.concatenate([jnp.where(first, own_l[...], other_l[...]), jnp.where(first, other_l[...], own_l[...])], axis=0)
        tail = tail.astype(F32)
        bc_o[...] = tail[:, :128]
        dt_o[...] = tail[:, 128:].T[: 2 * HEADS, :]
        sm = jnp.where(first, own_s[...], other_s[...]).astype(F32)
        for q in range(NCH):
            n = CH if q < NCH - 1 else 2 * STATE
            cw_o[:, CH * q : CH * q + n] = sm[CONV * q : CONV * (q + 1), :n]
            cb_o[CH * q : CH * q + n] = sm[CONV * NCH + q, :n]
        at = SMALL_AT
        dtb_o[...] = sm[at, : 2 * HEADS]
        alog_o[...] = sm[at, 128 : 128 + 2 * HEADS]
        for q in range(INNER // CH):
            og_o[CH * q : CH * (q + 1)] = sm[at + 1 + q, :]
        ng = own_e[...].astype(F32) + other_e[...].astype(F32)
        for q in range(D // CH):
            ng_o[CH * q : CH * (q + 1)] = ng[q, :]
        skip_o[...] = sm[at + 10, :HEADS]


def late(core, own, other):
    n = INNER // CH // 2
    taps = INNER + 2 * STATE
    shapes = [(D, 2 * INNER), (D, 2 * STATE), (2 * HEADS, D), (CONV, taps), (taps,), (2 * HEADS,), (2 * HEADS,), (HEADS,),
              (INNER,), (D,)]
    two = pl.BlockSpec((D, CH), lambda i: (i, 0))
    last = pl.BlockSpec((D // 2, CH), lambda i: (NCH - 1, 0))
    small = pl.BlockSpec((SMALL, CH), lambda i: (NCH * D // (2 * SMALL), 0))
    end = own.shape[0] // EXTRA - 1
    extra = pl.BlockSpec((EXTRA, CH), lambda i: (end, 0))
    return pl.pallas_call(
        late_kernel,
        grid=(n,),
        in_specs=[SMEM_SPEC, two, two, last, last, small, small, extra, extra],
        out_specs=[pl.BlockSpec((D, 2 * CH), lambda i: (0, n + i))] + [full(v) for v in shapes[1:]],
        out_shape=[jax.ShapeDtypeStruct(v, F32) for v in shapes],
        compiler_params=params(),
        name="late",
    )(core, own, other, own, other, own, other, own, other)


def early_kernel(wg, wo, zx, zx_o, wo_o):
    zx_o[...] = wg[...].astype(F32)
    wo_o[...] = wo[...].astype(F32).T


def early(wg, wo, zx):
    n = INNER // CH // 2
    row = pl.BlockSpec((2 * CH, D), lambda i: (i, 0))
    col = pl.BlockSpec((D, 2 * CH), lambda i: (0, i))
    return pl.pallas_call(
        early_kernel,
        grid=(n,),
        in_specs=[col, col, pl.BlockSpec(memory_space=pl.ANY)],
        out_specs=[col, row],
        out_shape=[jax.ShapeDtypeStruct((D, 2 * INNER), F32), jax.ShapeDtypeStruct((INNER, D), F32)],
        input_output_aliases={2: 0},
        compiler_params=params(),
        name="early",
    )(wg, wo, zx)


def apart(flag, part, args):
    def nothing(v):
        return jax.tree.map(lambda o: jnp.zeros(o.shape, o.dtype), jax.eval_shape(part, v))

    return lax.cond(flag[1] >= 1, part, nothing, args)


def body(tokens, norm_gain, w_zx, w_bc, w_dt, conv_w, conv_b, dt_bias, a_log, d_skip, out_gain, w_out, doc_lengths, out_grad):
    T = tokens.shape[1]
    devices = lax.axis_size("dir") * lax.axis_size("dp")
    side = lax.axis_index("dir")
    tok = tokens.reshape(T, D)
    og = out_grad.reshape(T, D)
    shard = w_zx.shape[0]
    half = INNER // 2
    mine = jnp.concatenate([w_zx[:, INNER:], w_bc, w_dt, jnp.zeros((shard, 128 - 2 * HEADS), BF)], axis=1)
    halo = lax.ppermute(tok[T - HALO :], "dir", [(0, 1)])
    flag = jnp.concatenate([side[None].astype(jnp.int32), doc_lengths[0]])
    wide = NCH * CH
    cw = jnp.pad(conv_w, ((0, 0), (0, wide - conv_w.shape[1])))
    cb = jnp.pad(conv_b, (0, wide - conv_b.shape[0]))[None]
    lanes = lambda v: jnp.pad(v, (0, 128 - v.shape[0]))[None]
    skip = jnp.repeat(d_skip, HEADDIM)[None]
    rest = jnp.concatenate([w_zx[:, :half], w_zx[:, half:INNER], w_out], axis=0)
    ready = (halo, flag, cw, cb, lanes(dt_bias), lanes(a_log), skip, norm_gain[None], out_gain[None], og.T)
    w1, ready, rest = gather_rows(mine, ready, rest)

    def finish(v):
        (flag, b, bt, c, ct, uv, keep, table, act, gm, z, pre, w1, cw, normt, nh, skip, bias, alog, tok, halo, ggain, og, gain_in,
         no, gg, wrc, st_in, rest) = v
        dcs, dlr, dst = aside(flag, gm, wrc, c, ct, st_in)
        dst_in = swap(dst)
        dx, rsum, csum, roff, coff, dkeep, dbc = unmix(flag, b, bt, c, ct, uv, keep, table, act, gm)
        dw1, dpl, dph, small = unproject(flag, dx, gm, act, z, pre, cw, table, dst_in, b, normt, nh, skip, bias, alog,
                                         rsum, csum, roff, coff, dkeep, dbc, dcs, dlr, ggain)
        rows = NCH * D
        total = -(-(rows + SMALL) // (16 * devices)) * 16 * devices
        small = jnp.pad(small, ((0, total - rows - SMALL), (0, 0)))

        def later(dpl, dph):
            bo, gn, gnh, part = deferred(dpl, dph, w1, gg, no, rest, tok, halo)
            back = lax.ppermute(gnh, "dir", [(1, 0)])
            gn = gn + jnp.pad(back, ((T - HALO, 0), (0, 0)))
            x32 = tok.astype(F32)
            rho = lax.rsqrt(jnp.mean(x32 * x32, axis=1, keepdims=True) + EPS)
            e_in = gn * gain_in
            gx = rho * e_in - x32 * (rho * rho * rho * jnp.mean(e_in * x32, axis=1, keepdims=True))
            return part, (bo, (og.astype(F32) + gx).astype(BF))

        own, other, core, (bo, grad_tokens) = reduce_all(dw1, small, later, (dpl, dph))
        return (bo, grad_tokens) + tuple(late(core, own, other))

    def rest_of(v):
        w1, rest, (halo, flag, cw, cb, bias, alog, skip, gain_in, gain_out, ogt), tok, og = v
        rest = lax.all_gather(rest, "dp", axis=0, tiled=False)
        if shard % 16:
            rest = jnp.concatenate([rest[:, :shard].reshape(D, D), rest[:, shard : 2 * shard].reshape(D, D),
                                    rest[:, 2 * shard :].reshape(INNER, D)], axis=0)[None]
        normed, normt, nh, pre, z, act, rows, wrc, uv, keep, b, bt, c, ct, st = project(
            flag, tok, halo, gain_in, w1, cw, cb, bias, alog)
        st_in = swap(st)
        y = mix(flag, b, bt, c, uv, keep, rows, act, skip)
        no, gg, gm, dwg, dwo, ggain = gate(y, wrc, c, st_in, normed, normt, rest, og, ogt, gain_out)
        dwo, dwg = lax.psum((dwo, dwg), BOTH)
        args = (flag, b, bt, c, ct, uv, keep, rows, act, gm, z, pre, w1, cw, normt, nh, skip, bias, alog, tok, halo, ggain, og,
                gain_in, no, gg, wrc, st_in, rest)
        bo, grad_tokens, zx, g_bc, g_dt, g_cw, g_cb, g_dtb, g_alog, g_skip, g_og, g_ng = apart(flag, finish, args)
        zx, g_wo = early(dwg, dwo, zx)
        return bo, grad_tokens, g_ng, zx, g_bc, g_dt.T, g_cw, g_cb, g_dtb, g_alog, g_skip, g_og, g_wo

    outs = rest_of((w1, rest, ready, tok, og))
    return (outs[0].reshape(tokens.shape), outs[1].reshape(tokens.shape)) + tuple(outs[2:])


def solution(mesh):
    rows, weight, whole = P("dp", "dir", None), P("dp", None), P()
    placed = (rows, whole, weight, weight, weight, whole, whole, whole, whole, whole, whole, weight, weight, rows)
    return jax.shard_map(body, mesh=mesh, in_specs=placed, out_specs=(rows, rows) + (whole,) * 11, check_vma=False)
```

time: 268 us -> 263 us (0.981)
  matrix products: 7.49 us -> 0 us
  other arithmetic: 11.6 us -> 17.4 us
  local copies, waits for them, and re-layouts: 10.7 us -> 16.4 us
  starting transfers between devices: 31.5 us -> 26.3 us
  waiting for transfers between devices: 89.9 us -> 85.6 us
    dot_general x2 -> x0, matrix products: 7.49 us -> none  [rest_of(): lax.dot_general(p, q, (((0,), (0,)), ((), ())), preferred_element_type=F32)]
    ppermute x17, waiting for transfers between devices: 89.9 us -> 82.8 us  [exchange(): lax.ppermute(v, BOTH, [(i, i ^ (mask_odd if i & 1 else mask_even)) for i...]
    ppermute x17, starting transfers between devices: 26.7 us -> 21 us  [exchange(): lax.ppermute(v, BOTH, [(i, i ^ (mask_odd if i & 1 else mask_even)) for i...]
    pallas_call x1, Pallas kernels: 22.4 us -> 18 us  [unproject(): pl.pallas_call(functools.partial(unproject_kernel, T), grid=(NCH,), in_sp...]
    convert_element_type x6 -> x10, other arithmetic: 5.28 us -> 8.8 us  [add(): return (p.astype(F32) + q.astype(F32)).astype(BF)]
    pallas_call x4 -> x6, Pallas kernels: 49.5 us -> 52.8 us  [the longest x1 18.8 us: unmix(): pl.pallas_call(functools.partial(unmix_kernel, T), grid=(INNER // CH,), i...]
    all_gather x1, waiting for transfers between devices: 0.02 us -> 2.74 us  [rest_of(): rest = lax.all_gather(rest, 'dp', axis=0, tiled=False)]
  transfers between devices with their start and end apart: 21 -> 21, of which waited for: 14 -> 14; matrix products, arithmetic and copies ran while one was open for 7% -> 11% of each run, Pallas kernels for 30% -> 30%
where the time goes in v3:
time: 263 us; the launch traced here: 262 us
  Pallas kernels  101 us (38%)
  waiting for transfers between devices  85.6 us (33%)
  starting transfers between devices  26.3 us (10%)
  other arithmetic  17.4 us (7%)
  local copies, waits for them, and re-layouts  16.4 us (6%)
  between operations  15 us (6%)
    ppermute x17, waiting for transfers between devices, exchange(): lax.ppermute(v, BOTH, [(i, i ^ (mask_odd if i & 1 else mask_even)) for i...  82.8 us
    ppermute x17, starting transfers between devices, exchange(): lax.ppermute(v, BOTH, [(i, i ^ (mask_odd if i & 1 else mask_even)) for i...  21 us
    pallas_call x1, Pallas kernels, unmix(): pl.pallas_call(functools.partial(unmix_kernel, T), grid=(INNER // CH,), i...  18.8 us
    pallas_call x1, Pallas kernels, unproject(): pl.pallas_call(functools.partial(unproject_kernel, T), grid=(NCH,), in_sp...  18 us
    pallas_call x1, Pallas kernels, gate(): pl.pallas_call(functools.partial(gate_kernel, rest.shape[1] // 4), grid=(...  15.7 us
    pallas_call x1, Pallas kernels, project(): pl.pallas_call(functools.partial(project_kernel, T), grid=(NCH,), in_spec...  14.5 us
    pallas_call x1, Pallas kernels, deferred(): pl.pallas_call(functools.partial(deferred_kernel, rest.shape[1] // 4), gr...  9.48 us
    pallas_call x1, Pallas kernels, mix(): pl.pallas_call(functools.partial(mix_kernel, T), grid=(INNER // CH,), in_...  9.13 us
  transfers between devices with their start and end apart: 21, of which 14 were waited for; matrix products, arithmetic and copies ran while one was open for 11% of the time, Pallas kernels for 30%

profile of v3, /device:TPU:0, one launch (start us, length us, event | category | flops | bytes accessed | tf_op | source)
XLA Modules:
  0.0 262.3 jit_solution(6846663316414013529)
XLA Ops:
  7.2 1.0 slice.46
  9.2 4.1 %collective-permute-start.13 = (bf16[48,1792]{1,0:T(8,128)(2,1)S(1)}, bf16[48,1792]{1,0:T(8,128)(2,1)S(1)}, u32[]{:S(2)}, u32[]{:S(2)}) collective-permute-start(bf16[48,1792]{1,0:T(8,128)(2,1)S(1)} %concatenate.38), channel_id=1, source_target_pairs={{0,8},{1,3},{2,10},{3,1},{4,12},{5,7},{6,14},{7,5},{8,0},{9,11},{1... | collective-permute-start | bytes 516104 | tf_op jit(solution)/shard_map/ppermute | solution.py:754
  14.2 1.6 pad_maximum_fusion.12
  15.9 2.6 %collective-permute-done.13 = bf16[48,1792]{1,0:T(8,128)(2,1)S(1)} collective-permute-done((bf16[48,1792]{1,0:T(8,128)(2,1)S(1)}, bf16[48,1792]{1,0:T(8,128)(2,1)S(1)}, u32[]{:S(2)}, u32[]{:S(2)}) %collective-permute-start.13) | collective-permute-done | bytes 172064 | tf_op jit(solution)/shard_map/ppermute | solution.py:754
  18.7 4.8 %collective-permute-start.14 = (bf16[2,48,1792]{2,1,0:T(8,128)(2,1)S(1)}, bf16[2,48,1792]{2,1,0:T(8,128)(2,1)S(1)}, u32[]{:S(2)}, u32[]{:S(2)}) collective-permute-start(bf16[2,48,1792]{2,1,0:T(8,128)(2,1)S(1)} %pad_maximum_fusion.11), channel_id=1, source_target_pairs={{0,4},{1,9},{2,6},{3,11},{4,0},{5,13},{6,2},{7,15},{8,12},{9,1},{1... | collective-permute-start | bytes 1032200 | tf_op jit(solution)/shard_map/ppermute | solution.py:754
  24.1 4.0 %collective-permute-start.15 = (bf16[16,768]{1,0:T(8,128)(2,1)}, bf16[16,768]{1,0:T(8,128)(2,1)}, u32[]{:S(2)}, u32[]{:S(2)}) collective-permute-start(bf16[16,768]{1,0:T(8,128)(2,1)} %slice_bitcast_fusion), channel_id=1, source_target_pairs={{0,16},{1,17},{2,18},{3,19},{4,20},{5,21},{6,22},{7,23},{8,24},{9,... | collective-permute-start | bytes 73736 | tf_op jit(solution)/shard_map/ppermute | solution.py:945
  30.1 1.2 copy.28
  32.5 1.6 collective-permute-start.16
  34.1 11.2 %collective-permute-done.16 = bf16[2,2,48,1792]{3,2,0,1:T(8,128)(2,1)S(1)} collective-permute-done((bf16[2,2,48,1792]{3,2,0,1:T(8,128)(2,1)S(1)}, bf16[2,2,48,1792]{3,2,0,1:T(8,128)(2,1)S(1)}, u32[]{:S(2)}, u32[]{:S(2)}) %collective-permute-start.16) | collective-permute-done | bytes 688160 | tf_op jit(solution)/shard_map/ppermute | solution.py:754
  45.5 1.2 copy.29
  46.7 3.3 %collective-permute-done.17 = bf16[2,2,2,48,1792]{4,3,2,0,1:T(8,128)(2,1)S(1)} collective-permute-done((bf16[2,2,2,48,1792]{4,3,2,0,1:T(8,128)(2,1)}, bf16[2,2,2,48,1792]{4,3,2,0,1:T(8,128)(2,1)S(1)}, u32[]{:S(2)}, u32[]{:S(2)}) %collective-permute-start.17) | collective-permute-done | bytes 1376288 | tf_op jit(solution)/shard_map/ppermute | solution.py:754
  51.6 14.5 %project.1 = (bf16[512,768]{1,0:T(8,128)(2,1)}, bf16[768,512]{1,0:T(8,128)(2,1)}, bf16[16,768]{1,0:T(8,128)(2,1)}, bf16[528,1792]{1,0:T(8,128)(2,1)}, bf16[512,1...) custom-call(s32[5]{0:T(128)S(1)} %copy-done.18, ...), custom_call_target="tpu_custom_call" | custom-call | tf_op jit(solution)/shard_map/project/pallas_call | solution.py:215
  66.1 1.4 collective-permute-start.18
  67.5 9.1 %mix.1.y = f32[512,1536]{1,0:T(8,128)} custom-call(s32[5]{0:T(128)S(1)} %copy-done.18, bf16[512,64]{1,0:T(8,128)(2,1)} %get-tuple-element.195.b, bf16[64,512]{1,0:T(8,128)(2,1)} %get-tuple-element.196.bt, bf16[512,64]{1,0:T(8,128)(2,1)S(1)} %get-tuple-element.197.c, bf16[512,128]{1,0:T(8,128)(2,1)} %get-tuple-element.199.uv, ...), custom_call_target="tpu_custom_call" | custom-call | tf_op jit(solution)/shard_map/mix/pallas_call | solution.py:317
  76.6 2.7 %all-gather.3.cloned.1.call-done = bf16[3072,768]{1,0:T(8,128)(2,1)} async-done(((bf16[192,768]{1,0:T(8,128)(2,1)}), bf16[3072,768]{1,0:T(8,128)(2,1)}) %all-gather.3.cloned.1.call-update) | async-done | bytes 4718608 | tf_op jit(solution)/shard_map/all_gather | solution.py:983
  79.4 15.7 %gate.1 = (bf16[512,1536]{1,0:T(8,128)(2,1)}, bf16[512,1536]{1,0:T(8,128)(2,1)}, bf16[512,1536]{1,0:T(8,128)(2,1)}, bf16[768,1536]{1,0:T(8,128)(2,1)}, bf16[768,1536]{1,0:T(8,128)(2,1)}, /*index=5*/f32[1,1536]{1,0:T(1,128)}) custom-call(f32[512,1536]{1,0:T(8,128)} %mix.1.y, bf16[512,128]{1,0:T(8,128)(2,1)} %get-tuple-element.204.wrc, ...), custom_call_target="tpu_custom_call" | custom-call | tf_op jit(solution)/shard_map/gate/pallas_call | solution.py:378
  95.1 1.2 slice.51
  96.9 152.1 %conditional.1 = (f32[768,3072]{1,0:T(8,128)}, f32[768,128]{1,0:T(8,128)}, f32[48,768]{1,0:T(8,128)}, f32[4,1664]{1,0:T(4,128)}, f32[1664]{0:T(1024)}, /*index=5...) conditional(s32[]{:T(128)} %bitcast.15, () %tuple.27, ...), branch_computations={%region_0.1_spmd, %region_1.4_spmd} | conditional | flops 26019908 | bytes 85444528 | solution.py:933
  97.1 4.3 %side.1 = (f32[512,64]{1,0:T(8,128)}, f32[512,128]{1,0:T(8,128)}, bf16[64,1536]{1,0:T(8,128)(2,1)}) custom-call(s32[5]{0:T(128)} %get-tuple-element.60.flag, bf16[512,1536]{1,0:T(8,128)(2,1)} %get-tuple-element.69.g.gm, bf16[512,128]{1,0:T(8,128)(2,1)} %get-tuple-element.74.wrc, bf16[512,64]{1,0:T(8,128)(2,1)} %get-tuple-element.63.c, ...), custom_call_target="tpu_custom_call" | custom-call | tf_op jit(solution)/shard_map/cond/branch_1_fun/side/pallas_call | solution.py:416
  101.4 1.5 collective-permute-start
  103.0 18.8 %unmix.1 = (f32[512,1536]{1,0:T(8,128)}, f32[128,512]{1,0:T(8,128)}, f32[512,128]{1,0:T(8,128)}, f32[512,128]{1,0:T(8,128)}, f32[512,128]{1,0:T(8,128)}, /*index=5*/f32[8,128]{1,0:T(8,128)}, f32[512,128]{1,0:T(8,128)}) custom-call(s32[5]{0:T(128)} %get-tuple-element.60.flag, bf16[512,64]{1,0:T(8,128)(2,1)} %get-tuple-element.61.b, ...), custom_call_target="tpu_custom_call" | custom-call | tf_op jit(solution)/shard_map/cond/branch_1_fun/unmix/pallas_call | solution.py:593
  121.8 18.0 %unproject.1 = (bf16[7,768,256]{2,1,0:T(8,128)(2,1)}, bf16[512,1792]{1,0:T(8,128)(2,1)}, bf16[16,1792]{1,0:T(8,128)(2,1)}, bf16[64,256]{1,0:T(8,128)(2,1)}) custom-call(s32[5]{0:T(128)S(1)} %copy-done.19, f32[512,1536]{1,0:T(8,128)} %get-tuple-element.70.dx, bf16[512,1536]{1,0:T(8,128)(2,1)} %get-tuple-element.69.g.gm, ...), custom_call_target="tpu_custom_call" | custom-call | tf_op jit(solution)/shard_map/cond/branch_1_fun/unproject/pallas_call | solution.py:726
  139.8 2.5 constant_dynamic-slice_fusion
  143.1 1.1 collective-permute-start.2
  144.3 1.7 collective-permute-done.2
  146.8 3.3 %add_convert_fusion = bf16[7,384,256]{2,1,0:T(8,128)(2,1)} fusion(bf16[7,384,256]{2,1,0:T(8,128)(2,1)} %collective-permute-done.1, bf16[7,768,256]{2,1,0:T(8,128)(2,1)} %get-tuple-element.91, s32[]{:T(128)S(6)} %select_n.175), kind=kLoop, calls=%fused_computation | loop fusion | flops 2752512 | bytes 4128772 | tf_op jit(solution)/shard_map/cond/branch_1_fun/convert_element_type | solution.py:808
  150.1 2.9 %fusion.5 = bf16[1408,256]{1,0:T(8,128)(2,1)} fusion(s32[]{:T(128)S(6)} %select_n.183, bf16[2688,256]{1,0:T(8,128)(2,1)} %bitcast.1, bf16[128,256]{1,0:T(8,128)(2,1)S(1)} %add_convert_fusion.8), kind=kLoop, calls=%fused_computation.18 | loop fusion | flops 1441792 | bytes 2162692 | tf_op jit(solution)/shard_map/cond/branch_1_fun/concatenate | solution.py:822
  153.6 9.5 %deferred.1 = (bf16[512,768]{1,0:T(8,128)(2,1)}, f32[512,768]{1,0:T(8,128)}, f32[16,768]{1,0:T(8,128)}, bf16[16,256]{1,0:T(8,128)(2,1)}) custom-call(bf16[512,1792]{1,0:T(8,128)(2,1)} %get-tuple-element.96.dpl, bf16[16,1792]{1,0:T(8,128)(2,1)} %get-tuple-element.97.dph, bf16[768,1792]{1,0:T(8,128)(2,1)S(1)} %get-tuple-element.98.w1, ...), custom_call_target="tpu_custom_call" | custom-call | tf_op jit(solution)/shard_map/cond/branch_1_fun/deferred/pallas_call | solution.py:462
  163.1 1.9 collective-permute-done.3
  165.0 2.6 add_convert_fusion.2
  167.6 1.5 collective-permute-start.4
  169.1 6.3 %collective-permute-done.4 = bf16[704,256]{1,0:T(8,128)(2,1)S(1)} collective-permute-done((bf16[704,256]{1,0:T(8,128)(2,1)S(1)}, bf16[704,256]{1,0:T(8,128)(2,1)S(1)}, u32[]{:S(2)}, u32[]{:S(2)}) %collective-permute-start.4) | collective-permute-done | bytes 360480 | tf_op jit(solution)/shard_map/cond/branch_1_fun/ppermute | solution.py:754
  175.5 1.6 collective-permute-start.5
  177.1 6.2 %collective-permute-done.5 = bf16[352,256]{1,0:T(8,128)(2,1)S(1)} collective-permute-done((bf16[352,256]{1,0:T(8,128)(2,1)S(1)}, bf16[352,256]{1,0:T(8,128)(2,1)S(1)}, u32[]{:S(2)}, u32[]{:S(2)}) %collective-permute-start.5) | collective-permute-done | bytes 180256 | tf_op jit(solution)/shard_map/cond/branch_1_fun/ppermute | solution.py:754
  184.0 1.0 add_convert_fusion.6
  185.0 1.0 collective-permute-start.6
  186.0 5.4 %collective-permute-done.6 = bf16[176,256]{1,0:T(8,128)(2,1)S(1)} collective-permute-done((bf16[176,256]{1,0:T(8,128)(2,1)S(1)}, bf16[176,256]{1,0:T(8,128)(2,1)S(1)}, u32[]{:S(2)}, u32[]{:S(2)}) %collective-permute-start.6) | collective-permute-done | bytes 90144 | tf_op jit(solution)/shard_map/cond/branch_1_fun/ppermute | solution.py:754
  192.4 1.2 copy.35
  193.6 1.3 collective-permute-start.10
  194.9 9.8 %collective-permute-done.7 = bf16[192,256]{1,0:T(8,128)(2,1)S(1)} collective-permute-done((bf16[192,256]{1,0:T(8,128)(2,1)S(1)}, bf16[192,256]{1,0:T(8,128)(2,1)S(1)}, u32[]{:S(2)}, u32[]{:S(2)}) %collective-permute-start.7) | collective-permute-done | bytes 98336 | tf_op jit(solution)/shard_map/cond/branch_1_fun/ppermute | solution.py:754
  205.3 5.1 %collective-permute-done.8 = bf16[368,256]{1,0:T(8,128)(2,1)S(1)} collective-permute-done((bf16[368,256]{1,0:T(8,128)(2,1)S(1)}, bf16[368,256]{1,0:T(8,128)(2,1)S(1)}, u32[]{:S(2)}, u32[]{:S(2)}) %collective-permute-start.8) | collective-permute-done | bytes 188448 | tf_op jit(solution)/shard_map/cond/branch_1_fun/ppermute | solution.py:754
  211.3 1.3 fusion.4
  212.7 13.3 %collective-permute-done.9 = bf16[720,256]{1,0:T(8,128)(2,1)S(1)} collective-permute-done((bf16[720,256]{1,0:T(8,128)(2,1)S(1)}, bf16[720,256]{1,0:T(8,128)(2,1)S(1)}, u32[]{:S(2)}, u32[]{:S(2)}) %collective-permute-start.9) | collective-permute-done | bytes 368672 | tf_op jit(solution)/shard_map/cond/branch_1_fun/ppermute | solution.py:754
  227.0 12.6 %collective-permute-done.11 = bf16[1424,256]{1,0:T(8,128)(2,1)S(1)} collective-permute-done((bf16[1424,256]{1,0:T(8,128)(2,1)S(1)}, bf16[1424,256]{1,0:T(8,128)(2,1)S(1)}, u32[]{:S(2)}, u32[]{:S(2)}) %collective-permute-start.11) | collective-permute-done | bytes 729120 | tf_op jit(solution)/shard_map/cond/branch_1_fun/ppermute | solution.py:754
  239.9 3.2 %collective-permute-done.12.other.other_l.other_s.other_e = bf16[2832,256]{1,0:T(8,128)(2,1)S(1)} collective-permute-done((bf16[2832,256]{1,0:T(8,128)(2,1)S(1)}, bf16[2832,256]{1,0:T(8,128)(2,1)S(1)}, u32[]{:S(2)}, u32[]{:S(2)}) %collective-permute-start.12) | collective-permute-done | bytes 1450016 | tf_op jit(solution)/shard_map/cond/branch_1_fun/ppermute | solution.py:754
  243.1 1.1 copy-done.1
  244.2 4.8 %late.1 = (f32[768,3072]{1,0:T(8,128)}, f32[768,128]{1,0:T(8,128)}, f32[48,768]{1,0:T(8,128)}, f32[4,1664]{1,0:T(4,128)}, f32[1664]{0:T(1024)}, /*index=5*/f32[4...) custom-call(s32[1]{0:T(128)} %bitcast.core, bf16[2832,256]{1,0:T(8,128)(2,1)} %copy-done, ...), custom_call_target="tpu_custom_call" | custom-call | tf_op jit(solution)/shard_map/cond/branch_1_fun/late/pallas_call | solution.py:897
  249.1 6.3 %early.1 = (f32[768,3072]{1,0:T(8,128)}, f32[1536,768]{1,0:T(8,128)}) custom-call(bf16[768,1536]{1,0:T(8,128)(2,1)} %get-tuple-element.265.wg, bf16[768,1536]{1,0:T(8,128)(2,1)} %get-tuple-element.266.wo, f32[768,3072]{1,0:T(8,128)} %get-tuple-element.223.zx), custom_call_target="tpu_custom_call", output_to_operand_aliasing={{0}: (2, {})} | custom-call | tf_op jit(solution)/shard_map/early/pallas_call | solution.py:917
  (126 shorter events, 14.3 us)
Async XLA Ops:
  7.2 16.3 %copy-start.2 = (bf16[1,512,768]{2,1,0:T(8,128)(2,1)S(1)}, bf16[1,512,768]{2,1,0:T(8,128)(2,1)}, u32[]{:S(2)}) copy-start(bf16[1,512,768]{2,1,0:T(8,128)(2,1)} %param.16) | copy-start | bytes 2359300
  7.2 72.2 %all-gather.3.cloned.1.call-start = ((), (), s32[]{:S(2)}) async-start(), calls=%async_computation | async-start | bytes 5013504 | tf_op jit(solution)/shard_map/all_gather | solution.py:983
  8.2 19.9 %copy-start.27 = (f32[768]{0:T(1024)S(1)}, f32[768]{0:T(1024)}, u32[]{:S(2)}) copy-start(f32[768]{0:T(1024)} %param.17) | copy-start | bytes 9220
  8.2 19.8 %copy-start.20 = (f32[1536]{0:T(1024)S(1)}, f32[1536]{0:T(1024)}, u32[]{:S(2)}) copy-start(f32[1536]{0:T(1024)} %param.26) | copy-start | bytes 18436
  8.2 20.4 %copy-start.21 = (f32[1664]{0:T(1024)S(1)}, f32[1664]{0:T(1024)}, u32[]{:S(2)}) copy-start(f32[1664]{0:T(1024)} %param.22) | copy-start | bytes 19972
  8.3 21.0 %copy-start.28 = (f32[24]{0:T(128)S(1)}, f32[24]{0:T(128)}, u32[]{:S(2)}) copy-start(f32[24]{0:T(128)} %param.25) | copy-start | bytes 292
  8.3 21.2 %copy-start.17 = (f32[4,1664]{1,0:T(4,128)S(1)}, f32[4,1664]{1,0:T(4,128)}, u32[]{:S(2)}) copy-start(f32[4,1664]{1,0:T(4,128)} %param.21) | copy-start | bytes 79876
  8.3 21.8 %copy-start.7 = (bf16[1,512,768]{2,1,0:T(8,128)(2,1)S(1)}, bf16[1,512,768]{2,1,0:T(8,128)(2,1)}, u32[]{:S(2)}) copy-start(bf16[1,512,768]{2,1,0:T(8,128)(2,1)} %param.29) | copy-start | bytes 2359300
  9.2 9.3 %collective-permute-start.13 = (bf16[48,1792]{1,0:T(8,128)(2,1)S(1)}, bf16[48,1792]{1,0:T(8,128)(2,1)S(1)}, u32[]{:S(2)}, u32[]{:S(2)}) collective-permute-start(bf16[48,1792]{1,0:T(8,128)(2,1)S(1)} %concatenate.38), channel_id=1, source_target_pairs={{0,8},{1,3},{2,10},{3,1},{4,12},{5,7},{6,14},{7,5},{8,0},{9,11},{1... | collective-permute-start | bytes 516104 | tf_op jit(solution)/shard_map/ppermute | solution.py:754
  15.9 15.4 %copy-start.31 = (s32[1,4]{1,0:T(1,128)S(1)}, s32[1,4]{1,0:T(1,128)}, u32[]{:S(2)}) copy-start(s32[1,4]{1,0:T(1,128)} %param.28) | copy-start | bytes 52
  15.9 16.0 %copy-start.29 = (f32[48]{0:T(128)S(1)}, f32[48]{0:T(128)}, u32[]{:S(2)}) copy-start(f32[48]{0:T(128)} %param.24) | copy-start | bytes 580
  15.9 16.0 %copy-start.30 = (f32[48]{0:T(128)S(1)}, f32[48]{0:T(128)}, u32[]{:S(2)}) copy-start(f32[48]{0:T(128)} %param.23) | copy-start | bytes 580
  18.6 230.5 %all-reduce.9.cloned.1.call-start = ((), (), s32[]{:S(2)}) async-start(), calls=%async_computation.1 | async-start | bytes 9437184 | tf_op jit(solution)/shard_map/psum | solution.py:992
  18.7 13.7 %collective-permute-start.14 = (bf16[2,48,1792]{2,1,0:T(8,128)(2,1)S(1)}, bf16[2,48,1792]{2,1,0:T(8,128)(2,1)S(1)}, u32[]{:S(2)}, u32[]{:S(2)}) collective-permute-start(bf16[2,48,1792]{2,1,0:T(8,128)(2,1)S(1)} %pad_maximum_fusion.11), channel_id=1, source_target_pairs={{0,4},{1,9},{2,6},{3,11},{4,0},{5,13},{6,2},{7,15},{8,12},{9,1},{1... | collective-permute-start | bytes 1032200 | tf_op jit(solution)/shard_map/ppermute | solution.py:754
  24.1 8.5 %collective-permute-start.15 = (bf16[16,768]{1,0:T(8,128)(2,1)}, bf16[16,768]{1,0:T(8,128)(2,1)}, u32[]{:S(2)}, u32[]{:S(2)}) collective-permute-start(bf16[16,768]{1,0:T(8,128)(2,1)} %slice_bitcast_fusion), channel_id=1, source_target_pairs={{0,16},{1,17},{2,18},{3,19},{4,20},{5,21},{6,22},{7,23},{8,24},{9,... | collective-permute-start | bytes 73736 | tf_op jit(solution)/shard_map/ppermute | solution.py:945
  32.5 12.8 %collective-permute-start.16 = (bf16[2,2,48,1792]{3,2,0,1:T(8,128)(2,1)S(1)}, bf16[2,2,48,1792]{3,2,0,1:T(8,128)(2,1)S(1)}, u32[]{:S(2)}, u32[]{:S(2)}) collective-permute-start(bf16[2,2,48,1792]{3,2,0,1:T(8,128)(2,1)S(1)} %pad_maximum_fusion.10), channel_id=1, source_target_pairs={{0,2},{1,5},{2,0},{3,7},{4,6},{5,1},{6,4},{7,3},{8,10},{9,13},{10,... | collective-permute-start | bytes 2064392 | tf_op jit(solution)/shard_map/ppermute | solution.py:754
  46.7 3.3 %collective-permute-start.17 = (bf16[2,2,2,48,1792]{4,3,2,0,1:T(8,128)(2,1)}, bf16[2,2,2,48,1792]{4,3,2,0,1:T(8,128)(2,1)S(1)}, u32[]{:S(2)}, u32[]{:S(2)}) collective-permute-start(bf16[2,2,2,48,1792]{4,3,2,0,1:T(8,128)(2,1)} %copy.29), channel_id=1, source_target_pairs={{0,1},{1,0},{2,3},{3,2},{4,5},{5,4},{6,7},{7,6},{8,9},{9,8},{10,11... | collective-permute-start | bytes 4128776 | tf_op jit(solution)/shard_map/ppermute | solution.py:754
  66.1 10.5 %copy-start.5 = (f32[12,16,512]{2,1,0:T(8,128)}, f32[12,16,512]{2,1,0:T(8,128)S(1)}, u32[]{:S(2)}) copy-start(f32[12,16,512]{2,1,0:T(8,128)S(1)} %get-tuple-element.201.rows) | copy-start | bytes 1179652
  66.1 10.5 %copy-start.9 = (bf16[512,64]{1,0:T(8,128)(2,1)}, bf16[512,64]{1,0:T(8,128)(2,1)S(1)}, u32[]{:S(2)}) copy-start(bf16[512,64]{1,0:T(8,128)(2,1)S(1)} %get-tuple-element.197.c) | copy-start | bytes 196612
  66.1 10.5 %collective-permute-start.18 = (bf16[64,1536]{1,0:T(8,128)(2,1)}, bf16[64,1536]{1,0:T(8,128)(2,1)}, u32[]{:S(2)}, u32[]{:S(2)}) collective-permute-start(bf16[64,1536]{1,0:T(8,128)(2,1)} %get-tuple-element.205), channel_id=1, source_target_pairs={{0,16},{1,17},{2,18},{3,19},{4,20},{5,21},{6,22},{7,23},{8,24},{9,... | collective-permute-start | bytes 589832 | tf_op jit(solution)/shard_map/ppermute | solution.py:754
  101.4 20.4 %collective-permute-start = (bf16[64,1536]{1,0:T(8,128)(2,1)}, bf16[64,1536]{1,0:T(8,128)(2,1)}, u32[]{:S(2)}, u32[]{:S(2)}) collective-permute-start(bf16[64,1536]{1,0:T(8,128)(2,1)} %get-tuple-element.76), channel_id=1, source_target_pairs={{0,16},{1,17},{2,18},{3,19},{4,20},{5,21},{6,22},{7,23},{8,24},{9,... | collective-permute-start | bytes 589832 | tf_op jit(solution)/shard_map/cond/branch_1_fun/ppermute | solution.py:754
  102.9 18.8 %copy-start.6 = (f32[12,16,512]{2,1,0:T(8,128)S(1)}, f32[12,16,512]{2,1,0:T(8,128)}, u32[]{:S(2)}) copy-start(f32[12,16,512]{2,1,0:T(8,128)} %get-tuple-element.67.rows) | copy-start | bytes 1179652 | tf_op jit(solution)/shard_map/cond
  102.9 18.8 %copy-start.10 = (bf16[512,64]{1,0:T(8,128)(2,1)S(1)}, bf16[512,64]{1,0:T(8,128)(2,1)}, u32[]{:S(2)}) copy-start(bf16[512,64]{1,0:T(8,128)(2,1)} %get-tuple-element.61.b) | copy-start | bytes 196612 | tf_op jit(solution)/shard_map/cond
  102.9 18.8 %copy-start.14 = (f32[4,1792]{1,0:T(4,128)S(1)}, f32[4,1792]{1,0:T(4,128)}, u32[]{:S(2)}) copy-start(f32[4,1792]{1,0:T(4,128)} %get-tuple-element.73.cw) | copy-start | bytes 86020 | tf_op jit(solution)/shard_map/cond
  102.9 18.9 %copy-start.19 = (s32[5]{0:T(128)S(1)}, s32[5]{0:T(128)}, u32[]{:S(2)}) copy-start(s32[5]{0:T(128)} %get-tuple-element.60.flag) | copy-start | bytes 64 | tf_op jit(solution)/shard_map/cond
  102.9 18.9 %copy-start.22 = (f32[1,1536]{1,0:T(1,128)S(1)}, f32[1,1536]{1,0:T(1,128)}, u32[]{:S(2)}) copy-start(f32[1,1536]{1,0:T(1,128)} %get-tuple-element.90.ggain) | copy-start | bytes 18436 | tf_op jit(solution)/shard_map/cond
  102.9 18.9 %copy-start.24 = (f32[1,128]{1,0:T(1,128)S(1)}, f32[1,128]{1,0:T(1,128)}, u32[]{:S(2)}) copy-start(f32[1,128]{1,0:T(1,128)} %get-tuple-element.81.alog) | copy-start | bytes 1540 | tf_op jit(solution)/shard_map/cond
  102.9 18.9 %copy-start.26 = (f32[1,128]{1,0:T(1,128)S(1)}, f32[1,128]{1,0:T(1,128)}, u32[]{:S(2)}) copy-start(f32[1,128]{1,0:T(1,128)} %get-tuple-element.80.bias) | copy-start | bytes 1540 | tf_op jit(solution)/shard_map/cond
  142.4 4.4 %collective-permute-start.1 = (bf16[7,384,256]{2,1,0:T(8,128)(2,1)}, bf16[7,384,256]{2,1,0:T(8,128)(2,1)}, u32[]{:S(2)}, u32[]{:S(2)}) collective-permute-start(bf16[7,384,256]{2,1,0:T(8,128)(2,1)} %constant_dynamic-slice_fusion), channel_id=1, source_target_pairs={{0,1},{1,0},{2,3},{3,2},{4,5},{5,4},{6,7},{7,6},{8,9},{9,8},{10,11... | collective-permute-start | bytes 4128776 | tf_op jit(solution)/shard_map/cond/branch_1_fun/ppermute | solution.py:754
  143.1 2.8 %collective-permute-start.2 = (bf16[128,256]{1,0:T(8,128)(2,1)}, bf16[128,256]{1,0:T(8,128)(2,1)}, u32[]{:S(2)}, u32[]{:S(2)}) collective-permute-start(bf16[128,256]{1,0:T(8,128)(2,1)} %pad_dynamic-slice_fusion.6), channel_id=1, source_target_pairs={{0,1},{1,0},{2,3},{3,2},{4,5},{5,4},{6,7},{7,6},{8,9},{9,8},{10,11... | collective-permute-start | bytes 196616 | tf_op jit(solution)/shard_map/cond/branch_1_fun/ppermute | solution.py:754
  146.8 3.3 %copy-start.11 = (bf16[128,256]{1,0:T(8,128)(2,1)}, bf16[128,256]{1,0:T(8,128)(2,1)S(1)}, u32[]{:S(2)}) copy-start(bf16[128,256]{1,0:T(8,128)(2,1)S(1)} %add_convert_fusion.8) | copy-start | bytes 196612 | tf_op jit(solution)/shard_map/cond
  153.0 12.0 %collective-permute-start.3 = (bf16[1408,256]{1,0:T(8,128)(2,1)}, bf16[1408,256]{1,0:T(8,128)(2,1)}, u32[]{:S(2)}, u32[]{:S(2)}) collective-permute-start(bf16[1408,256]{1,0:T(8,128)(2,1)} %fusion.5), channel_id=1, source_target_pairs={{0,16},{1,3},{2,18},{3,1},{4,20},{5,7},{6,22},{7,5},{8,24},{9,11},... | collective-permute-start | bytes 2162696 | tf_op jit(solution)/shard_map/cond/branch_1_fun/ppermute | solution.py:754
  153.6 11.4 %copy-start.12 = (bf16[128,256]{1,0:T(8,128)(2,1)S(1)}, bf16[128,256]{1,0:T(8,128)(2,1)}, u32[]{:S(2)}) copy-start(bf16[128,256]{1,0:T(8,128)(2,1)} %copy-done.11) | copy-start | bytes 196612 | tf_op jit(solution)/shard_map/cond
  167.6 24.7 %copy-start.16 = (bf16[16,256]{1,0:T(8,128)(2,1)S(1)}, bf16[16,256]{1,0:T(8,128)(2,1)}, u32[]{:S(2)}) copy-start(bf16[16,256]{1,0:T(8,128)(2,1)} %get-tuple-element.106) | copy-start | bytes 24580 | tf_op jit(solution)/shard_map/cond
  167.6 24.8 %copy-start.3 = (bf16[512,768]{0,1:T(8,128)(2,1)S(1)}, bf16[512,768]{0,1:T(8,128)(2,1)}, u32[]{:S(2)}) copy-start(bf16[512,768]{0,1:T(8,128)(2,1)} %get-tuple-element.261) | copy-start | bytes 2359300 | tf_op jit(solution)/shard_map/cond
  167.6 7.8 %collective-permute-start.4 = (bf16[704,256]{1,0:T(8,128)(2,1)S(1)}, bf16[704,256]{1,0:T(8,128)(2,1)S(1)}, u32[]{:S(2)}, u32[]{:S(2)}) collective-permute-start(bf16[704,256]{1,0:T(8,128)(2,1)S(1)} %get-tuple-element.105), channel_id=1, source_target_pairs={{0,2},{1,17},{2,0},{3,19},{4,6},{5,21},{6,4},{7,23},{8,10},{9,25},... | collective-permute-start | bytes 1081352 | tf_op jit(solution)/shard_map/cond/branch_1_fun/ppermute | solution.py:754
  175.5 7.8 %collective-permute-start.5 = (bf16[352,256]{1,0:T(8,128)(2,1)S(1)}, bf16[352,256]{1,0:T(8,128)(2,1)S(1)}, u32[]{:S(2)}, u32[]{:S(2)}) collective-permute-start(bf16[352,256]{1,0:T(8,128)(2,1)S(1)} %get-tuple-element.274), channel_id=1, source_target_pairs={{0,4},{1,9},{2,6},{3,11},{4,0},{5,13},{6,2},{7,15},{8,12},{9,1},{1... | collective-permute-start | bytes 540680 | tf_op jit(solution)/shard_map/cond/branch_1_fun/ppermute | solution.py:754
  184.0 20.9 %copy-start.4 = (f32[512,768]{1,0:T(8,128)S(1)}, f32[512,768]{1,0:T(8,128)}, u32[]{:S(2)}) copy-start(f32[512,768]{1,0:T(8,128)} %get-tuple-element.109) | copy-start | bytes 4718596 | tf_op jit(solution)/shard_map/cond
  185.0 6.4 %collective-permute-start.6 = (bf16[176,256]{1,0:T(8,128)(2,1)S(1)}, bf16[176,256]{1,0:T(8,128)(2,1)S(1)}, u32[]{:S(2)}, u32[]{:S(2)}) collective-permute-start(bf16[176,256]{1,0:T(8,128)(2,1)S(1)} %add_convert_fusion.6), channel_id=1, source_target_pairs={{0,8},{1,5},{2,10},{3,7},{4,12},{5,1},{6,14},{7,3},{8,0},{9,13},{1... | collective-permute-start | bytes 270344 | tf_op jit(solution)/shard_map/cond/branch_1_fun/ppermute | solution.py:754
  192.3 12.4 %collective-permute-start.7 = (bf16[192,256]{1,0:T(8,128)(2,1)S(1)}, bf16[192,256]{1,0:T(8,128)(2,1)S(1)}, u32[]{:S(2)}, u32[]{:S(2)}) collective-permute-start(bf16[192,256]{1,0:T(8,128)(2,1)S(1)} %pad_maximum_fusion.7), channel_id=1, source_target_pairs={{0,8},{1,5},{2,10},{3,7},{4,12},{5,1},{6,14},{7,3},{8,0},{9,13},{1... | collective-permute-start | bytes 294920 | tf_op jit(solution)/shard_map/cond/branch_1_fun/ppermute | solution.py:754
  193.6 11.2 %collective-permute-start.10 = (f32[16,768]{1,0:T(8,128)}, f32[16,768]{1,0:T(8,128)S(1)}, u32[]{:S(2)}, u32[]{:S(2)}) collective-permute-start(f32[16,768]{1,0:T(8,128)} %get-tuple-element.110), channel_id=1, source_target_pairs={{16,0},{17,1},{18,2},{19,3},{20,4},{21,5},{22,6},{23,7},{24,8},{25... | collective-permute-start | bytes 147464 | tf_op jit(solution)/shard_map/cond/branch_1_fun/ppermute | solution.py:970
  204.8 5.6 %collective-permute-start.8 = (bf16[368,256]{1,0:T(8,128)(2,1)S(1)}, bf16[368,256]{1,0:T(8,128)(2,1)S(1)}, u32[]{:S(2)}, u32[]{:S(2)}) collective-permute-start(bf16[368,256]{1,0:T(8,128)(2,1)S(1)} %pad_maximum_fusion.5), channel_id=1, source_target_pairs={{0,4},{1,9},{2,6},{3,11},{4,0},{5,13},{6,2},{7,15},{8,12},{9,1},{1... | collective-permute-start | bytes 565256 | tf_op jit(solution)/shard_map/cond/branch_1_fun/ppermute | solution.py:754
  204.9 6.5 %copy-start.8 = (bf16[512,768]{1,0:T(8,128)(2,1)S(1)}, bf16[512,768]{1,0:T(8,128)(2,1)}, u32[]{:S(2)}) copy-start(bf16[512,768]{1,0:T(8,128)(2,1)} %copy.35) | copy-start | bytes 2359300 | tf_op jit(solution)/shard_map/cond
  210.5 15.5 %collective-permute-start.9 = (bf16[720,256]{1,0:T(8,128)(2,1)S(1)}, bf16[720,256]{1,0:T(8,128)(2,1)S(1)}, u32[]{:S(2)}, u32[]{:S(2)}) collective-permute-start(bf16[720,256]{1,0:T(8,128)(2,1)S(1)} %pad_maximum_fusion.3), channel_id=1, source_target_pairs={{0,2},{1,17},{2,0},{3,19},{4,6},{5,21},{6,4},{7,23},{8,10},{9,25},... | collective-permute-start | bytes 1105928 | tf_op jit(solution)/shard_map/cond/branch_1_fun/ppermute | solution.py:754
  226.2 13.4 %collective-permute-start.11 = (bf16[1424,256]{1,0:T(8,128)(2,1)S(1)}, bf16[1424,256]{1,0:T(8,128)(2,1)S(1)}, u32[]{:S(2)}, u32[]{:S(2)}) collective-permute-start(bf16[1424,256]{1,0:T(8,128)(2,1)S(1)} %pad_maximum_fusion.1), channel_id=1, source_target_pairs={{0,16},{1,3},{2,18},{3,1},{4,20},{5,7},{6,22},{7,5},{8,24},{9,11},... | collective-permute-start | bytes 2187272 | tf_op jit(solution)/shard_map/cond/branch_1_fun/ppermute | solution.py:754
  239.8 3.3 %copy-start = (bf16[2832,256]{1,0:T(8,128)(2,1)}, bf16[2832,256]{1,0:T(8,128)(2,1)S(1)}, u32[]{:S(2)}) copy-start(bf16[2832,256]{1,0:T(8,128)(2,1)S(1)} %pad_maximum_fusion.own.own_l.own_s.own_e) | copy-start | bytes 4349956 | tf_op jit(solution)/shard_map/cond
  239.8 3.3 %collective-permute-start.12 = (bf16[2832,256]{1,0:T(8,128)(2,1)S(1)}, bf16[2832,256]{1,0:T(8,128)(2,1)S(1)}, u32[]{:S(2)}, u32[]{:S(2)}) collective-permute-start(bf16[2832,256]{1,0:T(8,128)(2,1)S(1)} %pad_maximum_fusion.own.own_l.own_s.own_e), channel_id=1, source_target_pairs={{0,1},{1,0},{2,3},{3,2},{4,5},{5,4},{6,7},{7,6},{8,9},{9,8},{10,11... | collective-permute-start | bytes 4349960 | tf_op jit(solution)/shard_map/cond/branch_1_fun/ppermute | solution.py:754
  243.1 1.1 copy-start.1
  (5 other events, 3.6 us)
Sparse Core Ops, SparseCore 0:
  18.7 60.5 all-gather.2
  95.2 149.4 all-reduce.8

commit v4 on v3

--- a/solution.py
+++ b/solution.py
@@ -606,10 +606,11 @@
 
 def unproject_kernel(T, flag, dx, g, act, z, pre, cw, rows, dst, b, nt_s, nh, skip, bias, alog,
                      rsum, csum, roff, coff, dkeep, dbc, dcs, dlr, ggain,
-                     dw_o, dpl_o, dph_o, small_o,
+                     keep_o, send_o, dpl_o, dph_o, skeep_o, ssend_o,
                      ht_s, tot, hd_s, dbs, dls, small, shifts, shifts_back):
     step = pl.program_id(0)
     E = T + HALO
+    first_core = flag[5] == 0
 
     @pl.when(step == 0)
     def _():
@@ -651,7 +652,10 @@
     def emit(local, halo):
         local = local.astype(BF)
         hd_s[0:HALO, :] = halo.astype(BF)
-        dw_o[0] = (nn(nt_s[...], local) + nn(ht_s[...], hd_s[...])).astype(BF)
+        dw = (nn(nt_s[...], local) + nn(ht_s[...], hd_s[...])).astype(BF)
+        top, bottom = dw[: D // 2], dw[D // 2 :]
+        keep_o[0] = jnp.where(first_core, top, bottom)
+        send_o[0] = jnp.where(first_core, bottom, top)
         dpl_o[...] = local
         dph_o[...] = hd_s[0:HALO, :]
 
@@ -713,7 +717,9 @@
         small[at : at + 1, 128:] = jnp.sum(dl * dt * a, axis=0, keepdims=True)
         for q in range(INNER // CH):
             small[at + 1 + q : at + 2 + q, :] = ggain[:, CH * q : CH * (q + 1)]
-        small_o[...] = small[...].astype(BF)
+        data = small[...].astype(BF)
+        skeep_o[...] = jnp.where(first_core, data, jnp.zeros_like(data))
+        ssend_o[...] = jnp.where(first_core, jnp.zeros_like(data), data)
 
 
 def unproject(flag, dx, g, act, z, pre, conv_w, rows, dst, b, normt, nh, skip, bias, alog,
@@ -722,7 +728,8 @@
     E = T + HALO
     col = lambda rows: pl.BlockSpec((rows, CH), lambda i: (0, i))
     xcol = lambda rows: pl.BlockSpec((rows, CH), lambda i: (0, jnp.minimum(i, NCH - 2)))
-    shapes = [((NCH, D, CH), BF), ((T, NCH * CH), BF), ((HALO, NCH * CH), BF), ((SMALL, CH), BF)]
+    shapes = [((NCH, D // 2, CH), BF), ((NCH, D // 2, CH), BF), ((T, NCH * CH), BF), ((HALO, NCH * CH), BF),
+              ((SMALL, CH), BF), ((SMALL, CH), BF)]
     return pl.pallas_call(
         functools.partial(unproject_kernel, T),
         grid=(NCH,),
@@ -730,7 +737,7 @@
                   xcol(64), full((T, 64)), full((D, T)), full((HALO, D)), xcol(1), full((1, 128)), full((1, 128)),
                   full((128, T)), full((T, 128)), full((T, 128)), full((T, 128)), full((8, 128)), full((T, 128)),
                   full((T, 64)), full((T, 128)), full((1, INNER))],
-        out_specs=[pl.BlockSpec((1, D, CH), lambda i: (i, 0, 0)), col(T), col(HALO), full((SMALL, CH))],
+        out_specs=[pl.BlockSpec((1, D // 2, CH), lambda i: (i, 0, 0))] * 2 + [col(T), col(HALO)] + [full((SMALL, CH))] * 2,
         out_shape=[jax.ShapeDtypeStruct(s, d) for s, d in shapes],
         scratch_shapes=[pltpu.VMEM((D, 128), BF), pltpu.VMEM((E, CH), F32),
                         pltpu.VMEM((128, CH), BF), pltpu.VMEM((T, 64), F32), pltpu.VMEM((T, 128), F32),
@@ -808,32 +815,31 @@
     return (p.astype(F32) + q.astype(F32)).astype(BF)
 
 
-def reduce_all(main, small, later, inputs):
+def reduce_all(keep, send, keep_s, send_s, rows_s, later, inputs):
     bits = width("dp")
     masks = [1 << b for b in [bits] * width("dir") + list(range(1, bits))]
     odd = list(masks)
     for i in range(0, len(masks) - 1, 2):
         odd[i], odd[i + 1] = masks[i + 1], masks[i]
     order = list(zip(masks, odd))
-    core = side_of(1, 1)
-    if bits:
-        (keep, send), (keep_s, send_s) = halves(main, core, 1), halves(small, core)
-        main, small = add(keep, exchange(send, 1, 1)), add(keep_s, exchange(send_s, 1, 1))
-    buf = jnp.concatenate([main.reshape(-1, CH), small], axis=0)
-    if order:
-        keep, send = halves(buf, side_of(*order[0]))
-        send, inputs = lax.optimization_barrier((send, inputs))
-        got = exchange(send, *order[0])
+    got, got_s = exchange(send, 1, 1), exchange(send_s, 1, 1)
+    small = jnp.pad(add(keep_s, got_s), ((0, rows_s - SMALL), (0, 0)))
+    high = side_of(*order[0])
+    (keep, send), (got, got_send) = halves(keep, high, 1), halves(got, high, 1)
+    none = jnp.zeros_like(small)
+    send = jnp.concatenate([add(send, got_send).reshape(-1, CH), jnp.where(high, small, none)], axis=0)
+    send, inputs = lax.optimization_barrier((send, inputs))
+    keep = jnp.concatenate([add(keep, got).reshape(-1, CH), jnp.where(high, none, small)], axis=0)
+    got = exchange(send, *order[0])
     extra, beside = later(*inputs)
-    if order:
-        for at, pair in enumerate(order[1:]):
-            high = side_of(*pair)
-            (keep, send), (got, got_send) = halves(keep, high), halves(got, high)
-            send = add(send, got_send)
-            if at == 0:
-                send, extra = lax.optimization_barrier((send, extra))
-            keep, got = add(keep, got), exchange(send, *pair)
-        buf = add(keep, got)
+    for at, pair in enumerate(order[1:]):
+        high = side_of(*pair)
+        (keep, send), (got, got_send) = halves(keep, high), halves(got, high)
+        send = add(send, got_send)
+        if at == 0:
+            send, extra = lax.optimization_barrier((send, extra))
+        keep, got = add(keep, got), exchange(send, *pair)
+    buf = add(keep, got)
     for at, pair in enumerate(reversed(order)):
         n = buf.shape[0]
         if at == len(order) - 1:
@@ -842,33 +848,28 @@
         extra = add(extra, got[n:])
         high = side_of(*pair)
         buf = jnp.concatenate([jnp.where(high, got[:n], buf), jnp.where(high, buf, got[:n])], axis=0)
-    if not bits:
-        rows = NCH * D
-        both = buf[:rows].reshape(NCH, 2, D // 2, CH)
-        parts = [jnp.concatenate([both[:, q].reshape(rows // 2, CH), buf[rows : rows + (buf.shape[0] - rows) // 2], e], axis=0)
-                 for q, e in ((0, extra), (1, jnp.zeros_like(extra)))]
-        return parts[0], parts[1], jnp.zeros((1,), jnp.int32), beside
-    buf = jnp.concatenate([buf, extra], axis=0)
-    return buf, exchange(buf, 1, 1), core.astype(jnp.int32)[None], beside
-
-
-def late_kernel(core, own, other, own_l, other_l, own_s, other_s, own_e, other_e, zx_o, bc_o, dt_o, cw_o, cb_o, dtb_o, alog_o,
+    own = buf.reshape(2, -1, CH)
+    return own, exchange(own, 1, 1), extra, exchange(extra, 1, 1), beside
+
+
+def late_kernel(flag, own, other, own_l, other_l, own_s, other_s, own_e, other_e, zx_o, bc_o, dt_o, cw_o, cb_o, dtb_o, alog_o,
                 skip_o, og_o, ng_o):
-    half = D // 2
-    first = core[0] == 0
+    half, part = D // 2, D // 4
+    first = flag[5] == 0
     upper = jnp.where(first, own[...], other[...]).astype(F32)
     lower = jnp.where(first, other[...], own[...]).astype(F32)
     for q in range(2):
-        zx_o[0:half, CH * q : CH * (q + 1)] = upper[half * q : half * (q + 1)]
-        zx_o[half:, CH * q : CH * (q + 1)] = lower[half * q : half * (q + 1)]
+        for r in range(2):
+            zx_o[part * r : part * (r + 1), CH * q : CH * (q + 1)] = upper[r, part * q : part * (q + 1)]
+            zx_o[half + part * r : half + part * (r + 1), CH * q : CH * (q + 1)] = lower[r, part * q : part * (q + 1)]
 
     @pl.when(pl.program_id(0) == 0)
     def _():
-        tail = jnp.concatenate([jnp.where(first, own_l[...], other_l[...]), jnp.where(first, other_l[...], own_l[...])], axis=0)
-        tail = tail.astype(F32)
+        tops, bottoms = jnp.where(first, own_l[...], other_l[...]), jnp.where(first, other_l[...], own_l[...])
+        tail = jnp.concatenate([tops[0], tops[1], bottoms[0], bottoms[1]], axis=0).astype(F32)
         bc_o[...] = tail[:, :128]
         dt_o[...] = tail[:, 128:].T[: 2 * HEADS, :]
-        sm = jnp.where(first, own_s[...], other_s[...]).astype(F32)
+        sm = jnp.where(first, own_s[0], other_s[0]).astype(F32)
         for q in range(NCH):
             n = CH if q < NCH - 1 else 2 * STATE
             cw_o[:, CH * q : CH * q + n] = sm[CONV * q : CONV * (q + 1), :n]
@@ -884,16 +885,15 @@
         skip_o[...] = sm[at + 10, :HEADS]
 
 
-def late(core, own, other):
+def late(flag, own, other, own_e, other_e):
     n = INNER // CH // 2
     taps = INNER + 2 * STATE
     shapes = [(D, 2 * INNER), (D, 2 * STATE), (2 * HEADS, D), (CONV, taps), (taps,), (2 * HEADS,), (2 * HEADS,), (HEADS,),
               (INNER,), (D,)]
-    two = pl.BlockSpec((D, CH), lambda i: (i, 0))
-    last = pl.BlockSpec((D // 2, CH), lambda i: (NCH - 1, 0))
-    small = pl.BlockSpec((SMALL, CH), lambda i: (NCH * D // (2 * SMALL), 0))
-    end = own.shape[0] // EXTRA - 1
-    extra = pl.BlockSpec((EXTRA, CH), lambda i: (end, 0))
+    two = pl.BlockSpec((2, D // 2, CH), lambda i: (0, i, 0))
+    last = pl.BlockSpec((2, D // 4, CH), lambda i: (0, NCH - 1, 0))
+    small = pl.BlockSpec((1, SMALL, CH), lambda i: (0, NCH * D // (4 * SMALL), 0))
+    extra = full((EXTRA, CH))
     return pl.pallas_call(
         late_kernel,
         grid=(n,),
@@ -902,7 +902,7 @@
         out_shape=[jax.ShapeDtypeStruct(v, F32) for v in shapes],
         compiler_params=params(),
         name="late",
-    )(core, own, other, own, other, own, other, own, other)
+    )(flag, own, other, own, other, own, other, own_e, other_e)
 
 
 def early_kernel(wg, wo, zx, zx_o, wo_o):
@@ -912,13 +912,12 @@
 
 def early(wg, wo, zx):
     n = INNER // CH // 2
-    row = pl.BlockSpec((2 * CH, D), lambda i: (i, 0))
     col = pl.BlockSpec((D, 2 * CH), lambda i: (0, i))
     return pl.pallas_call(
         early_kernel,
         grid=(n,),
         in_specs=[col, col, pl.BlockSpec(memory_space=pl.ANY)],
-        out_specs=[col, row],
+        out_specs=[col, pl.BlockSpec((2 * CH, D), lambda i: (i, 0))],
         out_shape=[jax.ShapeDtypeStruct((D, 2 * INNER), F32), jax.ShapeDtypeStruct((INNER, D), F32)],
         input_output_aliases={2: 0},
         compiler_params=params(),
@@ -943,7 +942,7 @@
     half = INNER // 2
     mine = jnp.concatenate([w_zx[:, INNER:], w_bc, w_dt, jnp.zeros((shard, 128 - 2 * HEADS), BF)], axis=1)
     halo = lax.ppermute(tok[T - HALO :], "dir", [(0, 1)])
-    flag = jnp.concatenate([side[None].astype(jnp.int32), doc_lengths[0]])
+    flag = jnp.concatenate([side[None].astype(jnp.int32), doc_lengths[0], lax.rem(lax.axis_index("dp"), 2)[None].astype(jnp.int32)])
     wide = NCH * CH
     cw = jnp.pad(conv_w, ((0, 0), (0, wide - conv_w.shape[1])))
     cb = jnp.pad(conv_b, (0, wide - conv_b.shape[0]))[None]
@@ -959,11 +958,11 @@
         dcs, dlr, dst = aside(flag, gm, wrc, c, ct, st_in)
         dst_in = swap(dst)
         dx, rsum, csum, roff, coff, dkeep, dbc = unmix(flag, b, bt, c, ct, uv, keep, table, act, gm)
-        dw1, dpl, dph, small = unproject(flag, dx, gm, act, z, pre, cw, table, dst_in, b, normt, nh, skip, bias, alog,
-                                         rsum, csum, roff, coff, dkeep, dbc, dcs, dlr, ggain)
+        keep_w, send_w, dpl, dph, keep_s, send_s = unproject(
+            flag, dx, gm, act, z, pre, cw, table, dst_in, b, normt, nh, skip, bias, alog, rsum, csum, roff, coff, dkeep, dbc,
+            dcs, dlr, ggain)
         rows = NCH * D
-        total = -(-(rows + SMALL) // (16 * devices)) * 16 * devices
-        small = jnp.pad(small, ((0, total - rows - SMALL), (0, 0)))
+        total = -(-(rows + 4 * SMALL) // (16 * devices)) * 16 * devices
 
         def later(dpl, dph):
             bo, gn, gnh, part = deferred(dpl, dph, w1, gg, no, rest, tok, halo)
@@ -975,8 +974,9 @@
             gx = rho * e_in - x32 * (rho * rho * rho * jnp.mean(e_in * x32, axis=1, keepdims=True))
             return part, (bo, (og.astype(F32) + gx).astype(BF))
 
-        own, other, core, (bo, grad_tokens) = reduce_all(dw1, small, later, (dpl, dph))
-        return (bo, grad_tokens) + tuple(late(core, own, other))
+        own, other, own_e, other_e, (bo, grad_tokens) = reduce_all(
+            keep_w, send_w, keep_s, send_s, (total - rows) // 4, later, (dpl, dph))
+        return (bo, grad_tokens) + tuple(late(flag, own, other, own_e, other_e))
 
     def rest_of(v):
         w1, rest, (halo, flag, cw, cb, bias, alog, skip, gain_in, gain_out, ogt), tok, og = v

time: 263 us -> 254 us (0.966)
  local copies, waits for them, and re-layouts: 16.4 us -> 11.2 us
  waiting for transfers between devices: 85.6 us -> 82.9 us
    ppermute x17 -> x18, waiting for transfers between devices: 82.8 us -> 79 us  [exchange(): lax.ppermute(v, BOTH, [(i, i ^ (mask_odd if i & 1 else mask_even)) for i...]
    convert_element_type x10 -> x9, other arithmetic: 8.8 us -> 5.57 us  [add(): return (p.astype(F32) + q.astype(F32)).astype(BF)]
    dynamic_slice x2 -> x0, local copies, waits for them, and re-layouts: 3.17 us -> none  [halves(): lax.dynamic_slice_in_dim(v, n - at, n, axis)]
    ppermute x17 -> x18, starting transfers between devices: 21 us -> 22.5 us  [exchange(): lax.ppermute(v, BOTH, [(i, i ^ (mask_odd if i & 1 else mask_even)) for i...]
  transfers between devices with their start and end apart: 21 -> 22, of which waited for: 14 -> 16; matrix products, arithmetic and copies ran while one was open for 11% -> 10% of each run, Pallas kernels for 30% -> 31%
where the time goes in v4:
time: 254 us
  Pallas kernels  101 us (40%)
  waiting for transfers between devices  82.9 us (33%)
  starting transfers between devices  27.9 us (11%)
  other arithmetic  15.1 us (6%)
  between operations  15 us (6%)
  local copies, waits for them, and re-layouts  11.2 us (4%)
    ppermute x18, waiting for transfers between devices, exchange(): lax.ppermute(v, BOTH, [(i, i ^ (mask_odd if i & 1 else mask_even)) for i...  79 us
    ppermute x18, starting transfers between devices, exchange(): lax.ppermute(v, BOTH, [(i, i ^ (mask_odd if i & 1 else mask_even)) for i...  22.5 us
    pallas_call x1, Pallas kernels, unmix(): pl.pallas_call(functools.partial(unmix_kernel, T), grid=(INNER // CH,), i...  18.6 us
    pallas_call x1, Pallas kernels, unproject(): pl.pallas_call(functools.partial(unproject_kernel, T), grid=(NCH,), in_sp...  18.3 us
    pallas_call x1, Pallas kernels, gate(): pl.pallas_call(functools.partial(gate_kernel, rest.shape[1] // 4), grid=(...  15.6 us
    pallas_call x1, Pallas kernels, project(): pl.pallas_call(functools.partial(project_kernel, T), grid=(NCH,), in_spec...  14.6 us
    pallas_call x1, Pallas kernels, deferred(): pl.pallas_call(functools.partial(deferred_kernel, rest.shape[1] // 4), gr...  9.38 us
    pallas_call x1, Pallas kernels, mix(): pl.pallas_call(functools.partial(mix_kernel, T), grid=(INNER // CH,), in_...  9.14 us
  transfers between devices with their start and end apart: 22, of which 16 were waited for; matrix products, arithmetic and copies ran while one was open for 10% of the time, Pallas kernels for 31%

profile of v4, /device:TPU:0, one launch (start us, length us, event | category | flops | bytes accessed | tf_op | source)
XLA Modules:
  0.0 253.6 jit_solution(6745780205067134221)
XLA Ops:
  7.2 1.0 slice.46
  8.3 0.9 concatenate.41
  9.2 4.1 %collective-permute-start.14 = (bf16[48,1792]{1,0:T(8,128)(2,1)S(1)}, bf16[48,1792]{1,0:T(8,128)(2,1)S(1)}, u32[]{:S(2)}, u32[]{:S(2)}) collective-permute-start(bf16[48,1792]{1,0:T(8,128)(2,1)S(1)} %concatenate.41), channel_id=1, source_target_pairs={{0,8},{1,3},{2,10},{3,1},{4,12},{5,7},{6,14},{7,5},{8,0},{9,11},{1... | collective-permute-start | bytes 516104 | tf_op jit(solution)/shard_map/ppermute | solution.py:761
  13.3 0.9 fusion.9
  14.2 1.6 pad_maximum_fusion.13
  15.9 2.6 %collective-permute-done.14 = bf16[48,1792]{1,0:T(8,128)(2,1)S(1)} collective-permute-done((bf16[48,1792]{1,0:T(8,128)(2,1)S(1)}, bf16[48,1792]{1,0:T(8,128)(2,1)S(1)}, u32[]{:S(2)}, u32[]{:S(2)}) %collective-permute-start.14) | collective-permute-done | bytes 172064 | tf_op jit(solution)/shard_map/ppermute | solution.py:761
  18.7 4.8 %collective-permute-start.15 = (bf16[2,48,1792]{2,1,0:T(8,128)(2,1)S(1)}, bf16[2,48,1792]{2,1,0:T(8,128)(2,1)S(1)}, u32[]{:S(2)}, u32[]{:S(2)}) collective-permute-start(bf16[2,48,1792]{2,1,0:T(8,128)(2,1)S(1)} %pad_maximum_fusion.12), channel_id=1, source_target_pairs={{0,4},{1,9},{2,6},{3,11},{4,0},{5,13},{6,2},{7,15},{8,12},{9,1},{1... | collective-permute-start | bytes 1032200 | tf_op jit(solution)/shard_map/ppermute | solution.py:761
  24.1 4.0 %collective-permute-start.16 = (bf16[16,768]{1,0:T(8,128)(2,1)}, bf16[16,768]{1,0:T(8,128)(2,1)}, u32[]{:S(2)}, u32[]{:S(2)}) collective-permute-start(bf16[16,768]{1,0:T(8,128)(2,1)} %slice_bitcast_fusion), channel_id=1, source_target_pairs={{0,16},{1,17},{2,18},{3,19},{4,20},{5,21},{6,22},{7,23},{8,24},{9,... | collective-permute-start | bytes 73736 | tf_op jit(solution)/shard_map/ppermute | solution.py:944
  31.2 1.2 copy.28
  33.7 1.6 collective-permute-start.17
  35.2 10.1 %collective-permute-done.17 = bf16[2,2,48,1792]{3,2,0,1:T(8,128)(2,1)S(1)} collective-permute-done((bf16[2,2,48,1792]{3,2,0,1:T(8,128)(2,1)S(1)}, bf16[2,2,48,1792]{3,2,0,1:T(8,128)(2,1)S(1)}, u32[]{:S(2)}, u32[]{:S(2)}) %collective-permute-start.17) | collective-permute-done | bytes 688160 | tf_op jit(solution)/shard_map/ppermute | solution.py:761
  45.5 1.2 copy.29
  46.7 3.3 %collective-permute-done.18 = bf16[2,2,2,48,1792]{4,3,2,0,1:T(8,128)(2,1)S(1)} collective-permute-done((bf16[2,2,2,48,1792]{4,3,2,0,1:T(8,128)(2,1)}, bf16[2,2,2,48,1792]{4,3,2,0,1:T(8,128)(2,1)S(1)}, u32[]{:S(2)}, u32[]{:S(2)}) %collective-permute-start.18) | collective-permute-done | bytes 1376288 | tf_op jit(solution)/shard_map/ppermute | solution.py:761
  51.0 14.6 %project.1 = (bf16[512,768]{1,0:T(8,128)(2,1)}, bf16[768,512]{1,0:T(8,128)(2,1)}, bf16[16,768]{1,0:T(8,128)(2,1)}, bf16[528,1792]{1,0:T(8,128)(2,1)}, bf16[512,1...) custom-call(s32[6]{0:T(128)} %pad_add_fusion.flag, ...), custom_call_target="tpu_custom_call" | custom-call | tf_op jit(solution)/shard_map/project/pallas_call | solution.py:215
  65.7 1.4 collective-permute-start.19
  67.1 9.1 %mix.1.y = f32[512,1536]{1,0:T(8,128)} custom-call(s32[6]{0:T(128)} %pad_add_fusion.flag, bf16[512,64]{1,0:T(8,128)(2,1)} %get-tuple-element.197.b, bf16[64,512]{1,0:T(8,128)(2,1)S(1)} %get-tuple-element.198.bt, bf16[512,64]{1,0:T(8,128)(2,1)S(1)} %get-tuple-element.199.c, bf16[512,128]{1,0:T(8,128)(2,1)} %get-tuple-element.201.uv, ...), custom_call_target="tpu_custom_call" | custom-call | tf_op jit(solution)/shard_map/mix/pallas_call | solution.py:317
  76.2 3.1 %all-gather.3.cloned.1.call-done = bf16[3072,768]{1,0:T(8,128)(2,1)} async-done(((bf16[192,768]{1,0:T(8,128)(2,1)}), bf16[3072,768]{1,0:T(8,128)(2,1)}) %all-gather.3.cloned.1.call-update) | async-done | bytes 4718608 | tf_op jit(solution)/shard_map/all_gather | solution.py:983
  79.4 15.6 %gate.1 = (bf16[512,1536]{1,0:T(8,128)(2,1)}, bf16[512,1536]{1,0:T(8,128)(2,1)}, bf16[512,1536]{1,0:T(8,128)(2,1)}, bf16[768,1536]{1,0:T(8,128)(2,1)}, bf16[768,1536]{1,0:T(8,128)(2,1)}, /*index=5*/f32[1,1536]{1,0:T(1,128)}) custom-call(f32[512,1536]{1,0:T(8,128)} %mix.1.y, bf16[512,128]{1,0:T(8,128)(2,1)} %get-tuple-element.206.wrc, ...), custom_call_target="tpu_custom_call" | custom-call | tf_op jit(solution)/shard_map/gate/pallas_call | solution.py:378
  95.0 1.2 slice.51
  96.8 142.9 %conditional.1 = (f32[768,3072]{1,0:T(8,128)}, f32[768,128]{1,0:T(8,128)}, f32[48,768]{1,0:T(8,128)}, f32[4,1664]{1,0:T(4,128)}, f32[1664]{0:T(1024)}, /*index=5...) conditional(s32[]{:T(128)} %bitcast.17, () %tuple.27, ...), branch_computations={%region_0.1_spmd, %region_1.4_spmd} | conditional | flops 24520756 | bytes 71271984 | solution.py:932
  97.0 4.3 %side.1 = (f32[512,64]{1,0:T(8,128)}, f32[512,128]{1,0:T(8,128)}, bf16[64,1536]{1,0:T(8,128)(2,1)}) custom-call(s32[6]{0:T(128)} %get-tuple-element.60.flag, bf16[512,1536]{1,0:T(8,128)(2,1)} %get-tuple-element.69.g.gm, bf16[512,128]{1,0:T(8,128)(2,1)} %get-tuple-element.74.wrc, bf16[512,64]{1,0:T(8,128)(2,1)} %get-tuple-element.63.c, ...), custom_call_target="tpu_custom_call" | custom-call | tf_op jit(solution)/shard_map/cond/branch_1_fun/side/pallas_call | solution.py:416
  101.3 1.5 collective-permute-start
  102.9 18.6 %unmix.1 = (f32[512,1536]{1,0:T(8,128)}, f32[128,512]{1,0:T(8,128)}, f32[512,128]{1,0:T(8,128)}, f32[512,128]{1,0:T(8,128)}, f32[512,128]{1,0:T(8,128)}, /*index=5*/f32[8,128]{1,0:T(8,128)}, f32[512,128]{1,0:T(8,128)}) custom-call(s32[6]{0:T(128)} %get-tuple-element.60.flag, bf16[512,64]{1,0:T(8,128)(2,1)} %get-tuple-element.61.b, ...), custom_call_target="tpu_custom_call" | custom-call | tf_op jit(solution)/shard_map/cond/branch_1_fun/unmix/pallas_call | solution.py:593
  121.5 18.3 %unproject.1 = (bf16[7,384,256]{2,1,0:T(8,128)(2,1)}, bf16[7,384,256]{2,1,0:T(8,128)(2,1)}, bf16[512,1792]{1,0:T(8,128)(2,1)}, bf16[16,1792]{1,0:T(8,128)(2,1)},...) custom-call(s32[6]{0:T(128)} %get-tuple-element.60.flag, f32[512,1536]{1,0:T(8,128)} %get-tuple-element.70.dx, ...), custom_call_target="tpu_custom_call" | custom-call | tf_op jit(solution)/shard_map/cond/branch_1_fun/unproject/pallas_call | solution.py:733
  140.4 3.0 %collective-permute-done.2 = bf16[64,256]{1,0:T(8,128)(2,1)} collective-permute-done((bf16[64,256]{1,0:T(8,128)(2,1)}, bf16[64,256]{1,0:T(8,128)(2,1)}, u32[]{:S(2)}, u32[]{:S(2)}) %collective-permute-start.2) | collective-permute-done | bytes 32800 | tf_op jit(solution)/shard_map/cond/branch_1_fun/ppermute | solution.py:761
  143.4 1.4 broadcast_select_fusion.8
  144.8 3.0 %add_convert_fusion = (bf16[7,192,256]{2,1,0:T(8,128)(2,1)S(1)}, bf16[7,192,256]{2,1,0:T(8,128)(2,1)}) fusion(bf16[7,384,256]{2,1,0:T(8,128)(2,1)} %collective-permute-done.1, s32[]{:T(128)S(6)} %select_n.175, bf16[7,384,256]{2,1,0:T(8,128)(2,1)} %get-tuple-element.91, s32[]{:T(128)S(6)} %select_n.171), kind=kLoop, calls=%fused_computation.10 | loop fusion | flops 2752512 | bytes 4128776 | tf_op jit(solution)/shard_map/cond/branch_1_fun/convert_element_type | solution.py:815
  147.8 0.9 pad_maximum_fusion.2
  149.3 9.4 %deferred.1 = (bf16[512,768]{1,0:T(8,128)(2,1)}, f32[512,768]{1,0:T(8,128)}, f32[16,768]{1,0:T(8,128)}, bf16[16,256]{1,0:T(8,128)(2,1)}) custom-call(bf16[512,1792]{1,0:T(8,128)(2,1)} %get-tuple-element.98.dpl, bf16[16,1792]{1,0:T(8,128)(2,1)} %get-tuple-element.99.dph, bf16[768,1792]{1,0:T(8,128)(2,1)S(1)} %get-tuple-element.100.w1, ...), custom_call_target="tpu_custom_call" | custom-call | tf_op jit(solution)/shard_map/cond/branch_1_fun/deferred/pallas_call | solution.py:462
  158.6 3.2 %collective-permute-done.3 = bf16[1408,256]{1,0:T(8,128)(2,1)} collective-permute-done((bf16[1408,256]{1,0:T(8,128)(2,1)}, bf16[1408,256]{1,0:T(8,128)(2,1)}, u32[]{:S(2)}, u32[]{:S(2)}) %collective-permute-start.3) | collective-permute-done | bytes 720928 | tf_op jit(solution)/shard_map/cond/branch_1_fun/ppermute | solution.py:761
  161.9 2.4 add_convert_fusion.3
  164.9 6.9 %collective-permute-done.4 = bf16[704,256]{1,0:T(8,128)(2,1)S(1)} collective-permute-done((bf16[704,256]{1,0:T(8,128)(2,1)S(1)}, bf16[704,256]{1,0:T(8,128)(2,1)S(1)}, u32[]{:S(2)}, u32[]{:S(2)}) %collective-permute-start.4) | collective-permute-done | bytes 360480 | tf_op jit(solution)/shard_map/cond/branch_1_fun/ppermute | solution.py:761
  171.9 1.6 collective-permute-start.5
  173.5 5.8 %collective-permute-done.5 = bf16[352,256]{1,0:T(8,128)(2,1)S(1)} collective-permute-done((bf16[352,256]{1,0:T(8,128)(2,1)S(1)}, bf16[352,256]{1,0:T(8,128)(2,1)S(1)}, u32[]{:S(2)}, u32[]{:S(2)}) %collective-permute-start.5) | collective-permute-done | bytes 180256 | tf_op jit(solution)/shard_map/cond/branch_1_fun/ppermute | solution.py:761
  179.3 0.8 collective-permute-start.6
  180.1 5.2 %collective-permute-done.6 = bf16[176,256]{1,0:T(8,128)(2,1)S(1)} collective-permute-done((bf16[176,256]{1,0:T(8,128)(2,1)S(1)}, bf16[176,256]{1,0:T(8,128)(2,1)S(1)}, u32[]{:S(2)}, u32[]{:S(2)}) %collective-permute-start.6) | collective-permute-done | bytes 90144 | tf_op jit(solution)/shard_map/cond/branch_1_fun/ppermute | solution.py:761
  186.1 1.3 collective-permute-start.10
  187.4 7.2 %collective-permute-done.7 = bf16[192,256]{1,0:T(8,128)(2,1)S(1)} collective-permute-done((bf16[192,256]{1,0:T(8,128)(2,1)S(1)}, bf16[192,256]{1,0:T(8,128)(2,1)S(1)}, u32[]{:S(2)}, u32[]{:S(2)}) %collective-permute-start.7) | collective-permute-done | bytes 98336 | tf_op jit(solution)/shard_map/cond/branch_1_fun/ppermute | solution.py:761
  194.8 1.9 fusion
  196.7 4.8 %collective-permute-done.8 = bf16[368,256]{1,0:T(8,128)(2,1)S(1)} collective-permute-done((bf16[368,256]{1,0:T(8,128)(2,1)S(1)}, bf16[368,256]{1,0:T(8,128)(2,1)S(1)}, u32[]{:S(2)}, u32[]{:S(2)}) %collective-permute-start.8) | collective-permute-done | bytes 188448 | tf_op jit(solution)/shard_map/cond/branch_1_fun/ppermute | solution.py:761
  201.7 0.9 collective-permute-start.9
  202.6 1.3 fusion.4
  203.9 8.2 %collective-permute-done.9 = bf16[720,256]{1,0:T(8,128)(2,1)S(1)} collective-permute-done((bf16[720,256]{1,0:T(8,128)(2,1)S(1)}, bf16[720,256]{1,0:T(8,128)(2,1)S(1)}, u32[]{:S(2)}, u32[]{:S(2)}) %collective-permute-start.9) | collective-permute-done | bytes 368672 | tf_op jit(solution)/shard_map/cond/branch_1_fun/ppermute | solution.py:761
  212.4 3.0 %collective-permute-start.11 = (bf16[1424,256]{1,0:T(8,128)(2,1)S(1)}, bf16[1424,256]{1,0:T(8,128)(2,1)S(1)}, u32[]{:S(2)}, u32[]{:S(2)}) collective-permute-start(bf16[1424,256]{1,0:T(8,128)(2,1)S(1)} %pad_maximum_fusion.1), channel_id=1, source_target_pairs={{0,16},{1,3},{2,18},{3,1},{4,20},{5,7},{6,22},{7,5},{8,24},{9,11},... | collective-permute-start | bytes 2187272 | tf_op jit(solution)/shard_map/cond/branch_1_fun/ppermute | solution.py:761
  215.4 15.7 %collective-permute-done.11 = bf16[1424,256]{1,0:T(8,128)(2,1)S(1)} collective-permute-done((bf16[1424,256]{1,0:T(8,128)(2,1)S(1)}, bf16[1424,256]{1,0:T(8,128)(2,1)S(1)}, u32[]{:S(2)}, u32[]{:S(2)}) %collective-permute-start.11) | collective-permute-done | bytes 729120 | tf_op jit(solution)/shard_map/cond/branch_1_fun/ppermute | solution.py:761
  231.9 2.4 collective-permute-done.13.other_e
  234.8 4.8 %late.1 = (f32[768,3072]{1,0:T(8,128)}, f32[768,128]{1,0:T(8,128)}, f32[48,768]{1,0:T(8,128)}, f32[4,1664]{1,0:T(4,128)}, f32[1664]{0:T(1024)}, /*index=5*/f32[4...) custom-call(s32[6]{0:T(128)} %get-tuple-element.60.flag, bf16[2,1408,256]{2,1,0:T(8,128)(2,1)} %bitcast.44, ...), custom_call_target="tpu_custom_call" | custom-call | tf_op jit(solution)/shard_map/cond/branch_1_fun/late/pallas_call | solution.py:897
  240.4 6.3 %early.1 = (f32[768,3072]{1,0:T(8,128)}, f32[1536,768]{1,0:T(8,128)}) custom-call(bf16[768,1536]{1,0:T(8,128)(2,1)} %get-tuple-element.267.wg, bf16[768,1536]{1,0:T(8,128)(2,1)} %get-tuple-element.268.wo, f32[768,3072]{1,0:T(8,128)} %get-tuple-element.225.zx), custom_call_target="tpu_custom_call", output_to_operand_aliasing={{0}: (2, {})} | custom-call | tf_op jit(solution)/shard_map/early/pallas_call | solution.py:916
  (112 shorter events, 11.6 us)
Async XLA Ops:
  7.2 16.3 %copy-start.1 = (bf16[1,512,768]{2,1,0:T(8,128)(2,1)S(1)}, bf16[1,512,768]{2,1,0:T(8,128)(2,1)}, u32[]{:S(2)}) copy-start(bf16[1,512,768]{2,1,0:T(8,128)(2,1)} %param.16) | copy-start | bytes 2359300
  7.2 72.2 %all-gather.3.cloned.1.call-start = ((), (), s32[]{:S(2)}) async-start(), calls=%async_computation | async-start | bytes 5013504 | tf_op jit(solution)/shard_map/all_gather | solution.py:983
  8.2 19.9 %copy-start.19 = (f32[768]{0:T(1024)S(1)}, f32[768]{0:T(1024)}, u32[]{:S(2)}) copy-start(f32[768]{0:T(1024)} %param.17) | copy-start | bytes 9220
  8.2 20.4 %copy-start.16 = (f32[1536]{0:T(1024)S(1)}, f32[1536]{0:T(1024)}, u32[]{:S(2)}) copy-start(f32[1536]{0:T(1024)} %param.26) | copy-start | bytes 18436
  8.2 21.0 %copy-start.17 = (f32[1664]{0:T(1024)S(1)}, f32[1664]{0:T(1024)}, u32[]{:S(2)}) copy-start(f32[1664]{0:T(1024)} %param.22) | copy-start | bytes 19972
  8.3 21.6 %copy-start.20 = (f32[24]{0:T(128)S(1)}, f32[24]{0:T(128)}, u32[]{:S(2)}) copy-start(f32[24]{0:T(128)} %param.25) | copy-start | bytes 292
  8.3 22.4 %copy-start.15 = (f32[4,1664]{1,0:T(4,128)S(1)}, f32[4,1664]{1,0:T(4,128)}, u32[]{:S(2)}) copy-start(f32[4,1664]{1,0:T(4,128)} %param.21) | copy-start | bytes 79876
  8.3 22.9 %copy-start.6 = (bf16[1,512,768]{2,1,0:T(8,128)(2,1)S(1)}, bf16[1,512,768]{2,1,0:T(8,128)(2,1)}, u32[]{:S(2)}) copy-start(bf16[1,512,768]{2,1,0:T(8,128)(2,1)} %param.29) | copy-start | bytes 2359300
  9.2 9.3 %collective-permute-start.14 = (bf16[48,1792]{1,0:T(8,128)(2,1)S(1)}, bf16[48,1792]{1,0:T(8,128)(2,1)S(1)}, u32[]{:S(2)}, u32[]{:S(2)}) collective-permute-start(bf16[48,1792]{1,0:T(8,128)(2,1)S(1)} %concatenate.41), channel_id=1, source_target_pairs={{0,8},{1,3},{2,10},{3,1},{4,12},{5,7},{6,14},{7,5},{8,0},{9,11},{1... | collective-permute-start | bytes 516104 | tf_op jit(solution)/shard_map/ppermute | solution.py:761
  15.9 16.6 %copy-start.21 = (s32[1,4]{1,0:T(1,128)S(1)}, s32[1,4]{1,0:T(1,128)}, u32[]{:S(2)}) copy-start(s32[1,4]{1,0:T(1,128)} %param.28) | copy-start | bytes 52
  15.9 17.1 %copy-start.22 = (f32[48]{0:T(128)S(1)}, f32[48]{0:T(128)}, u32[]{:S(2)}) copy-start(f32[48]{0:T(128)} %param.24) | copy-start | bytes 580
  15.9 17.1 %copy-start.23 = (f32[48]{0:T(128)S(1)}, f32[48]{0:T(128)}, u32[]{:S(2)}) copy-start(f32[48]{0:T(128)} %param.23) | copy-start | bytes 580
  18.6 221.8 %all-reduce.8.cloned.1.call-start = ((), (), s32[]{:S(2)}) async-start(), calls=%async_computation.1 | async-start | bytes 9437184 | tf_op jit(solution)/shard_map/psum | solution.py:992
  18.7 14.9 %collective-permute-start.15 = (bf16[2,48,1792]{2,1,0:T(8,128)(2,1)S(1)}, bf16[2,48,1792]{2,1,0:T(8,128)(2,1)S(1)}, u32[]{:S(2)}, u32[]{:S(2)}) collective-permute-start(bf16[2,48,1792]{2,1,0:T(8,128)(2,1)S(1)} %pad_maximum_fusion.12), channel_id=1, source_target_pairs={{0,4},{1,9},{2,6},{3,11},{4,0},{5,13},{6,2},{7,15},{8,12},{9,1},{1... | collective-permute-start | bytes 1032200 | tf_op jit(solution)/shard_map/ppermute | solution.py:761
  24.1 9.6 %collective-permute-start.16 = (bf16[16,768]{1,0:T(8,128)(2,1)}, bf16[16,768]{1,0:T(8,128)(2,1)}, u32[]{:S(2)}, u32[]{:S(2)}) collective-permute-start(bf16[16,768]{1,0:T(8,128)(2,1)} %slice_bitcast_fusion), channel_id=1, source_target_pairs={{0,16},{1,17},{2,18},{3,19},{4,20},{5,21},{6,22},{7,23},{8,24},{9,... | collective-permute-start | bytes 73736 | tf_op jit(solution)/shard_map/ppermute | solution.py:944
  33.7 11.6 %collective-permute-start.17 = (bf16[2,2,48,1792]{3,2,0,1:T(8,128)(2,1)S(1)}, bf16[2,2,48,1792]{3,2,0,1:T(8,128)(2,1)S(1)}, u32[]{:S(2)}, u32[]{:S(2)}) collective-permute-start(bf16[2,2,48,1792]{3,2,0,1:T(8,128)(2,1)S(1)} %pad_maximum_fusion.11), channel_id=1, source_target_pairs={{0,2},{1,5},{2,0},{3,7},{4,6},{5,1},{6,4},{7,3},{8,10},{9,13},{10,... | collective-permute-start | bytes 2064392 | tf_op jit(solution)/shard_map/ppermute | solution.py:761
  46.7 3.3 %collective-permute-start.18 = (bf16[2,2,2,48,1792]{4,3,2,0,1:T(8,128)(2,1)}, bf16[2,2,2,48,1792]{4,3,2,0,1:T(8,128)(2,1)S(1)}, u32[]{:S(2)}, u32[]{:S(2)}) collective-permute-start(bf16[2,2,2,48,1792]{4,3,2,0,1:T(8,128)(2,1)} %copy.29), channel_id=1, source_target_pairs={{0,1},{1,0},{2,3},{3,2},{4,5},{5,4},{6,7},{7,6},{8,9},{9,8},{10,11... | collective-permute-start | bytes 4128776 | tf_op jit(solution)/shard_map/ppermute | solution.py:761
  65.6 10.6 %copy-start.4 = (f32[12,16,512]{2,1,0:T(8,128)}, f32[12,16,512]{2,1,0:T(8,128)S(1)}, u32[]{:S(2)}) copy-start(f32[12,16,512]{2,1,0:T(8,128)S(1)} %get-tuple-element.203.rows) | copy-start | bytes 1179652
  65.7 10.5 %copy-start.7 = (bf16[512,64]{1,0:T(8,128)(2,1)}, bf16[512,64]{1,0:T(8,128)(2,1)S(1)}, u32[]{:S(2)}) copy-start(bf16[512,64]{1,0:T(8,128)(2,1)S(1)} %get-tuple-element.199.c) | copy-start | bytes 196612
  65.7 10.5 %copy-start.9 = (bf16[64,512]{1,0:T(8,128)(2,1)}, bf16[64,512]{1,0:T(8,128)(2,1)S(1)}, u32[]{:S(2)}) copy-start(bf16[64,512]{1,0:T(8,128)(2,1)S(1)} %get-tuple-element.198.bt) | copy-start | bytes 196612
  65.7 10.5 %collective-permute-start.19 = (bf16[64,1536]{1,0:T(8,128)(2,1)}, bf16[64,1536]{1,0:T(8,128)(2,1)}, u32[]{:S(2)}, u32[]{:S(2)}) collective-permute-start(bf16[64,1536]{1,0:T(8,128)(2,1)} %get-tuple-element.207), channel_id=1, source_target_pairs={{0,16},{1,17},{2,18},{3,19},{4,20},{5,21},{6,22},{7,23},{8,24},{9,... | collective-permute-start | bytes 589832 | tf_op jit(solution)/shard_map/ppermute | solution.py:761
  97.0 5.9 %copy-start.5 = (f32[12,16,512]{2,1,0:T(8,128)S(1)}, f32[12,16,512]{2,1,0:T(8,128)}, u32[]{:S(2)}) copy-start(f32[12,16,512]{2,1,0:T(8,128)} %get-tuple-element.67.rows) | copy-start | bytes 1179652 | tf_op jit(solution)/shard_map/cond
  97.0 5.9 %copy-start.8 = (bf16[512,64]{1,0:T(8,128)(2,1)S(1)}, bf16[512,64]{1,0:T(8,128)(2,1)}, u32[]{:S(2)}) copy-start(bf16[512,64]{1,0:T(8,128)(2,1)} %get-tuple-element.63.c) | copy-start | bytes 196612 | tf_op jit(solution)/shard_map/cond
  97.0 5.9 %copy-start.10 = (bf16[64,512]{1,0:T(8,128)(2,1)S(1)}, bf16[64,512]{1,0:T(8,128)(2,1)}, u32[]{:S(2)}) copy-start(bf16[64,512]{1,0:T(8,128)(2,1)} %get-tuple-element.62.bt) | copy-start | bytes 196612 | tf_op jit(solution)/shard_map/cond
  101.3 20.1 %collective-permute-start = (bf16[64,1536]{1,0:T(8,128)(2,1)}, bf16[64,1536]{1,0:T(8,128)(2,1)}, u32[]{:S(2)}, u32[]{:S(2)}) collective-permute-start(bf16[64,1536]{1,0:T(8,128)(2,1)} %get-tuple-element.76), channel_id=1, source_target_pairs={{0,16},{1,17},{2,18},{3,19},{4,20},{5,21},{6,22},{7,23},{8,24},{9,... | collective-permute-start | bytes 589832 | tf_op jit(solution)/shard_map/cond/branch_1_fun/ppermute | solution.py:761
  139.8 5.0 %collective-permute-start.1 = (bf16[7,384,256]{2,1,0:T(8,128)(2,1)}, bf16[7,384,256]{2,1,0:T(8,128)(2,1)}, u32[]{:S(2)}, u32[]{:S(2)}) collective-permute-start(bf16[7,384,256]{2,1,0:T(8,128)(2,1)} %get-tuple-element.92), channel_id=1, source_target_pairs={{0,1},{1,0},{2,3},{3,2},{4,5},{5,4},{6,7},{7,6},{8,9},{9,8},{10,11... | collective-permute-start | bytes 4128776 | tf_op jit(solution)/shard_map/cond/branch_1_fun/ppermute | solution.py:761
  140.0 3.4 %collective-permute-start.2 = (bf16[64,256]{1,0:T(8,128)(2,1)}, bf16[64,256]{1,0:T(8,128)(2,1)}, u32[]{:S(2)}, u32[]{:S(2)}) collective-permute-start(bf16[64,256]{1,0:T(8,128)(2,1)} %get-tuple-element.94), channel_id=1, source_target_pairs={{0,1},{1,0},{2,3},{3,2},{4,5},{5,4},{6,7},{7,6},{8,9},{9,8},{10,11... | collective-permute-start | bytes 98312 | tf_op jit(solution)/shard_map/cond/branch_1_fun/ppermute | solution.py:761
  148.7 13.2 %collective-permute-start.3 = (bf16[1408,256]{1,0:T(8,128)(2,1)}, bf16[1408,256]{1,0:T(8,128)(2,1)}, u32[]{:S(2)}, u32[]{:S(2)}) collective-permute-start(bf16[1408,256]{1,0:T(8,128)(2,1)} %pad_maximum_fusion.2), channel_id=1, source_target_pairs={{0,16},{1,3},{2,18},{3,1},{4,20},{5,7},{6,22},{7,5},{8,24},{9,11},... | collective-permute-start | bytes 2162696 | tf_op jit(solution)/shard_map/cond/branch_1_fun/ppermute | solution.py:761
  149.3 12.6 %copy-start.11 = (bf16[64,256]{1,0:T(8,128)(2,1)S(1)}, bf16[64,256]{1,0:T(8,128)(2,1)}, u32[]{:S(2)}) copy-start(bf16[64,256]{1,0:T(8,128)(2,1)} %get-tuple-element.284) | copy-start | bytes 98308 | tf_op jit(solution)/shard_map/cond
  161.9 23.5 %copy-start.12 = (bf16[16,256]{1,0:T(8,128)(2,1)S(1)}, bf16[16,256]{1,0:T(8,128)(2,1)}, u32[]{:S(2)}) copy-start(bf16[16,256]{1,0:T(8,128)(2,1)} %get-tuple-element.108) | copy-start | bytes 24580 | tf_op jit(solution)/shard_map/cond
  161.9 23.9 %copy-start.2 = (bf16[512,768]{0,1:T(8,128)(2,1)S(1)}, bf16[512,768]{0,1:T(8,128)(2,1)}, u32[]{:S(2)}) copy-start(bf16[512,768]{0,1:T(8,128)(2,1)} %get-tuple-element.263) | copy-start | bytes 2359300 | tf_op jit(solution)/shard_map/cond
  164.3 7.5 %collective-permute-start.4 = (bf16[704,256]{1,0:T(8,128)(2,1)S(1)}, bf16[704,256]{1,0:T(8,128)(2,1)S(1)}, u32[]{:S(2)}, u32[]{:S(2)}) collective-permute-start(bf16[704,256]{1,0:T(8,128)(2,1)S(1)} %get-tuple-element.107), channel_id=1, source_target_pairs={{0,2},{1,17},{2,0},{3,19},{4,6},{5,21},{6,4},{7,23},{8,10},{9,25},... | collective-permute-start | bytes 1081352 | tf_op jit(solution)/shard_map/cond/branch_1_fun/ppermute | solution.py:761
  171.8 14.3 %copy-start.14 = (f32[1,768]{1,0:T(1,128)S(1)}, f32[1,768]{1,0:T(1,128)}, u32[]{:S(2)}) copy-start(f32[1,768]{1,0:T(1,128)} %get-tuple-element.113) | copy-start | bytes 9220 | tf_op jit(solution)/shard_map/cond
  171.8 14.3 %copy-start.24 = (f32[16,768]{1,0:T(8,128)S(1)}, f32[16,768]{1,0:T(8,128)}, u32[]{:S(2)}) copy-start(f32[16,768]{1,0:T(8,128)} %get-tuple-element.112) | copy-start | bytes 147460 | tf_op jit(solution)/shard_map/cond
  171.9 7.3 %collective-permute-start.5 = (bf16[352,256]{1,0:T(8,128)(2,1)S(1)}, bf16[352,256]{1,0:T(8,128)(2,1)S(1)}, u32[]{:S(2)}, u32[]{:S(2)}) collective-permute-start(bf16[352,256]{1,0:T(8,128)(2,1)S(1)} %get-tuple-element.278), channel_id=1, source_target_pairs={{0,4},{1,9},{2,6},{3,11},{4,0},{5,13},{6,2},{7,15},{8,12},{9,1},{1... | collective-permute-start | bytes 540680 | tf_op jit(solution)/shard_map/cond/branch_1_fun/ppermute | solution.py:761
  179.3 6.0 %collective-permute-start.6 = (bf16[176,256]{1,0:T(8,128)(2,1)S(1)}, bf16[176,256]{1,0:T(8,128)(2,1)S(1)}, u32[]{:S(2)}, u32[]{:S(2)}) collective-permute-start(bf16[176,256]{1,0:T(8,128)(2,1)S(1)} %add_convert_fusion.7), channel_id=1, source_target_pairs={{0,8},{1,5},{2,10},{3,7},{4,12},{5,1},{6,14},{7,3},{8,0},{9,13},{1... | collective-permute-start | bytes 270344 | tf_op jit(solution)/shard_map/cond/branch_1_fun/ppermute | solution.py:761
  185.4 9.3 %collective-permute-start.7 = (bf16[192,256]{1,0:T(8,128)(2,1)S(1)}, bf16[192,256]{1,0:T(8,128)(2,1)S(1)}, u32[]{:S(2)}, u32[]{:S(2)}) collective-permute-start(bf16[192,256]{1,0:T(8,128)(2,1)S(1)} %pad_maximum_fusion.8), channel_id=1, source_target_pairs={{0,8},{1,5},{2,10},{3,7},{4,12},{5,1},{6,14},{7,3},{8,0},{9,13},{1... | collective-permute-start | bytes 294920 | tf_op jit(solution)/shard_map/cond/branch_1_fun/ppermute | solution.py:761
  186.1 8.7 %collective-permute-start.10 = (f32[16,768]{1,0:T(8,128)S(1)}, f32[16,768]{1,0:T(8,128)S(1)}, u32[]{:S(2)}, u32[]{:S(2)}) collective-permute-start(f32[16,768]{1,0:T(8,128)S(1)} %copy-done.24), channel_id=1, source_target_pairs={{16,0},{17,1},{18,2},{19,3},{20,4},{21,5},{22,6},{23,7},{24,8},{25... | collective-permute-start | bytes 147464 | tf_op jit(solution)/shard_map/cond/branch_1_fun/ppermute | solution.py:969
  194.7 6.8 %collective-permute-start.8 = (bf16[368,256]{1,0:T(8,128)(2,1)S(1)}, bf16[368,256]{1,0:T(8,128)(2,1)S(1)}, u32[]{:S(2)}, u32[]{:S(2)}) collective-permute-start(bf16[368,256]{1,0:T(8,128)(2,1)S(1)} %pad_maximum_fusion.6), channel_id=1, source_target_pairs={{0,4},{1,9},{2,6},{3,11},{4,0},{5,13},{6,2},{7,15},{8,12},{9,1},{1... | collective-permute-start | bytes 565256 | tf_op jit(solution)/shard_map/cond/branch_1_fun/ppermute | solution.py:761
  194.8 7.8 %copy-start.3 = (f32[512,768]{1,0:T(8,128)S(1)}, f32[512,768]{1,0:T(8,128)}, u32[]{:S(2)}) copy-start(f32[512,768]{1,0:T(8,128)} %get-tuple-element.111) | copy-start | bytes 4718596 | tf_op jit(solution)/shard_map/cond
  201.7 10.5 %collective-permute-start.9 = (bf16[720,256]{1,0:T(8,128)(2,1)S(1)}, bf16[720,256]{1,0:T(8,128)(2,1)S(1)}, u32[]{:S(2)}, u32[]{:S(2)}) collective-permute-start(bf16[720,256]{1,0:T(8,128)(2,1)S(1)} %pad_maximum_fusion.4), channel_id=1, source_target_pairs={{0,2},{1,17},{2,0},{3,19},{4,6},{5,21},{6,4},{7,23},{8,10},{9,25},... | collective-permute-start | bytes 1105928 | tf_op jit(solution)/shard_map/cond/branch_1_fun/ppermute | solution.py:761
  212.4 18.7 %collective-permute-start.11 = (bf16[1424,256]{1,0:T(8,128)(2,1)S(1)}, bf16[1424,256]{1,0:T(8,128)(2,1)S(1)}, u32[]{:S(2)}, u32[]{:S(2)}) collective-permute-start(bf16[1424,256]{1,0:T(8,128)(2,1)S(1)} %pad_maximum_fusion.1), channel_id=1, source_target_pairs={{0,16},{1,3},{2,18},{3,1},{4,20},{5,7},{6,22},{7,5},{8,24},{9,11},... | collective-permute-start | bytes 2187272 | tf_op jit(solution)/shard_map/cond/branch_1_fun/ppermute | solution.py:761
  231.3 3.6 %copy-start = (bf16[2816,256]{1,0:T(8,128)(2,1)}, bf16[2816,256]{1,0:T(8,128)(2,1)S(1)}, u32[]{:S(2)}) copy-start(bf16[2816,256]{1,0:T(8,128)(2,1)S(1)} %pad_maximum_fusion) | copy-start | bytes 4325380 | tf_op jit(solution)/shard_map/cond
  231.3 3.5 %collective-permute-start.12 = (bf16[2,1408,256]{2,1,0:T(8,128)(2,1)S(1)}, bf16[2,1408,256]{2,1,0:T(8,128)(2,1)}, u32[]{:S(2)}, u32[]{:S(2)}) collective-permute-start(bf16[2,1408,256]{2,1,0:T(8,128)(2,1)S(1)} %bitcast.43), channel_id=1, source_target_pairs={{0,1},{1,0},{2,3},{3,2},{4,5},{5,4},{6,7},{7,6},{8,9},{9,8},{10,11... | collective-permute-start | bytes 4325384 | tf_op jit(solution)/shard_map/cond/branch_1_fun/ppermute | solution.py:761
  231.4 3.4 %copy-start.13 = (bf16[16,256]{1,0:T(8,128)(2,1)}, bf16[16,256]{1,0:T(8,128)(2,1)S(1)}, u32[]{:S(2)}) copy-start(bf16[16,256]{1,0:T(8,128)(2,1)S(1)} %add_convert_fusion.10.own_e) | copy-start | bytes 24580 | tf_op jit(solution)/shard_map/cond
  231.4 2.8 %collective-permute-start.13 = (bf16[16,256]{1,0:T(8,128)(2,1)S(1)}, bf16[16,256]{1,0:T(8,128)(2,1)S(1)}, u32[]{:S(2)}, u32[]{:S(2)}) collective-permute-start(bf16[16,256]{1,0:T(8,128)(2,1)S(1)} %add_convert_fusion.10.own_e), channel_id=1, source_target_pairs={{0,1},{1,0},{2,3},{3,2},{4,5},{5,4},{6,7},{7,6},{8,9},{9,8},{10,11... | collective-permute-start | bytes 24584 | tf_op jit(solution)/shard_map/cond/branch_1_fun/ppermute | solution.py:761
  234.2 0.6 copy-start.18
Sparse Core Ops, SparseCore 0:
  18.7 60.5 all-gather.2
  95.1 145.2 all-reduce.7

commit v5 on v4

--- a/solution.py
+++ b/solution.py
@@ -308,7 +308,7 @@
             y = y + uf[lo:hi] * nn(c[lo:hi, :], ahead[i].astype(BF))
         if i < n - 1:
             y = y + ur[lo:hi] * nn(c[lo:hi, :], back[i].astype(BF))
-        y_o[lo:hi, :] = y
+        y_o[lo:hi, :] = y.astype(BF)
 
 
 def mix(flag, b, bt, c, uv, keep, rows, act, skip):
@@ -320,7 +320,7 @@
         in_specs=[SMEM_SPEC, full((T, 64)), full((64, T)), full((T, 64)), full((T, 128)), full((8, 128)),
                   pl.BlockSpec((GROUP // 2, 16, T), lambda i: (i, 0, 0)), blk, pl.BlockSpec((1, CH), lambda i: (0, i))],
         out_specs=blk,
-        out_shape=jax.ShapeDtypeStruct((T, INNER), F32),
+        out_shape=jax.ShapeDtypeStruct((T, INNER), BF),
         scratch_shapes=[pltpu.VMEM((T // Q, Q, Q), F32)],
         compiler_params=params(),
         name="mix",
@@ -334,7 +334,7 @@
 
 def gate_kernel(shard, y, wrc, c, st, normed, normt, rest, og, ogt, gain, no_o, gg_o, gm_o, dwg_o, dwo_o, ggain_o, acc_g, acc_o):
     step = pl.program_id(0)
-    mixed = y[...] + nn(c[...], st[...]) * seam_width(wrc)
+    mixed = y[...].astype(F32) + nn(c[...], st[...]) * seam_width(wrc)
     half = INNER // 2
     own = normed[...]
     gz = jnp.concatenate([nn(own, rest[:, :shard, :].reshape(D, half)), nn(own, rest[:, shard : 2 * shard, :].reshape(D, half))],
@@ -493,14 +493,14 @@
 
     x4 = x[...]
     g4 = g[...]
-    x32 = x4.astype(F32)
-    g32 = g4.astype(F32)
-    wide = nn(uv[...], jnp.concatenate([spread_of(step, slot) for slot in range(4)], axis=1))
-    uf, vf, ur, vr = [wide[:, CH * q : CH * (q + 1)] for q in range(4)]
+    wide = nn(uv[...], jnp.concatenate([spread_of(step, slot) for slot in (0, 2, 1, 3)], axis=1)).astype(BF)
+    x8 = jnp.concatenate([x4, x4], axis=1)
+    v8 = wide[:, 2 * CH :]
+    vx = v8 * x8
+    ug = wide[:, : 2 * CH] * jnp.concatenate([g4, g4], axis=1)
     keep_f = exact(keep[...], spread_of(step, 0, F32))
     keep_r = exact(keep[...], spread_of(step, 1, F32))
-    vxf, vxr = (vf * x32).astype(BF), (vr * x32).astype(BF)
-    ugf, ugr = (uf * g32).astype(BF), (ur * g32).astype(BF)
+    vxf, vxr, ugf, ugr = vx[:, :CH], vx[:, CH:], ug[:, :CH], ug[:, CH:]
     ahead, back = states(T, bt, vxf, vxr, keep_f, keep_r)
     lane = iota((Q, 128), 1)
     half = lane < HEADDIM
@@ -560,14 +560,12 @@
         into = jnp.concatenate([ahead[j].astype(BF) if j > 0 else zero, back[j].astype(BF) if j < n - 1 else zero], axis=1)
         outof = jnp.concatenate([dahead[j + 1].astype(BF) if j < n - 1 else zero, dback[j - 1].astype(BF) if j > 0 else zero],
                                 axis=1)
-        both_u = jnp.concatenate([ugf[lo:hi], ugr[lo:hi]], axis=1)
-        both_v = jnp.concatenate([vxf[lo:hi], vxr[lo:hi]], axis=1)
-        r_off.append((both_u.astype(F32) * nn(c[lo:hi, :], into)).astype(BF))
-        dv = nn(b[lo:hi, :], outof)
-        c_off.append((both_v.astype(F32) * dv).astype(BF))
-        dx_o[lo:hi, :] = dx + vf[lo:hi] * dv[:, :CH] + vr[lo:hi] * dv[:, CH:]
-        dc[lo:hi, :] += nt(both_u, into)
-        db[lo:hi, :] += nt(both_v, outof)
+        r_off.append(ug[lo:hi] * nn(c[lo:hi, :], into).astype(BF))
+        dv = v8[lo:hi] * nn(b[lo:hi, :], outof).astype(BF)
+        c_off.append(x8[lo:hi] * dv)
+        dx_o[lo:hi, :] = (dx + dv[:, :CH].astype(F32) + dv[:, CH:].astype(F32)).astype(BF)
+        dc[lo:hi, :] += nt(ug[lo:hi], into)
+        db[lo:hi, :] += nt(vx[lo:hi], outof)
         csum_o[lo:hi, :] += stat
     off = nn(jnp.concatenate(r_off + c_off, axis=0), gather)
     roff_o[...] += off[:T]
@@ -596,7 +594,7 @@
         in_specs=[SMEM_SPEC, full((T, 64)), full((64, T)), full((T, 64)), full((64, T)), full((T, 128)), full((8, 128)),
                   pl.BlockSpec((GROUP // 2, 16, T), lambda i: (i, 0, 0)), blk, blk],
         out_specs=[blk] + [full(v) for v in shapes[1:]],
-        out_shape=[jax.ShapeDtypeStruct(v, F32) for v in shapes],
+        out_shape=[jax.ShapeDtypeStruct(v, F32 if k else BF) for k, v in enumerate(shapes)],
         scratch_shapes=[pltpu.VMEM((n, Q, Q), F32), pltpu.VMEM((n, Q, Q), F32), pltpu.VMEM((T, 64), F32),
                         pltpu.VMEM((T, 64), F32)],
         compiler_params=params(),
@@ -677,7 +675,7 @@
         both = jnp.broadcast_to(jnp.sum(g32 * x32, axis=0, keepdims=True), (8, CH))
         both = lax.dot_general(both, heads, (((1,), (0,)), ((), ())), precision=HI, preferred_element_type=F32)
         small[SMALL_AT + 10 : SMALL_AT + 11, 0:128] += both[0:1, :]
-        total = through_conv(dx[...] + wq + skip[...] * g32)
+        total = through_conv(dx[...].astype(F32) + wq + skip[...] * g32)
         emit(total[HALO:], total[:HALO])
 
     @pl.when(step == NCH - 1)
@@ -925,11 +923,11 @@
     )(wg, wo, zx)
 
 
-def apart(flag, part, args):
+def apart(go, part, args):
     def nothing(v):
         return jax.tree.map(lambda o: jnp.zeros(o.shape, o.dtype), jax.eval_shape(part, v))
 
-    return lax.cond(flag[1] >= 1, part, nothing, args)
+    return lax.cond(go, part, nothing, args)
 
 
 def body(tokens, norm_gain, w_zx, w_bc, w_dt, conv_w, conv_b, dt_bias, a_log, d_skip, out_gain, w_out, doc_lengths, out_grad):
@@ -949,7 +947,7 @@
     lanes = lambda v: jnp.pad(v, (0, 128 - v.shape[0]))[None]
     skip = jnp.repeat(d_skip, HEADDIM)[None]
     rest = jnp.concatenate([w_zx[:, :half], w_zx[:, half:INNER], w_out], axis=0)
-    ready = (halo, flag, cw, cb, lanes(dt_bias), lanes(a_log), skip, norm_gain[None], out_gain[None], og.T)
+    ready = (halo, flag, cw, cb, lanes(dt_bias), lanes(a_log), skip, norm_gain[None], out_gain[None], og.T, doc_lengths[0, 0] >= 1)
     w1, ready, rest = gather_rows(mine, ready, rest)
 
     def finish(v):
@@ -979,7 +977,7 @@
         return (bo, grad_tokens) + tuple(late(flag, own, other, own_e, other_e))
 
     def rest_of(v):
-        w1, rest, (halo, flag, cw, cb, bias, alog, skip, gain_in, gain_out, ogt), tok, og = v
+        w1, rest, (halo, flag, cw, cb, bias, alog, skip, gain_in, gain_out, ogt, go), tok, og = v
         rest = lax.all_gather(rest, "dp", axis=0, tiled=False)
         if shard % 16:
             rest = jnp.concatenate([rest[:, :shard].reshape(D, D), rest[:, shard : 2 * shard].reshape(D, D),
@@ -992,7 +990,7 @@
         dwo, dwg = lax.psum((dwo, dwg), BOTH)
         args = (flag, b, bt, c, ct, uv, keep, rows, act, gm, z, pre, w1, cw, normt, nh, skip, bias, alog, tok, halo, ggain, og,
                 gain_in, no, gg, wrc, st_in, rest)
-        bo, grad_tokens, zx, g_bc, g_dt, g_cw, g_cb, g_dtb, g_alog, g_skip, g_og, g_ng = apart(flag, finish, args)
+        bo, grad_tokens, zx, g_bc, g_dt, g_cw, g_cb, g_dtb, g_alog, g_skip, g_og, g_ng = apart(go, finish, args)
         zx, g_wo = early(dwg, dwo, zx)
         return bo, grad_tokens, g_ng, zx, g_bc, g_dt.T, g_cw, g_cb, g_dtb, g_alog, g_skip, g_og, g_wo
 

time: 254 us -> 258 us (1.016)
  waiting for transfers between devices: 82.9 us -> 92.2 us
  starting transfers between devices: 27.9 us -> 24.9 us
    psum x1, waiting for transfers between devices: 0.74 us -> 19.2 us  [rest_of(): dwo, dwg = lax.psum((dwo, dwg), BOTH)]
    ppermute x18, waiting for transfers between devices: 79 us -> 69.9 us  [exchange(): lax.ppermute(v, BOTH, [(i, i ^ (mask_odd if i & 1 else mask_even)) for i...]
    ppermute x18, starting transfers between devices: 22.5 us -> 19.5 us  [exchange(): lax.ppermute(v, BOTH, [(i, i ^ (mask_odd if i & 1 else mask_even)) for i...]
  transfers between devices with their start and end apart: 22 -> 22, of which waited for: 16 -> 16; matrix products, arithmetic and copies ran while one was open for 10% -> 9% of each run, Pallas kernels for 31% -> 30%
where the time goes in v5:
time: 258 us; the launch traced here: 257 us
  Pallas kernels  100 us (39%)
  waiting for transfers between devices  92.2 us (36%)
  starting transfers between devices  24.9 us (10%)
  other arithmetic  15 us (6%)
  between operations  14.3 us (6%)
  local copies, waits for them, and re-layouts  10.1 us (4%)
    ppermute x18, waiting for transfers between devices, exchange(): lax.ppermute(v, BOTH, [(i, i ^ (mask_odd if i & 1 else mask_even)) for i...  69.9 us
    ppermute x18, starting transfers between devices, exchange(): lax.ppermute(v, BOTH, [(i, i ^ (mask_odd if i & 1 else mask_even)) for i...  19.5 us
    psum x1, waiting for transfers between devices, rest_of(): dwo, dwg = lax.psum((dwo, dwg), BOTH)  19.2 us
    pallas_call x1, Pallas kernels, unproject(): pl.pallas_call(functools.partial(unproject_kernel, T), grid=(NCH,), in_sp...  18.3 us
    pallas_call x1, Pallas kernels, unmix(): pl.pallas_call(functools.partial(unmix_kernel, T), grid=(INNER // CH,), i...  17.9 us
    pallas_call x1, Pallas kernels, gate(): pl.pallas_call(functools.partial(gate_kernel, rest.shape[1] // 4), grid=(...  15.5 us
    pallas_call x1, Pallas kernels, project(): pl.pallas_call(functools.partial(project_kernel, T), grid=(NCH,), in_spec...  14.6 us
    pallas_call x1, Pallas kernels, deferred(): pl.pallas_call(functools.partial(deferred_kernel, rest.shape[1] // 4), gr...  9.51 us
  transfers between devices with their start and end apart: 22, of which 16 were waited for; matrix products, arithmetic and copies ran while one was open for 9% of the time, Pallas kernels for 30%

profile of v5, /device:TPU:0, one launch (start us, length us, event | category | flops | bytes accessed | tf_op | source)
XLA Modules:
  0.0 257.4 jit_solution(8562103115955351235)
XLA Ops:
  7.2 1.0 slice.46
  8.3 0.9 concatenate.41
  9.2 4.1 %collective-permute-start.14 = (bf16[48,1792]{1,0:T(8,128)(2,1)S(1)}, bf16[48,1792]{1,0:T(8,128)(2,1)S(1)}, u32[]{:S(2)}, u32[]{:S(2)}) collective-permute-start(bf16[48,1792]{1,0:T(8,128)(2,1)S(1)} %concatenate.41), channel_id=1, source_target_pairs={{0,8},{1,3},{2,10},{3,1},{4,12},{5,7},{6,14},{7,5},{8,0},{9,11},{1... | collective-permute-start | bytes 516104 | tf_op jit(solution)/shard_map/ppermute | solution.py:759
  13.3 0.9 fusion.9
  14.2 1.6 pad_maximum_fusion.13
  15.9 2.6 %collective-permute-done.14 = bf16[48,1792]{1,0:T(8,128)(2,1)S(1)} collective-permute-done((bf16[48,1792]{1,0:T(8,128)(2,1)S(1)}, bf16[48,1792]{1,0:T(8,128)(2,1)S(1)}, u32[]{:S(2)}, u32[]{:S(2)}) %collective-permute-start.14) | collective-permute-done | bytes 172064 | tf_op jit(solution)/shard_map/ppermute | solution.py:759
  18.7 4.8 %collective-permute-start.15 = (bf16[2,48,1792]{2,1,0:T(8,128)(2,1)S(1)}, bf16[2,48,1792]{2,1,0:T(8,128)(2,1)S(1)}, u32[]{:S(2)}, u32[]{:S(2)}) collective-permute-start(bf16[2,48,1792]{2,1,0:T(8,128)(2,1)S(1)} %pad_maximum_fusion.12), channel_id=1, source_target_pairs={{0,4},{1,9},{2,6},{3,11},{4,0},{5,13},{6,2},{7,15},{8,12},{9,1},{1... | collective-permute-start | bytes 1032200 | tf_op jit(solution)/shard_map/ppermute | solution.py:759
  24.1 4.0 %collective-permute-start.16 = (bf16[16,768]{1,0:T(8,128)(2,1)}, bf16[16,768]{1,0:T(8,128)(2,1)}, u32[]{:S(2)}, u32[]{:S(2)}) collective-permute-start(bf16[16,768]{1,0:T(8,128)(2,1)} %slice_bitcast_fusion), channel_id=1, source_target_pairs={{0,16},{1,17},{2,18},{3,19},{4,20},{5,21},{6,22},{7,23},{8,24},{9,... | collective-permute-start | bytes 73736 | tf_op jit(solution)/shard_map/ppermute | solution.py:942
  31.3 1.2 copy.28
  33.8 1.6 collective-permute-start.17
  35.4 9.9 %collective-permute-done.17 = bf16[2,2,48,1792]{3,2,0,1:T(8,128)(2,1)S(1)} collective-permute-done((bf16[2,2,48,1792]{3,2,0,1:T(8,128)(2,1)S(1)}, bf16[2,2,48,1792]{3,2,0,1:T(8,128)(2,1)S(1)}, u32[]{:S(2)}, u32[]{:S(2)}) %collective-permute-start.17) | collective-permute-done | bytes 688160 | tf_op jit(solution)/shard_map/ppermute | solution.py:759
  45.5 1.2 copy.29
  46.7 3.3 %collective-permute-done.18 = bf16[2,2,2,48,1792]{4,3,2,0,1:T(8,128)(2,1)S(1)} collective-permute-done((bf16[2,2,2,48,1792]{4,3,2,0,1:T(8,128)(2,1)}, bf16[2,2,2,48,1792]{4,3,2,0,1:T(8,128)(2,1)S(1)}, u32[]{:S(2)}, u32[]{:S(2)}) %collective-permute-start.18) | collective-permute-done | bytes 1376288 | tf_op jit(solution)/shard_map/ppermute | solution.py:759
  51.0 14.6 %project.1 = (bf16[512,768]{1,0:T(8,128)(2,1)}, bf16[768,512]{1,0:T(8,128)(2,1)}, bf16[16,768]{1,0:T(8,128)(2,1)}, bf16[528,1792]{1,0:T(8,128)(2,1)}, bf16[512,1...) custom-call(s32[6]{0:T(128)} %pad_add_fusion.flag, ...), custom_call_target="tpu_custom_call" | custom-call | tf_op jit(solution)/shard_map/project/pallas_call | solution.py:215
  65.7 1.5 collective-permute-start.19
  67.2 9.1 %mix.1.y = bf16[512,1536]{1,0:T(8,128)(2,1)} custom-call(s32[6]{0:T(128)} %pad_add_fusion.flag, bf16[512,64]{1,0:T(8,128)(2,1)} %get-tuple-element.199.b, bf16[64,512]{1,0:T(8,128)(2,1)S(1)} %get-tuple-element.200.bt, bf16[512,64]{1,0:T(8,128)(2,1)S(1)} %get-tuple-element.201.c, bf16[512,128]{1,0:T(8,128)(2,1)} %get-tuple-element.203.uv, ...), custom_call_target="tpu_custom_call" | custom-call | tf_op jit(solution)/shard_map/mix/pallas_call | solution.py:317
  76.3 3.1 %all-gather.3.cloned.1.call-done = bf16[3072,768]{1,0:T(8,128)(2,1)} async-done(((bf16[192,768]{1,0:T(8,128)(2,1)}), bf16[3072,768]{1,0:T(8,128)(2,1)}) %all-gather.3.cloned.1.call-update) | async-done | bytes 4718608 | tf_op jit(solution)/shard_map/all_gather | solution.py:981
  79.4 15.5 %gate.1 = (bf16[512,1536]{1,0:T(8,128)(2,1)}, bf16[512,1536]{1,0:T(8,128)(2,1)}, bf16[512,1536]{1,0:T(8,128)(2,1)}, bf16[768,1536]{1,0:T(8,128)(2,1)}, bf16[768,1536]{1,0:T(8,128)(2,1)}, /*index=5*/f32[1,1536]{1,0:T(1,128)}) custom-call(bf16[512,1536]{1,0:T(8,128)(2,1)} %mix.1.y, bf16[512,128]{1,0:T(8,128)(2,1)} %get-tuple-element.208.wrc, ...), custom_call_target="tpu_custom_call" | custom-call | tf_op jit(solution)/shard_map/gate/pallas_call | solution.py:378
  94.9 130.2 %conditional.1 = (f32[768,3072]{1,0:T(8,128)}, f32[768,128]{1,0:T(8,128)}, f32[48,768]{1,0:T(8,128)}, f32[4,1664]{1,0:T(4,128)}, f32[1664]{0:T(1024)}, /*index=5...) conditional(s32[]{:T(128)} %convert_element_type.147, () %tuple.27, ...), branch_computations={%region_0.1_spmd, %region_1.4_spmd} | conditional | flops 24520756 | bytes 71272112 | solution.py:930
  95.1 4.3 %side.1 = (f32[512,64]{1,0:T(8,128)}, f32[512,128]{1,0:T(8,128)}, bf16[64,1536]{1,0:T(8,128)(2,1)}) custom-call(s32[6]{0:T(128)} %get-tuple-element.60.flag, bf16[512,1536]{1,0:T(8,128)(2,1)} %get-tuple-element.69.g.gm, bf16[512,128]{1,0:T(8,128)(2,1)} %get-tuple-element.74.wrc, bf16[512,64]{1,0:T(8,128)(2,1)} %get-tuple-element.63.c, ...), custom_call_target="tpu_custom_call" | custom-call | tf_op jit(solution)/shard_map/cond/branch_1_fun/side/pallas_call | solution.py:416
  99.4 1.5 collective-permute-start
  101.0 17.9 %unmix.1 = (bf16[512,1536]{1,0:T(8,128)(2,1)}, f32[128,512]{1,0:T(8,128)}, f32[512,128]{1,0:T(8,128)}, f32[512,128]{1,0:T(8,128)}, f32[512,128]{1,0:T(8,128)}, /*index=5*/f32[8,128]{1,0:T(8,128)}, f32[512,128]{1,0:T(8,128)}) custom-call(s32[6]{0:T(128)} %get-tuple-element.60.flag, bf16[512,64]{1,0:T(8,128)(2,1)} %get-tuple-element.61.b, ...), custom_call_target="tpu_custom_call" | custom-call | tf_op jit(solution)/shard_map/cond/branch_1_fun/unmix/pallas_call | solution.py:591
  118.9 18.3 %unproject.1 = (bf16[7,384,256]{2,1,0:T(8,128)(2,1)}, bf16[7,384,256]{2,1,0:T(8,128)(2,1)}, bf16[512,1792]{1,0:T(8,128)(2,1)}, bf16[16,1792]{1,0:T(8,128)(2,1)},...) custom-call(s32[6]{0:T(128)} %get-tuple-element.60.flag, bf16[512,1536]{1,0:T(8,128)(2,1)} %get-tuple-element.70.dx, ...), custom_call_target="tpu_custom_call" | custom-call | tf_op jit(solution)/shard_map/cond/branch_1_fun/unproject/pallas_call | solution.py:731
  137.7 3.0 %collective-permute-done.2 = bf16[64,256]{1,0:T(8,128)(2,1)} collective-permute-done((bf16[64,256]{1,0:T(8,128)(2,1)}, bf16[64,256]{1,0:T(8,128)(2,1)}, u32[]{:S(2)}, u32[]{:S(2)}) %collective-permute-start.2) | collective-permute-done | bytes 32800 | tf_op jit(solution)/shard_map/cond/branch_1_fun/ppermute | solution.py:759
  140.7 1.4 broadcast_select_fusion.8
  142.1 2.9 %add_convert_fusion = (bf16[7,192,256]{2,1,0:T(8,128)(2,1)S(1)}, bf16[7,192,256]{2,1,0:T(8,128)(2,1)}) fusion(bf16[7,384,256]{2,1,0:T(8,128)(2,1)} %collective-permute-done.1, s32[]{:T(128)S(6)} %select_n.175, bf16[7,384,256]{2,1,0:T(8,128)(2,1)} %get-tuple-element.91, s32[]{:T(128)S(6)} %select_n.171), kind=kLoop, calls=%fused_computation.10 | loop fusion | flops 2752512 | bytes 4128776 | tf_op jit(solution)/shard_map/cond/branch_1_fun/convert_element_type | solution.py:813
  145.1 0.9 pad_maximum_fusion.2
  146.5 9.5 %deferred.1 = (bf16[512,768]{1,0:T(8,128)(2,1)}, f32[512,768]{1,0:T(8,128)}, f32[16,768]{1,0:T(8,128)}, bf16[16,256]{1,0:T(8,128)(2,1)}) custom-call(bf16[512,1792]{1,0:T(8,128)(2,1)} %get-tuple-element.98.dpl, bf16[16,1792]{1,0:T(8,128)(2,1)} %get-tuple-element.99.dph, bf16[768,1792]{1,0:T(8,128)(2,1)S(1)} %get-tuple-element.100.w1, ...), custom_call_target="tpu_custom_call" | custom-call | tf_op jit(solution)/shard_map/cond/branch_1_fun/deferred/pallas_call | solution.py:462
  156.1 3.1 %collective-permute-done.3 = bf16[1408,256]{1,0:T(8,128)(2,1)} collective-permute-done((bf16[1408,256]{1,0:T(8,128)(2,1)}, bf16[1408,256]{1,0:T(8,128)(2,1)}, u32[]{:S(2)}, u32[]{:S(2)}) %collective-permute-start.3) | collective-permute-done | bytes 720928 | tf_op jit(solution)/shard_map/cond/branch_1_fun/ppermute | solution.py:759
  159.2 2.4 add_convert_fusion.3
  161.7 7.4 %collective-permute-done.4 = bf16[704,256]{1,0:T(8,128)(2,1)S(1)} collective-permute-done((bf16[704,256]{1,0:T(8,128)(2,1)S(1)}, bf16[704,256]{1,0:T(8,128)(2,1)S(1)}, u32[]{:S(2)}, u32[]{:S(2)}) %collective-permute-start.4) | collective-permute-done | bytes 360480 | tf_op jit(solution)/shard_map/cond/branch_1_fun/ppermute | solution.py:759
  169.2 1.6 collective-permute-start.5
  170.8 5.0 %collective-permute-done.5 = bf16[352,256]{1,0:T(8,128)(2,1)S(1)} collective-permute-done((bf16[352,256]{1,0:T(8,128)(2,1)S(1)}, bf16[352,256]{1,0:T(8,128)(2,1)S(1)}, u32[]{:S(2)}, u32[]{:S(2)}) %collective-permute-start.5) | collective-permute-done | bytes 180256 | tf_op jit(solution)/shard_map/cond/branch_1_fun/ppermute | solution.py:759
  176.0 6.8 %collective-permute-done.6 = bf16[176,256]{1,0:T(8,128)(2,1)S(1)} collective-permute-done((bf16[176,256]{1,0:T(8,128)(2,1)S(1)}, bf16[176,256]{1,0:T(8,128)(2,1)S(1)}, u32[]{:S(2)}, u32[]{:S(2)}) %collective-permute-start.6) | collective-permute-done | bytes 90144 | tf_op jit(solution)/shard_map/cond/branch_1_fun/ppermute | solution.py:759
  183.3 1.3 collective-permute-start.10
  184.6 6.5 %collective-permute-done.7 = bf16[192,256]{1,0:T(8,128)(2,1)S(1)} collective-permute-done((bf16[192,256]{1,0:T(8,128)(2,1)S(1)}, bf16[192,256]{1,0:T(8,128)(2,1)S(1)}, u32[]{:S(2)}, u32[]{:S(2)}) %collective-permute-start.7) | collective-permute-done | bytes 98336 | tf_op jit(solution)/shard_map/cond/branch_1_fun/ppermute | solution.py:759
  191.3 1.9 fusion
  193.2 3.6 %collective-permute-done.8 = bf16[368,256]{1,0:T(8,128)(2,1)S(1)} collective-permute-done((bf16[368,256]{1,0:T(8,128)(2,1)S(1)}, bf16[368,256]{1,0:T(8,128)(2,1)S(1)}, u32[]{:S(2)}, u32[]{:S(2)}) %collective-permute-start.8) | collective-permute-done | bytes 188448 | tf_op jit(solution)/shard_map/cond/branch_1_fun/ppermute | solution.py:759
  197.0 1.0 collective-permute-start.9
  198.0 1.3 fusion.4
  199.3 5.2 %collective-permute-done.9 = bf16[720,256]{1,0:T(8,128)(2,1)S(1)} collective-permute-done((bf16[720,256]{1,0:T(8,128)(2,1)S(1)}, bf16[720,256]{1,0:T(8,128)(2,1)S(1)}, u32[]{:S(2)}, u32[]{:S(2)}) %collective-permute-start.9) | collective-permute-done | bytes 368672 | tf_op jit(solution)/shard_map/cond/branch_1_fun/ppermute | solution.py:759
  204.8 1.2 collective-permute-start.11
  206.0 10.2 %collective-permute-done.11 = bf16[1424,256]{1,0:T(8,128)(2,1)S(1)} collective-permute-done((bf16[1424,256]{1,0:T(8,128)(2,1)S(1)}, bf16[1424,256]{1,0:T(8,128)(2,1)S(1)}, u32[]{:S(2)}, u32[]{:S(2)}) %collective-permute-start.11) | collective-permute-done | bytes 729120 | tf_op jit(solution)/shard_map/cond/branch_1_fun/ppermute | solution.py:759
  217.1 2.4 collective-permute-done.13.other_e
  219.5 0.7 collective-permute-done.12.other.other_l.other_s
  220.2 4.8 %late.1 = (f32[768,3072]{1,0:T(8,128)}, f32[768,128]{1,0:T(8,128)}, f32[48,768]{1,0:T(8,128)}, f32[4,1664]{1,0:T(4,128)}, f32[1664]{0:T(1024)}, /*index=5*/f32[4...) custom-call(s32[6]{0:T(128)S(1)} %copy-done.16, bf16[2,1408,256]{2,1,0:T(8,128)(2,1)} %bitcast.45, ...), custom_call_target="tpu_custom_call" | custom-call | tf_op jit(solution)/shard_map/cond/branch_1_fun/late/pallas_call | solution.py:895
  225.0 19.2 %all-reduce.8.cloned.1.call-done = (bf16[768,1536]{1,0:T(8,128)(2,1)}, bf16[768,1536]{1,0:T(8,128)(2,1)}) async-done(((bf16[768,1536]{1,0:T(8,128)(2,1)}, bf16[768,1536]{1,0:T(8,128)(2,1)}), (bf16[768,1536]{1,0:T(8,128)(2,1)}, bf16[768,1536]{1,0:T(8,128)(2,1)})) %all-reduce.8.cloned.1.call-update) | async-done | bytes 4718608 | tf_op jit(solution)/shard_map/psum | solution.py:990
  244.2 6.3 %early.1 = (f32[768,3072]{1,0:T(8,128)}, f32[1536,768]{1,0:T(8,128)}) custom-call(bf16[768,1536]{1,0:T(8,128)(2,1)} %get-tuple-element.269.wg, bf16[768,1536]{1,0:T(8,128)(2,1)} %get-tuple-element.270.wo, f32[768,3072]{1,0:T(8,128)} %get-tuple-element.227.zx), custom_call_target="tpu_custom_call", output_to_operand_aliasing={{0}: (2, {})} | custom-call | tf_op jit(solution)/shard_map/early/pallas_call | solution.py:914
  (113 shorter events, 9.8 us)
Async XLA Ops:
  7.2 16.3 %copy-start.1 = (bf16[1,512,768]{2,1,0:T(8,128)(2,1)S(1)}, bf16[1,512,768]{2,1,0:T(8,128)(2,1)}, u32[]{:S(2)}) copy-start(bf16[1,512,768]{2,1,0:T(8,128)(2,1)} %param.16) | copy-start | bytes 2359300
  7.2 72.2 %all-gather.3.cloned.1.call-start = ((), (), s32[]{:S(2)}) async-start(), calls=%async_computation | async-start | bytes 5013504 | tf_op jit(solution)/shard_map/all_gather | solution.py:981
  8.2 19.9 %copy-start.20 = (f32[768]{0:T(1024)S(1)}, f32[768]{0:T(1024)}, u32[]{:S(2)}) copy-start(f32[768]{0:T(1024)} %param.17) | copy-start | bytes 9220
  8.2 20.4 %copy-start.17 = (f32[1536]{0:T(1024)S(1)}, f32[1536]{0:T(1024)}, u32[]{:S(2)}) copy-start(f32[1536]{0:T(1024)} %param.26) | copy-start | bytes 18436
  8.2 21.0 %copy-start.18 = (f32[1664]{0:T(1024)S(1)}, f32[1664]{0:T(1024)}, u32[]{:S(2)}) copy-start(f32[1664]{0:T(1024)} %param.22) | copy-start | bytes 19972
  8.3 21.6 %copy-start.21 = (f32[24]{0:T(128)S(1)}, f32[24]{0:T(128)}, u32[]{:S(2)}) copy-start(f32[24]{0:T(128)} %param.25) | copy-start | bytes 292
  8.3 22.4 %copy-start.15 = (f32[4,1664]{1,0:T(4,128)S(1)}, f32[4,1664]{1,0:T(4,128)}, u32[]{:S(2)}) copy-start(f32[4,1664]{1,0:T(4,128)} %param.21) | copy-start | bytes 79876
  8.3 23.0 %copy-start.6 = (bf16[1,512,768]{2,1,0:T(8,128)(2,1)S(1)}, bf16[1,512,768]{2,1,0:T(8,128)(2,1)}, u32[]{:S(2)}) copy-start(bf16[1,512,768]{2,1,0:T(8,128)(2,1)} %param.29) | copy-start | bytes 2359300
  9.2 9.3 %collective-permute-start.14 = (bf16[48,1792]{1,0:T(8,128)(2,1)S(1)}, bf16[48,1792]{1,0:T(8,128)(2,1)S(1)}, u32[]{:S(2)}, u32[]{:S(2)}) collective-permute-start(bf16[48,1792]{1,0:T(8,128)(2,1)S(1)} %concatenate.41), channel_id=1, source_target_pairs={{0,8},{1,3},{2,10},{3,1},{4,12},{5,7},{6,14},{7,5},{8,0},{9,11},{1... | collective-permute-start | bytes 516104 | tf_op jit(solution)/shard_map/ppermute | solution.py:759
  15.9 16.5 %copy-start.22 = (s32[1,4]{1,0:T(1,128)S(1)}, s32[1,4]{1,0:T(1,128)}, u32[]{:S(2)}) copy-start(s32[1,4]{1,0:T(1,128)} %param.28) | copy-start | bytes 52
  15.9 17.2 %copy-start.23 = (f32[48]{0:T(128)S(1)}, f32[48]{0:T(128)}, u32[]{:S(2)}) copy-start(f32[48]{0:T(128)} %param.24) | copy-start | bytes 580
  15.9 17.2 %copy-start.24 = (f32[48]{0:T(128)S(1)}, f32[48]{0:T(128)}, u32[]{:S(2)}) copy-start(f32[48]{0:T(128)} %param.23) | copy-start | bytes 580
  18.6 225.6 %all-reduce.8.cloned.1.call-start = ((), (), s32[]{:S(2)}) async-start(), calls=%async_computation.1 | async-start | bytes 9437184 | tf_op jit(solution)/shard_map/psum | solution.py:990
  18.7 15.0 %collective-permute-start.15 = (bf16[2,48,1792]{2,1,0:T(8,128)(2,1)S(1)}, bf16[2,48,1792]{2,1,0:T(8,128)(2,1)S(1)}, u32[]{:S(2)}, u32[]{:S(2)}) collective-permute-start(bf16[2,48,1792]{2,1,0:T(8,128)(2,1)S(1)} %pad_maximum_fusion.12), channel_id=1, source_target_pairs={{0,4},{1,9},{2,6},{3,11},{4,0},{5,13},{6,2},{7,15},{8,12},{9,1},{1... | collective-permute-start | bytes 1032200 | tf_op jit(solution)/shard_map/ppermute | solution.py:759
  24.1 9.7 %collective-permute-start.16 = (bf16[16,768]{1,0:T(8,128)(2,1)}, bf16[16,768]{1,0:T(8,128)(2,1)}, u32[]{:S(2)}, u32[]{:S(2)}) collective-permute-start(bf16[16,768]{1,0:T(8,128)(2,1)} %slice_bitcast_fusion), channel_id=1, source_target_pairs={{0,16},{1,17},{2,18},{3,19},{4,20},{5,21},{6,22},{7,23},{8,24},{9,... | collective-permute-start | bytes 73736 | tf_op jit(solution)/shard_map/ppermute | solution.py:942
  33.8 11.5 %collective-permute-start.17 = (bf16[2,2,48,1792]{3,2,0,1:T(8,128)(2,1)S(1)}, bf16[2,2,48,1792]{3,2,0,1:T(8,128)(2,1)S(1)}, u32[]{:S(2)}, u32[]{:S(2)}) collective-permute-start(bf16[2,2,48,1792]{3,2,0,1:T(8,128)(2,1)S(1)} %pad_maximum_fusion.11), channel_id=1, source_target_pairs={{0,2},{1,5},{2,0},{3,7},{4,6},{5,1},{6,4},{7,3},{8,10},{9,13},{10,... | collective-permute-start | bytes 2064392 | tf_op jit(solution)/shard_map/ppermute | solution.py:759
  46.7 3.3 %collective-permute-start.18 = (bf16[2,2,2,48,1792]{4,3,2,0,1:T(8,128)(2,1)}, bf16[2,2,2,48,1792]{4,3,2,0,1:T(8,128)(2,1)S(1)}, u32[]{:S(2)}, u32[]{:S(2)}) collective-permute-start(bf16[2,2,2,48,1792]{4,3,2,0,1:T(8,128)(2,1)} %copy.29), channel_id=1, source_target_pairs={{0,1},{1,0},{2,3},{3,2},{4,5},{5,4},{6,7},{7,6},{8,9},{9,8},{10,11... | collective-permute-start | bytes 4128776 | tf_op jit(solution)/shard_map/ppermute | solution.py:759
  65.6 10.6 %copy-start.4 = (f32[12,16,512]{2,1,0:T(8,128)}, f32[12,16,512]{2,1,0:T(8,128)S(1)}, u32[]{:S(2)}) copy-start(f32[12,16,512]{2,1,0:T(8,128)S(1)} %get-tuple-element.205.rows) | copy-start | bytes 1179652
  65.6 10.6 %copy-start.7 = (bf16[512,64]{1,0:T(8,128)(2,1)}, bf16[512,64]{1,0:T(8,128)(2,1)S(1)}, u32[]{:S(2)}) copy-start(bf16[512,64]{1,0:T(8,128)(2,1)S(1)} %get-tuple-element.201.c) | copy-start | bytes 196612
  65.6 10.6 %copy-start.9 = (bf16[64,512]{1,0:T(8,128)(2,1)}, bf16[64,512]{1,0:T(8,128)(2,1)S(1)}, u32[]{:S(2)}) copy-start(bf16[64,512]{1,0:T(8,128)(2,1)S(1)} %get-tuple-element.200.bt) | copy-start | bytes 196612
  65.7 10.6 %collective-permute-start.19 = (bf16[64,1536]{1,0:T(8,128)(2,1)}, bf16[64,1536]{1,0:T(8,128)(2,1)}, u32[]{:S(2)}, u32[]{:S(2)}) collective-permute-start(bf16[64,1536]{1,0:T(8,128)(2,1)} %get-tuple-element.209), channel_id=1, source_target_pairs={{0,16},{1,17},{2,18},{3,19},{4,20},{5,21},{6,22},{7,23},{8,24},{9,... | collective-permute-start | bytes 589832 | tf_op jit(solution)/shard_map/ppermute | solution.py:759
  95.1 5.9 %copy-start.5 = (f32[12,16,512]{2,1,0:T(8,128)S(1)}, f32[12,16,512]{2,1,0:T(8,128)}, u32[]{:S(2)}) copy-start(f32[12,16,512]{2,1,0:T(8,128)} %get-tuple-element.67.rows) | copy-start | bytes 1179652 | tf_op jit(solution)/shard_map/cond
  95.1 5.9 %copy-start.8 = (bf16[512,64]{1,0:T(8,128)(2,1)S(1)}, bf16[512,64]{1,0:T(8,128)(2,1)}, u32[]{:S(2)}) copy-start(bf16[512,64]{1,0:T(8,128)(2,1)} %get-tuple-element.63.c) | copy-start | bytes 196612 | tf_op jit(solution)/shard_map/cond
  95.1 5.9 %copy-start.10 = (bf16[64,512]{1,0:T(8,128)(2,1)S(1)}, bf16[64,512]{1,0:T(8,128)(2,1)}, u32[]{:S(2)}) copy-start(bf16[64,512]{1,0:T(8,128)(2,1)} %get-tuple-element.62.bt) | copy-start | bytes 196612 | tf_op jit(solution)/shard_map/cond
  99.4 19.5 %collective-permute-start = (bf16[64,1536]{1,0:T(8,128)(2,1)}, bf16[64,1536]{1,0:T(8,128)(2,1)}, u32[]{:S(2)}, u32[]{:S(2)}) collective-permute-start(bf16[64,1536]{1,0:T(8,128)(2,1)} %get-tuple-element.76), channel_id=1, source_target_pairs={{0,16},{1,17},{2,18},{3,19},{4,20},{5,21},{6,22},{7,23},{8,24},{9,... | collective-permute-start | bytes 589832 | tf_op jit(solution)/shard_map/cond/branch_1_fun/ppermute | solution.py:759
  137.2 5.0 %collective-permute-start.1 = (bf16[7,384,256]{2,1,0:T(8,128)(2,1)}, bf16[7,384,256]{2,1,0:T(8,128)(2,1)}, u32[]{:S(2)}, u32[]{:S(2)}) collective-permute-start(bf16[7,384,256]{2,1,0:T(8,128)(2,1)} %get-tuple-element.92), channel_id=1, source_target_pairs={{0,1},{1,0},{2,3},{3,2},{4,5},{5,4},{6,7},{7,6},{8,9},{9,8},{10,11... | collective-permute-start | bytes 4128776 | tf_op jit(solution)/shard_map/cond/branch_1_fun/ppermute | solution.py:759
  137.2 3.5 %collective-permute-start.2 = (bf16[64,256]{1,0:T(8,128)(2,1)}, bf16[64,256]{1,0:T(8,128)(2,1)}, u32[]{:S(2)}, u32[]{:S(2)}) collective-permute-start(bf16[64,256]{1,0:T(8,128)(2,1)} %get-tuple-element.94), channel_id=1, source_target_pairs={{0,1},{1,0},{2,3},{3,2},{4,5},{5,4},{6,7},{7,6},{8,9},{9,8},{10,11... | collective-permute-start | bytes 98312 | tf_op jit(solution)/shard_map/cond/branch_1_fun/ppermute | solution.py:759
  146.0 13.2 %collective-permute-start.3 = (bf16[1408,256]{1,0:T(8,128)(2,1)}, bf16[1408,256]{1,0:T(8,128)(2,1)}, u32[]{:S(2)}, u32[]{:S(2)}) collective-permute-start(bf16[1408,256]{1,0:T(8,128)(2,1)} %pad_maximum_fusion.2), channel_id=1, source_target_pairs={{0,16},{1,3},{2,18},{3,1},{4,20},{5,7},{6,22},{7,5},{8,24},{9,11},... | collective-permute-start | bytes 2162696 | tf_op jit(solution)/shard_map/cond/branch_1_fun/ppermute | solution.py:759
  146.5 12.6 %copy-start.11 = (bf16[64,256]{1,0:T(8,128)(2,1)S(1)}, bf16[64,256]{1,0:T(8,128)(2,1)}, u32[]{:S(2)}) copy-start(bf16[64,256]{1,0:T(8,128)(2,1)} %get-tuple-element.286) | copy-start | bytes 98308 | tf_op jit(solution)/shard_map/cond
  159.1 23.8 %copy-start.12 = (bf16[16,256]{1,0:T(8,128)(2,1)S(1)}, bf16[16,256]{1,0:T(8,128)(2,1)}, u32[]{:S(2)}) copy-start(bf16[16,256]{1,0:T(8,128)(2,1)} %get-tuple-element.108) | copy-start | bytes 24580 | tf_op jit(solution)/shard_map/cond
  159.1 23.9 %copy-start.2 = (bf16[512,768]{0,1:T(8,128)(2,1)S(1)}, bf16[512,768]{0,1:T(8,128)(2,1)}, u32[]{:S(2)}) copy-start(bf16[512,768]{0,1:T(8,128)(2,1)} %get-tuple-element.265) | copy-start | bytes 2359300 | tf_op jit(solution)/shard_map/cond
  161.6 7.5 %collective-permute-start.4 = (bf16[704,256]{1,0:T(8,128)(2,1)S(1)}, bf16[704,256]{1,0:T(8,128)(2,1)S(1)}, u32[]{:S(2)}, u32[]{:S(2)}) collective-permute-start(bf16[704,256]{1,0:T(8,128)(2,1)S(1)} %get-tuple-element.107), channel_id=1, source_target_pairs={{0,2},{1,17},{2,0},{3,19},{4,6},{5,21},{6,4},{7,23},{8,10},{9,25},... | collective-permute-start | bytes 1081352 | tf_op jit(solution)/shard_map/cond/branch_1_fun/ppermute | solution.py:759
  169.1 14.2 %copy-start.14 = (f32[1,768]{1,0:T(1,128)S(1)}, f32[1,768]{1,0:T(1,128)}, u32[]{:S(2)}) copy-start(f32[1,768]{1,0:T(1,128)} %get-tuple-element.113) | copy-start | bytes 9220 | tf_op jit(solution)/shard_map/cond
  169.1 14.3 %copy-start.25 = (f32[16,768]{1,0:T(8,128)S(1)}, f32[16,768]{1,0:T(8,128)}, u32[]{:S(2)}) copy-start(f32[16,768]{1,0:T(8,128)} %get-tuple-element.112) | copy-start | bytes 147460 | tf_op jit(solution)/shard_map/cond
  169.2 6.5 %collective-permute-start.5 = (bf16[352,256]{1,0:T(8,128)(2,1)S(1)}, bf16[352,256]{1,0:T(8,128)(2,1)S(1)}, u32[]{:S(2)}, u32[]{:S(2)}) collective-permute-start(bf16[352,256]{1,0:T(8,128)(2,1)S(1)} %get-tuple-element.280), channel_id=1, source_target_pairs={{0,4},{1,9},{2,6},{3,11},{4,0},{5,13},{6,2},{7,15},{8,12},{9,1},{1... | collective-permute-start | bytes 540680 | tf_op jit(solution)/shard_map/cond/branch_1_fun/ppermute | solution.py:759
  175.7 7.1 %collective-permute-start.6 = (bf16[176,256]{1,0:T(8,128)(2,1)S(1)}, bf16[176,256]{1,0:T(8,128)(2,1)S(1)}, u32[]{:S(2)}, u32[]{:S(2)}) collective-permute-start(bf16[176,256]{1,0:T(8,128)(2,1)S(1)} %add_convert_fusion.7), channel_id=1, source_target_pairs={{0,8},{1,5},{2,10},{3,7},{4,12},{5,1},{6,14},{7,3},{8,0},{9,13},{1... | collective-permute-start | bytes 270344 | tf_op jit(solution)/shard_map/cond/branch_1_fun/ppermute | solution.py:759
  182.9 8.2 %collective-permute-start.7 = (bf16[192,256]{1,0:T(8,128)(2,1)S(1)}, bf16[192,256]{1,0:T(8,128)(2,1)S(1)}, u32[]{:S(2)}, u32[]{:S(2)}) collective-permute-start(bf16[192,256]{1,0:T(8,128)(2,1)S(1)} %pad_maximum_fusion.8), channel_id=1, source_target_pairs={{0,8},{1,5},{2,10},{3,7},{4,12},{5,1},{6,14},{7,3},{8,0},{9,13},{1... | collective-permute-start | bytes 294920 | tf_op jit(solution)/shard_map/cond/branch_1_fun/ppermute | solution.py:759
  183.3 8.0 %collective-permute-start.10 = (f32[16,768]{1,0:T(8,128)S(1)}, f32[16,768]{1,0:T(8,128)S(1)}, u32[]{:S(2)}, u32[]{:S(2)}) collective-permute-start(f32[16,768]{1,0:T(8,128)S(1)} %copy-done.25), channel_id=1, source_target_pairs={{16,0},{17,1},{18,2},{19,3},{20,4},{21,5},{22,6},{23,7},{24,8},{25... | collective-permute-start | bytes 147464 | tf_op jit(solution)/shard_map/cond/branch_1_fun/ppermute | solution.py:967
  191.2 5.6 %collective-permute-start.8 = (bf16[368,256]{1,0:T(8,128)(2,1)S(1)}, bf16[368,256]{1,0:T(8,128)(2,1)S(1)}, u32[]{:S(2)}, u32[]{:S(2)}) collective-permute-start(bf16[368,256]{1,0:T(8,128)(2,1)S(1)} %pad_maximum_fusion.6), channel_id=1, source_target_pairs={{0,4},{1,9},{2,6},{3,11},{4,0},{5,13},{6,2},{7,15},{8,12},{9,1},{1... | collective-permute-start | bytes 565256 | tf_op jit(solution)/shard_map/cond/branch_1_fun/ppermute | solution.py:759
  191.3 6.7 %copy-start.3 = (f32[512,768]{1,0:T(8,128)S(1)}, f32[512,768]{1,0:T(8,128)}, u32[]{:S(2)}) copy-start(f32[512,768]{1,0:T(8,128)} %get-tuple-element.111) | copy-start | bytes 4718596 | tf_op jit(solution)/shard_map/cond
  197.0 7.6 %collective-permute-start.9 = (bf16[720,256]{1,0:T(8,128)(2,1)S(1)}, bf16[720,256]{1,0:T(8,128)(2,1)S(1)}, u32[]{:S(2)}, u32[]{:S(2)}) collective-permute-start(bf16[720,256]{1,0:T(8,128)(2,1)S(1)} %pad_maximum_fusion.4), channel_id=1, source_target_pairs={{0,2},{1,17},{2,0},{3,19},{4,6},{5,21},{6,4},{7,23},{8,10},{9,25},... | collective-permute-start | bytes 1105928 | tf_op jit(solution)/shard_map/cond/branch_1_fun/ppermute | solution.py:759
  204.8 11.4 %collective-permute-start.11 = (bf16[1424,256]{1,0:T(8,128)(2,1)S(1)}, bf16[1424,256]{1,0:T(8,128)(2,1)S(1)}, u32[]{:S(2)}, u32[]{:S(2)}) collective-permute-start(bf16[1424,256]{1,0:T(8,128)(2,1)S(1)} %pad_maximum_fusion.1), channel_id=1, source_target_pairs={{0,16},{1,3},{2,18},{3,1},{4,20},{5,7},{6,22},{7,5},{8,24},{9,11},... | collective-permute-start | bytes 2187272 | tf_op jit(solution)/shard_map/cond/branch_1_fun/ppermute | solution.py:759
  216.3 3.8 %copy-start.16 = (s32[6]{0:T(128)S(1)}, s32[6]{0:T(128)}, u32[]{:S(2)}) copy-start(s32[6]{0:T(128)} %get-tuple-element.60.flag) | copy-start | bytes 76 | tf_op jit(solution)/shard_map/cond
  216.5 3.7 %copy-start = (bf16[2816,256]{1,0:T(8,128)(2,1)}, bf16[2816,256]{1,0:T(8,128)(2,1)S(1)}, u32[]{:S(2)}) copy-start(bf16[2816,256]{1,0:T(8,128)(2,1)S(1)} %pad_maximum_fusion) | copy-start | bytes 4325380 | tf_op jit(solution)/shard_map/cond
  216.5 3.7 %collective-permute-start.12 = (bf16[2,1408,256]{2,1,0:T(8,128)(2,1)S(1)}, bf16[2,1408,256]{2,1,0:T(8,128)(2,1)}, u32[]{:S(2)}, u32[]{:S(2)}) collective-permute-start(bf16[2,1408,256]{2,1,0:T(8,128)(2,1)S(1)} %bitcast.44), channel_id=1, source_target_pairs={{0,1},{1,0},{2,3},{3,2},{4,5},{5,4},{6,7},{7,6},{8,9},{9,8},{10,11... | collective-permute-start | bytes 4325384 | tf_op jit(solution)/shard_map/cond/branch_1_fun/ppermute | solution.py:759
  216.6 3.6 %copy-start.13 = (bf16[16,256]{1,0:T(8,128)(2,1)}, bf16[16,256]{1,0:T(8,128)(2,1)S(1)}, u32[]{:S(2)}) copy-start(bf16[16,256]{1,0:T(8,128)(2,1)S(1)} %add_convert_fusion.10.own_e) | copy-start | bytes 24580 | tf_op jit(solution)/shard_map/cond
  216.6 2.9 %collective-permute-start.13 = (bf16[16,256]{1,0:T(8,128)(2,1)S(1)}, bf16[16,256]{1,0:T(8,128)(2,1)S(1)}, u32[]{:S(2)}, u32[]{:S(2)}) collective-permute-start(bf16[16,256]{1,0:T(8,128)(2,1)S(1)} %add_convert_fusion.10.own_e), channel_id=1, source_target_pairs={{0,1},{1,0},{2,3},{3,2},{4,5},{5,4},{6,7},{7,6},{8,9},{9,8},{10,11... | collective-permute-start | bytes 24584 | tf_op jit(solution)/shard_map/cond/branch_1_fun/ppermute | solution.py:759
  219.5 0.7 copy-start.19
Sparse Core Ops, SparseCore 0:
  18.7 60.5 all-gather.2
  95.0 149.1 all-reduce.7
